TPU v7x, 512 devices: a whole 4x4x16 slice. The times are simulated.
512 devices in a mesh: tile: 64 (over x, z), dp: 8 (over y, core).
Axes of the slice: x: 4, y: 4, z: 16, core: 2. Of those that a mesh axis runs over, the one named last changes fastest.
Arguments:
- feature_map: bfloat16 [8, 1024, 64, 256], P('dp', 'tile'), may hold values from -16 to 16
- weight: bfloat16 [9, 256, 256], replicated, may hold values from -0.125 to 0.125
- mask_grad: bfloat16 [8, 64, 2, 14, 14, 256], P('dp', 'tile'), may hold values from -6 to 6
- send_count: int32 [8, 64, 8], P('dp', 'tile'), may hold values from 0 to 2, as said below
- send_row: int32 [8, 64, 8, 2], P('dp', 'tile'), may hold values from 0 to 15
- send_col: int32 [8, 64, 8, 2], P('dp', 'tile'), may hold values from 0 to 50
Outputs:
- map_grad: float32 [8, 1024, 64, 256], P('dp', 'tile')
- weight_grad: float32 [9, 256, 256], replicated
Inputs may be any that keep to these rules, and one draw needn't show every extreme that they name: `send_count`: in every tile column each head receives exactly 2 live slots in all; one owner image sends 2 * 2 crops in all, one sends none, every other one 2, which is which drawn for each column; in every column some count equals 2.
All inputs are finite; a program needn't handle non-finite values.
Results may differ from a plain program's by a relative error of at most 0.004.
Values may be sent and summed in bfloat16 or wider, within the bound.
No kernel may reach another device: no remote copies, remote signals or barrier semaphores. Data moves between devices by JAX's collectives and lax.ppermute only.
A program may use at most 64 MiB of HBM per device.

v0:
```python
import jax
import jax.numpy as jnp
from jax import lax
from jax.sharding import PartitionSpec as P

GELU_SCALE = 0.7978845608
GELU_CUBIC = 0.044715


def shifted(array, axis, by):
    length = lax.axis_size(axis)
    pairs = [(i, i + by) for i in range(length) if 0 <= i + by < length]
    return lax.ppermute(array, axis, pairs)


def gelu_slope(values):
    inner = GELU_SCALE * (values + GELU_CUBIC * values * values * values)
    tangent = jnp.tanh(inner)
    outer = (
        0.5
        * values
        * (1.0 - tangent * tangent)
        * GELU_SCALE
        * (1.0 + 3.0 * GELU_CUBIC * values * values)
    )
    return 0.5 * (1.0 + tangent) + outer


def conv_backward(crops, weight, upstream):
    box_count = crops.shape[0]
    crop_side = crops.shape[1]
    channels = crops.shape[3]
    padded = jnp.pad(crops, ((0, 0), (1, 1), (1, 1), (0, 0)))
    windows = []
    for tap_index in range(9):
        tap_row = tap_index // 3
        tap_col = tap_index % 3
        windows.append(
            padded[:, tap_row : tap_row + crop_side, tap_col : tap_col + crop_side, :].reshape(
                -1, channels
            )
        )
    pre_act = jnp.zeros((windows[0].shape[0], weight.shape[2]), jnp.float32)
    for tap_index in range(9):
        pre_act = pre_act + jnp.dot(
            windows[tap_index], weight[tap_index], preferred_element_type=jnp.float32
        )
    slope = (upstream.reshape(pre_act.shape).astype(jnp.float32) * gelu_slope(pre_act)).astype(
        jnp.bfloat16
    )
    weight_list = []
    for tap_index in range(9):
        weight_list.append(
            lax.dot_general(
                windows[tap_index],
                slope,
                (((0,), (0,)), ((), ())),
                preferred_element_type=jnp.float32,
            )
        )
    weight_terms = jnp.stack(weight_list)
    grad_pad = jnp.zeros((box_count, crop_side + 2, crop_side + 2, channels), jnp.float32)
    for tap_index in range(9):
        tap_row = tap_index // 3
        tap_col = tap_index % 3
        part_grad = lax.dot_general(
            slope, weight[tap_index], (((1,), (1,)), ((), ())), preferred_element_type=jnp.float32
        )
        grad_pad = grad_pad.at[
            :, tap_row : tap_row + crop_side, tap_col : tap_col + crop_side, :
        ].add(part_grad.reshape(box_count, crop_side, crop_side, channels))
    crop_grad = grad_pad[:, 1 : crop_side + 1, 1 : crop_side + 1, :].astype(jnp.bfloat16)
    return (weight_terms, crop_grad)


def selector(live, slot_total):
    ranks = jnp.cumsum(live) - 1
    targets = lax.broadcasted_iota(jnp.int32, (slot_total, live.shape[0]), 0)
    chosen = (ranks[None, :] == targets) & (live[None, :] > 0)
    return chosen.astype(jnp.bfloat16)


def cut_crops(extended, top_rows, left_cols, crop_side):

    def single(top_row, left_col):
        return lax.dynamic_slice(
            extended, (top_row, left_col, top_row * 0), (crop_side, crop_side, extended.shape[2])
        )

    return jax.vmap(single)(top_rows, left_cols)


def add_crops(canvas, pieces, top_rows, left_cols, live):
    crop_side = pieces.shape[1]
    channels = canvas.shape[2]

    def place(slot_index, running):
        anchor = (top_rows[slot_index], left_cols[slot_index], top_rows[slot_index] * 0)
        current = lax.dynamic_slice(running, anchor, (crop_side, crop_side, channels))
        update = current + pieces[slot_index].astype(running.dtype) * live[slot_index]
        return lax.dynamic_update_slice(running, update, anchor)

    return lax.fori_loop(0, pieces.shape[0], place, canvas)


def on_device(feature_map, weight, mask_grad, send_count, send_row, send_col):
    tile_map = feature_map[0]
    tile_height = tile_map.shape[0]
    map_width = tile_map.shape[1]
    channels = tile_map.shape[2]
    boxes_head = mask_grad.shape[2]
    crop_side = mask_grad.shape[3]
    halo_rows = crop_side - 1
    owners = send_row.shape[2]
    slot_cap = send_row.shape[3]
    slot_total = owners * slot_cap
    below = shifted(tile_map[:halo_rows], "tile", -1)
    extended = jnp.concatenate([tile_map, below], 0)
    top_rows = send_row[0, 0].reshape(-1)
    left_cols = send_col[0, 0].reshape(-1)
    slot_iota = lax.broadcasted_iota(jnp.int32, (owners, slot_cap), 1)
    live = (slot_iota < send_count[0, 0][:, None]).astype(jnp.int32)
    upstream = mask_grad[0, 0]
    crops = cut_crops(extended, top_rows, left_cols, crop_side)
    got_crops, got_live = (
        lax.all_to_all(
            crops.reshape(owners, slot_cap, -1), "dp", split_axis=0, concat_axis=0, tiled=True
        ),
        lax.all_to_all(live, "dp", split_axis=0, concat_axis=0, tiled=True),
    )
    picker = selector(got_live.reshape(-1), boxes_head)
    head_crops = jnp.dot(
        picker, got_crops.reshape(slot_total, -1), preferred_element_type=jnp.float32
    ).astype(jnp.bfloat16)
    weight_terms, crop_grad = conv_backward(
        head_crops.reshape(boxes_head, crop_side, crop_side, channels), weight, upstream
    )
    back_slots = jnp.dot(
        picker.T, crop_grad.reshape(boxes_head, -1), preferred_element_type=jnp.float32
    ).astype(jnp.bfloat16)
    slot_grads = lax.all_to_all(
        back_slots.reshape(owners, slot_cap, -1), "dp", split_axis=0, concat_axis=0, tiled=True
    )
    slot_grads = slot_grads.reshape(slot_total, crop_side, crop_side, channels)
    canvas = jnp.zeros((tile_height + halo_rows, map_width, channels), jnp.float32)
    canvas = add_crops(
        canvas, slot_grads, top_rows, left_cols, live.reshape(-1).astype(jnp.float32)
    )
    arriving = shifted(canvas[tile_height:], "tile", 1)
    map_grad = jnp.concatenate([canvas[:halo_rows] + arriving, canvas[halo_rows:tile_height]], 0)
    box_total = boxes_head * lax.axis_size("tile") * lax.axis_size("dp")
    summed = lax.psum(weight_terms, ("tile", "dp"))
    return (map_grad[None], summed / box_total)


def solution(mesh):
    in_specs = (
        P("dp", "tile", None, None),
        P(),
        P("dp", "tile", None, None, None, None),
        P("dp", "tile", None),
        P("dp", "tile", None, None),
        P("dp", "tile", None, None),
    )
    out_specs = (P("dp", "tile", None, None), P())
    return jax.shard_map(
        on_device, mesh=mesh, in_specs=in_specs, out_specs=out_specs, check_vma=False
    )
```

profile of v0, /device:TPU:2, one launch (start us, length us, event | category | flops | bytes accessed | tf_op | source)
XLA Modules:
  0.0 623.2 jit_solution(12296041353185789032)
XLA Ops:
  8.2 11.4 %collective-permute-start = (bf16[13,64,256]{2,1,0:T(8,128)(2,1)S(1)}, bf16[13,64,256]{2,1,0:T(8,128)(2,1)S(1)}, u32[]{:S(2)}, u32[]{:S(2)}) collective-permute-start(bf16[13,64,256]{2,1,0:T(8,128)(2,1)S(1)} %slice_bitcast_fusion), channel_id=1, source_target_pairs={{8,0},{16,8},{24,16},{32,24},{40,32},{48,40},{56,48},{64,56},{72,6... | collective-permute-start | bytes 1277960 | tf_op jit(solution)/shard_map/ppermute | solution.py:13
  20.9 4.5 all-to-all-start
  27.1 1.6 collective-permute-done
  29.8 33.8 %while.24 = (s32[]{:T(128)}, bf16[29,64,256]{2,1,0:T(8,128)(2,1)S(1)}, s32[16,3]{0,1:T(4,128)S(1)}, bf16[16,14,14,256]{3,2,1,0:T(8,128)(2,1)S(1)}, s32[]{:T(128)}) while((s32[]{:T(128)}, bf16[29,64,256]{2,1,0:T(8,128)(2,1)S(1)}, s32[16,3]{0,1:T(4,128)S(1)}, bf16[16,14,14,256]{3,2,1,0:T(8,128)(2,1)S(1)}, s32[]{:T(128)}) %tuple.92), condition=%wide.while_cond.9, body=%wide.while_body.9.sunk | while | flops 2 | bytes 229501 | solution.py:86
  30.5 1.4 bitcast_dynamic-update-slice_fusion.2
  32.6 1.4 bitcast_dynamic-update-slice_fusion.2
  34.7 1.4 bitcast_dynamic-update-slice_fusion.2
  36.8 1.4 bitcast_dynamic-update-slice_fusion.2
  38.9 1.4 bitcast_dynamic-update-slice_fusion.2
  41.0 1.4 bitcast_dynamic-update-slice_fusion.2
  43.1 1.4 bitcast_dynamic-update-slice_fusion.2
  45.2 1.4 bitcast_dynamic-update-slice_fusion.2
  47.3 1.4 bitcast_dynamic-update-slice_fusion.2
  51.6 1.4 bitcast_dynamic-update-slice_fusion.2
  53.7 1.4 bitcast_dynamic-update-slice_fusion.2
  57.9 1.4 bitcast_dynamic-update-slice_fusion.2
  63.6 2.0 reshape.579
  65.6 4.6 all-to-all-start.1
  75.1 17.0 %all-to-all-done.1 = bf16[8,2,50176]{2,1,0:T(2,128)(2,1)S(1)} async-done(((bf16[8,2,50176]{2,1,0:T(2,128)(2,1)}), bf16[8,2,50176]{2,1,0:T(2,128)(2,1)S(1)}, u32[]{:S(2)}, u32[]{:S(2)}) %all-to-all-start.1) | async-done | bytes 1605664 | tf_op jit(solution)/shard_map/all_to_all | solution.py:126
  94.3 1.8 reshape.590
  102.3 1.4 convolution_add_fusion.7
  103.7 1.7 scatter-add.31
  105.4 2.2 fusion
  107.6 1.8 scatter-add.34
  114.7 1.5 reshape.596
  116.2 3.7 all-to-all-start.2
  128.0 13.8 %all-to-all-done.2 = bf16[8,2,50176]{2,1,0:T(2,128)(2,1)S(1)} async-done(((bf16[8,2,50176]{2,1,0:T(2,128)(2,1)}), bf16[8,2,50176]{2,1,0:T(2,128)(2,1)S(1)}, u32[]{:S(2)}, u32[]{:S(2)}) %all-to-all-start.2) | async-done | bytes 1605664 | tf_op jit(solution)/shard_map/all_to_all | solution.py:141
  141.8 2.3 reshape.597
  144.3 122.0 %while.23 = (s32[]{:T(128)}, f32[29,64,256]{2,1,0:T(8,128)S(1)}, s32[16]{0:T(128)S(1)}, s32[16]{0:T(128)S(1)}, bf16[16,14,14,256]{3,2,1,0:T(8,128)(2,1)}, /*inde...) while((s32[]{:T(128)}, f32[29,64,256]{2,1,0:T(8,128)S(1)}, s32[16]{0:T(128)S(1)}, ...), condition=%wide.region_3.4_spmd, body=%wide.region_2.3_spmd.sunk | while | flops 150536 | bytes 903401 | solution.py:103
  150.0 1.6 bitcast_add_fusion.2
  157.6 1.6 bitcast_add_fusion.2
  165.3 1.6 bitcast_add_fusion.2
  172.9 1.6 bitcast_add_fusion.2
  180.5 1.6 bitcast_add_fusion.2
  188.1 1.6 bitcast_add_fusion.2
  195.6 1.6 bitcast_add_fusion.2
  203.3 1.6 bitcast_add_fusion.2
  210.9 1.6 bitcast_add_fusion.2
  218.5 1.6 bitcast_add_fusion.2
  226.2 1.6 bitcast_add_fusion.2
  233.8 1.6 bitcast_add_fusion.2
  241.5 1.6 bitcast_add_fusion.2
  249.1 1.6 bitcast_add_fusion.2
  256.8 1.6 bitcast_add_fusion.2
  264.4 1.6 bitcast_add_fusion.2
  267.3 1.9 collective-permute-start.1
  269.2 342.6 %all-reduce.4.cloned.1.call-done = f32[9,256,256]{2,1,0:T(8,128)} async-done(((f32[9,256,256]{2,1,0:T(8,128)}), f32[9,256,256]{2,1,0:T(8,128)}) %all-reduce.4.cloned.1.call-update) | async-done | bytes 2359312 | tf_op jit(solution)/shard_map/psum | solution.py:152
  611.8 3.3 broadcast_multiply_fusion
  (222 shorter events, 84.0 us)
Async XLA Ops:
  8.2 20.4 %collective-permute-start = (bf16[13,64,256]{2,1,0:T(8,128)(2,1)S(1)}, bf16[13,64,256]{2,1,0:T(8,128)(2,1)S(1)}, u32[]{:S(2)}, u32[]{:S(2)}) collective-permute-start(bf16[13,64,256]{2,1,0:T(8,128)(2,1)S(1)} %slice_bitcast_fusion), channel_id=1, source_target_pairs={{8,0},{16,8},{24,16},{32,24},{40,32},{48,40},{56,48},{64,56},{72,6... | collective-permute-start | bytes 1277960 | tf_op jit(solution)/shard_map/ppermute | solution.py:13
  20.9 44.6 %all-to-all-start = ((s32[8,1,2]{2,1,0:T(1,128)}), s32[8,1,2]{2,1,0:T(1,128)S(1)}, u32[]{:S(2)}, u32[]{:S(2)}) async-start(s32[8,1,2]{2,1,0:T(1,128)} %compare_convert_fusion), calls=%async_computation | async-start | bytes 8192 | tf_op jit(solution)/shard_map/all_to_all | solution.py:129
  65.6 4.8 copy-start.16
  65.6 4.9 copy-start.15
  65.6 7.1 %copy-start.17 = (s32[4]{0:T(128)S(1)}, s32[4]{0:T(128)}, u32[]{:S(2)}) copy-start(s32[4]{0:T(128)} %constant.328.clone.1) | copy-start | bytes 52
  65.6 26.5 %all-to-all-start.1 = ((bf16[8,2,50176]{2,1,0:T(2,128)(2,1)}), bf16[8,2,50176]{2,1,0:T(2,128)(2,1)S(1)}, u32[]{:S(2)}, u32[]{:S(2)}) async-start(bf16[8,2,50176]{2,1,0:T(2,128)(2,1)} %reshape.579), calls=%async_computation.1 | async-start | bytes 3211264 | tf_op jit(solution)/shard_map/all_to_all | solution.py:126
  94.3 3.0 copy-start
  96.1 2.5 copy-start.9
  96.2 2.4 copy-start.7
  96.3 2.6 copy-start.5
  96.4 3.0 copy-start.3
  96.4 3.2 copy-start.1
  99.4 0.9 copy-start.12
  99.4 1.1 copy-start.14
  99.8 1.1 copy-start.11
  116.2 3.8 copy-start.10
  116.2 4.8 copy-start.8
  116.2 5.8 copy-start.6
  116.2 25.5 %all-to-all-start.2 = ((bf16[8,2,50176]{2,1,0:T(2,128)(2,1)}), bf16[8,2,50176]{2,1,0:T(2,128)(2,1)S(1)}, u32[]{:S(2)}, u32[]{:S(2)}) async-start(bf16[8,2,50176]{2,1,0:T(2,128)(2,1)} %reshape.596), calls=%async_computation.2 | async-start | bytes 3211264 | tf_op jit(solution)/shard_map/all_to_all | solution.py:141
  120.0 4.0 copy-start.4
  120.0 5.0 copy-start.2
  120.0 491.8 %all-reduce.4.cloned.1.call-start = ((), (), s32[]{:S(2)}) async-start(), calls=%async_computation.3 | async-start | bytes 4718592 | tf_op jit(solution)/shard_map/psum | solution.py:152
  121.0 5.9 copy-start.13
  267.3 347.8 %collective-permute-start.1 = (f32[13,64,256]{2,1,0:T(8,128)}, f32[13,64,256]{2,1,0:T(8,128)S(1)}, u32[]{:S(2)}, u32[]{:S(2)}) collective-permute-start(f32[13,64,256]{2,1,0:T(8,128)} %slice.420), channel_id=1, source_target_pairs={{0,8},{8,16},{16,24},{24,32},{32,40},{40,48},{48,56},{56,64},{64,7... | collective-permute-start | bytes 2555912 | tf_op jit(solution)/shard_map/ppermute | solution.py:13
Sparse Core Ops, SparseCore 0:
  128.1 483.6 all-reduce.3
where the time goes:
time: 626 us; the launch traced here: 623 us
  waiting for transfers between devices  375 us (60%)
  local copies, waits for them, and re-layouts  91.9 us (15%)
  loops' own time  63 us (10%)
  other arithmetic  34.2 us (5%)
  starting transfers between devices  26.1 us (4%)
  matrix products  18.4 us (3%)
  between operations  14.6 us (2%)
    psum x1, waiting for transfers between devices, on_device(): summed = lax.psum(weight_terms, ('tile', 'dp'))  343 us
    another operation x1, loops' own time, add_crops(): return lax.fori_loop(0, pieces.shape[0], place, canvas)  62.7 us
    gather x48, local copies, waits for them, and re-layouts  33.4 us
    add x16, other arithmetic, place(): current + pieces[slot_index].astype(running.dtype) * live[slot_index]  25.5 us
    all_to_all x1, waiting for transfers between devices, on_device(): lax.all_to_all(crops.reshape(owners, slot_cap, -1), 'dp', split_axis=0, c...  17 us
    all_to_all x1, waiting for transfers between devices, on_device(): lax.all_to_all(back_slots.reshape(owners, slot_cap, -1), 'dp', split_axis...  13.8 us
    ppermute x2, starting transfers between devices, shifted(): return lax.ppermute(array, axis, pairs)  13.3 us
  transfers between devices with their start and end apart: 6, of which 4 were waited for; matrix products, arithmetic and copies ran while one was open for 19% of the time, Pallas kernels for 0%

commit v1 on v0

v1 whole, which is shorter than its diff:
```python
import jax
import jax.numpy as jnp
from jax import lax
from jax.experimental import pallas as pl
from jax.experimental.pallas import tpu as pltpu
from jax.sharding import PartitionSpec as P

GELU_SCALE = 0.7978845608
GELU_CUBIC = 0.044715
F32 = jnp.float32
BF16 = jnp.bfloat16
XP = 16
LEFT = 8


def gelu_slope(values):
    inner = GELU_SCALE * (values + GELU_CUBIC * values * values * values)
    tangent = jnp.tanh(inner)
    outer = (
        0.5
        * values
        * (1.0 - tangent * tangent)
        * GELU_SCALE
        * (1.0 + 3.0 * GELU_CUBIC * values * values)
    )
    return 0.5 * (1.0 + tangent) + outer


def column_iota(rows):
    flat = lax.broadcasted_iota(jnp.int32, (rows, 1), 0)
    return lax.rem(flat, XP)


def forward_kernel(dims, me_ref, counts_ref, own_ref, row_ref, col_ref, map_ref, halo_ref, up_ref, weight_ref,
                   wgrad_ref, slope_ref, wide, shifted, slid, slot):
    side, slots, heads, cap, owners = dims
    high = map_ref.shape[0]
    halo = halo_ref.shape[0]
    width = map_ref.shape[1]
    channels = map_ref.shape[2]
    area = side * XP
    padded = (side + 2) * XP
    me = me_ref[0]

    for index in range(slots):
        for field in range(4):
            slot[field, index] = 0

    def head(j, used):
        before = lax.fori_loop(0, me, lambda i, total: total + counts_ref[i, j], 0)
        count = own_ref[j]
        for r in range(cap):
            live = (r < count) & (used < slots)

            @pl.when(live)
            def _():
                slot[0, used] = j
                slot[1, used] = before + r
                slot[2, used] = row_ref[j, r]
                slot[3, used] = col_ref[j, r]

            used = used + live.astype(jnp.int32)
        return used

    used = lax.fori_loop(0, heads, head, 0)

    wide[pl.ds(0, high), pl.ds(LEFT, width), :] = map_ref[...].astype(F32)
    wide[pl.ds(high, halo), pl.ds(LEFT, width), :] = halo_ref[...].astype(F32)

    columns = lax.broadcasted_iota(jnp.int32, (side, XP, channels), 1)
    flat_columns = lax.broadcasted_iota(jnp.int32, (side, XP, channels), 1).reshape(area, channels)
    none = jnp.zeros((XP, channels), BF16)
    for s in range(slots):
        live = s < used
        top = slot[2, s]
        left = slot[3, s]
        base = pl.multiple_of(left // 8 * 8, 8)
        window_all = wide[pl.ds(top, side), pl.ds(base, 2 * XP), :]
        window_all = pltpu.roll(window_all, 2 * XP - (LEFT - 1) - lax.rem(left, 8), 1)
        for b in range(3):
            window = (window_all if b == 0 else pltpu.roll(window_all, 2 * XP - b, 1))[:, :XP]
            low = jnp.where(live, max(0, 1 - b), XP)
            keep = (columns >= low) & (columns < min(side, side + 1 - b))
            shifted[b, pl.ds(s * padded, XP), :] = none
            shifted[b, pl.ds(s * padded + XP, area), :] = (
                jnp.where(keep, window, 0.0).astype(BF16).reshape(area, channels)
            )
            shifted[b, pl.ds(s * padded + XP + area, XP), :] = none

    for s in range(slots):
        taps = [
            shifted[b, pl.ds(s * padded + a * XP, area), :] for a in range(3) for b in range(3)
        ]
        lhs = jnp.concatenate(taps, axis=1)
        pre = jnp.dot(lhs, weight_ref[...].reshape(9 * channels, channels), preferred_element_type=F32)
        upstream = up_ref[slot[0, s], slot[1, s]].astype(F32).reshape(area, channels)
        last = jnp.where(s < used, side, 0)
        slope = jnp.where(flat_columns < last, upstream * gelu_slope(pre), 0.0).astype(BF16)
        slope_ref[pl.ds(s * area, area), :] = slope
        for a in range(3):
            if a > 0:
                slid[a, pl.ds(s * padded, a * XP), :] = jnp.zeros((a * XP, channels), BF16)
            slid[a, pl.ds(s * padded + a * XP, area), :] = slope
            if a < 2:
                slid[a, pl.ds(s * padded + a * XP + area, (2 - a) * XP), :] = jnp.zeros(
                    ((2 - a) * XP, channels), BF16
                )

    half = channels // 2
    rows = channels // 8
    for b in range(3):
        rhs = jnp.concatenate([slid[a] for a in range(3)], axis=1)
        terms = lax.dot_general(
            shifted[b], rhs, (((0,), (0,)), ((), ())), preferred_element_type=F32
        )
        for a in range(3):
            for part in range(2):
                piece = terms[:, a * channels + part * half : a * channels + (part + 1) * half]
                wgrad_ref[pl.ds((3 * a + b) * rows, rows), part] = piece.reshape(rows, 8, half)


def backward_kernel(dims, own_ref, row_ref, col_ref, slope_ref, weight_ref, main_ref, spill_ref, canvas, shifted,
                    slot):
    side, slots, heads, cap, owners = dims
    high = main_ref.shape[0]
    width = main_ref.shape[1]
    channels = main_ref.shape[2]
    halo = spill_ref.shape[0]
    area = side * XP
    padded = (side + 2) * XP

    for index in range(slots):
        for field in range(2):
            slot[field, index] = 0

    def head(j, used):
        count = own_ref[j]
        for r in range(cap):
            live = (r < count) & (used < slots)

            @pl.when(live)
            def _():
                slot[0, used] = row_ref[j, r]
                slot[1, used] = col_ref[j, r]

            used = used + live.astype(jnp.int32)
        return used

    used = lax.fori_loop(0, heads, head, 0)

    canvas[...] = jnp.zeros(canvas.shape, F32)
    none = jnp.zeros((XP, channels), BF16)
    rhs = jnp.concatenate([weight_ref[k] for k in range(9)], axis=1)
    columns = lax.broadcasted_iota(jnp.int32, (side, XP, channels), 1)
    for s in range(slots):
        slope = slope_ref[pl.ds(s * area, area), :].astype(F32)
        for b in range(3):
            moved = slope if b == 1 else pltpu.roll(slope, (area + b - 1) % area, 0)
            shifted[b, pl.ds(0, XP), :] = none
            shifted[b, pl.ds(XP, area), :] = moved.astype(BF16)
            shifted[b, pl.ds(XP + area, XP), :] = none
        taps = [shifted[b, pl.ds((2 - a) * XP, area), :] for a in range(3) for b in range(3)]
        lhs = jnp.concatenate(taps, axis=1)
        grad = lax.dot_general(lhs, rhs, (((1,), (1,)), ((), ())), preferred_element_type=F32)
        grad = grad.astype(BF16).astype(F32).reshape(side, XP, channels)
        last = jnp.where(s < used, side, 0)
        grad = jnp.where(columns < last, grad, 0.0)
        left = slot[1, s]
        grad = jnp.concatenate([grad, jnp.zeros((side, XP // 2, channels), F32)], axis=1)
        grad = pltpu.roll(grad, lax.rem(left, 8), 1)
        base = pl.multiple_of(left // 8 * 8, 8)
        place = (pl.ds(slot[0, s], side), pl.ds(base, XP + XP // 2), slice(None))
        canvas[place] = canvas[place] + grad
    main_ref[...] = canvas[pl.ds(0, high), pl.ds(0, width), :]
    spill_ref[...] = canvas[pl.ds(high, halo), pl.ds(0, width), :].astype(spill_ref.dtype)


def finish_kernel(core_ref, mine_ref, other_ref, out_ref):
    rows = mine_ref.shape[0] // 16
    half = out_ref.shape[0] // 2
    lanes = mine_ref.shape[1]
    core = core_ref[0]
    for part in range(2):
        source = jnp.where(core == part, mine_ref[...], other_ref[...]).astype(F32)
        source = source.reshape(rows, 2, 8, lanes)
        for piece in range(2):
            out_ref[pl.ds(part * half, half), pl.ds(piece * lanes, lanes)] = source[:, piece].reshape(half, lanes)


def smem():
    return pl.BlockSpec(memory_space=pltpu.SMEM)


def vmem():
    return pl.BlockSpec(memory_space=pltpu.VMEM)


def shift(array, axis, by):
    length = lax.axis_size(axis)
    pairs = [(i, i + by) for i in range(length) if 0 <= i + by < length]
    return lax.ppermute(array, axis, pairs)


def repeated(array, times):
    return jnp.broadcast_to(array[None], (times,) + array.shape)


def on_device(feature_map, weight, mask_grad, send_count, send_row, send_col):
    tile_map = feature_map[0]
    high, width, channels = tile_map.shape
    boxes, side = mask_grad.shape[2], mask_grad.shape[3]
    heads, cap = send_row.shape[2], send_row.shape[3]
    owners = lax.axis_size("dp")
    tiles = lax.axis_size("tile")
    slots = boxes * cap
    halo = side - 1
    area, padded = side * XP, (side + 2) * XP
    dims = (side, slots, heads, cap, owners)
    me = lax.axis_index("dp")
    me_array = me.reshape(1).astype(jnp.int32)
    own, top_rows, left_cols = send_count[0, 0], send_row[0, 0], send_col[0, 0]

    below = shift(tile_map[:halo], "tile", -1)
    counts = lax.all_to_all(repeated(own, owners), "dp", 0, 0, tiled=True)
    up = jnp.pad(mask_grad[0, 0], ((0, 0), (0, 0), (0, XP - side), (0, 0)))
    ups = lax.all_to_all(repeated(up, owners), "dp", 0, 0, tiled=True)

    wgrad, slope = pl.pallas_call(
        lambda *refs: forward_kernel(dims, *refs),
        out_shape=(
            jax.ShapeDtypeStruct((9 * channels // 8, 2, 8, channels // 2), F32),
            jax.ShapeDtypeStruct((slots * area, channels), BF16),
        ),
        in_specs=[smem()] * 5 + [vmem()] * 4,
        out_specs=(vmem(), vmem()),
        scratch_shapes=[
            pltpu.VMEM((high + halo, width + 2 * LEFT, channels), F32),
            pltpu.VMEM((3, slots * padded, channels), BF16),
            pltpu.VMEM((3, slots * padded, channels), BF16),
            pltpu.SMEM((4, slots), jnp.int32),
        ],
        name="forward",
    )(me_array, counts, own, top_rows, left_cols, tile_map, below, ups, weight)

    main, spill = pl.pallas_call(
        lambda *refs: backward_kernel(dims, *refs),
        out_shape=(
            jax.ShapeDtypeStruct((high, width, channels), F32),
            jax.ShapeDtypeStruct((halo, width, channels), BF16),
        ),
        in_specs=[smem()] * 3 + [vmem()] * 2,
        out_specs=(vmem(), vmem()),
        scratch_shapes=[
            pltpu.VMEM((high + halo, width + XP, channels), F32),
            pltpu.VMEM((3, padded, channels), BF16),
            pltpu.SMEM((2, slots), jnp.int32),
        ],
        name="backward",
    )(own, top_rows, left_cols, slope, weight)
    arriving = shift(spill, "tile", 1).astype(F32)
    map_grad = jnp.concatenate([main[:halo] + arriving, main[halo:]], 0)

    core = lax.rem(me, 2)
    partner = [(i, i ^ 1) for i in range(owners)]
    chips = owners // 2
    same_core = [[2 * i + c for i in range(chips)] for c in range(2)]
    lanes = channels // 2
    total = 9 * channels * 2
    halves = wgrad.reshape(2, total // 2, lanes)
    mine = jnp.where(core == 0, halves[0], halves[1])
    theirs = jnp.where(core == 0, halves[1], halves[0])
    pair = (mine + lax.ppermute(theirs, "dp", partner)).astype(BF16)
    quarter = total // 2 // chips
    got = lax.all_to_all(
        pair.reshape(chips, quarter, lanes), "dp", 0, 0, axis_index_groups=same_core, tiled=True
    )
    column = got.astype(F32).sum(0)
    got = lax.all_to_all(column.reshape(tiles, quarter // tiles, lanes), "tile", 0, 0, tiled=True)
    chunk = (got.sum(0) / (boxes * tiles * owners)).astype(BF16)
    got = lax.all_to_all(repeated(chunk, tiles), "tile", 0, 0, tiled=True).reshape(quarter, lanes)
    got = lax.all_to_all(repeated(got, chips), "dp", 0, 0, axis_index_groups=same_core, tiled=True)
    got = got.reshape(total // 2, lanes)
    other = lax.ppermute(got, "dp", partner)
    weight_grad = pl.pallas_call(
        finish_kernel,
        out_shape=jax.ShapeDtypeStruct((9 * channels, channels), F32),
        in_specs=[smem(), vmem(), vmem()],
        out_specs=vmem(),
        name="finish",
    )(core.reshape(1), got, other)
    return map_grad[None], weight_grad.reshape(9, channels, channels)


def solution(mesh):
    in_specs = (
        P("dp", "tile", None, None),
        P(),
        P("dp", "tile", None, None, None, None),
        P("dp", "tile", None),
        P("dp", "tile", None, None),
        P("dp", "tile", None, None),
    )
    out_specs = (P("dp", "tile", None, None), P())
    return jax.shard_map(
        on_device, mesh=mesh, in_specs=in_specs, out_specs=out_specs, check_vma=False
    )
```

time: 626 us -> 175 us (0.28)
  the two profiles are of different devices: /device:TPU:2 before, /device:TPU:14 now
where the time goes in v1:
time: 175 us; the launch traced here: 174 us
  blocking collectives  89.3 us (51%)
  starting transfers between devices  33.3 us (19%)
  waiting for transfers between devices  22.9 us (13%)
  Pallas kernels  14.7 us (8%)
  local copies, waits for them, and re-layouts  9.09 us (5%)
  other arithmetic  4.39 us (3%)
    all_to_all x1, blocking collectives, on_device(): lax.all_to_all(column.reshape(tiles, quarter // tiles, lanes), 'tile', 0,...  49 us
    all_to_all x1, blocking collectives, on_device(): lax.all_to_all(repeated(chunk, tiles), 'tile', 0, 0, tiled=True)  27.2 us
    ppermute x2, waiting for transfers between devices, shift(): return lax.ppermute(array, axis, pairs)  15.4 us
    ppermute x2, starting transfers between devices, shift(): return lax.ppermute(array, axis, pairs)  14.6 us
    all_to_all x1, blocking collectives, on_device(): lax.all_to_all(pair.reshape(chips, quarter, lanes), 'dp', 0, 0, axis_inde...  13.1 us
    pallas_call x1, Pallas kernels, on_device(): pl.pallas_call(lambda *refs: forward_kernel(dims, *refs), out_shape=(jax....  7.1 us
    all_to_all x1, starting transfers between devices, on_device(): ups = lax.all_to_all(repeated(up, owners), 'dp', 0, 0, tiled=True)  5.11 us
    all_to_all x1, starting transfers between devices, on_device(): counts = lax.all_to_all(repeated(own, owners), 'dp', 0, 0, tiled=True)  4.92 us
  transfers between devices with their start and end apart: 7, of which 5 were waited for; matrix products, arithmetic and copies ran while one was open for 3% of the time, Pallas kernels for 3%

profile of v1, /device:TPU:14, one launch (start us, length us, event | category | flops | bytes accessed | tf_op | source)
XLA Modules:
  0.0 174.4 jit_solution(10500976931506902708)
XLA Ops:
  0.6 1.3 broadcast_in_dim.12
  1.9 4.9 %all-to-all-start = ((s32[8,1,8]{2,1,0:T(1,128)}), s32[8,1,8]{2,1,0:T(1,128)S(1)}, u32[]{:S(2)}, u32[]{:S(2)}) async-start(s32[8,1,8]{2,1,0:T(1,128)} %broadcast_in_dim.12), calls=%async_computation | async-start | bytes 8192 | tf_op jit(solution)/shard_map/all_to_all | solution.py:224
  6.8 1.0 copy.23
  7.8 2.8 %all-to-all-done = s32[8,1,8]{2,1,0:T(1,128)S(1)} async-done(((s32[8,1,8]{2,1,0:T(1,128)}), s32[8,1,8]{2,1,0:T(1,128)S(1)}, u32[]{:S(2)}, u32[]{:S(2)}) %all-to-all-start) | async-done | bytes 288 | tf_op jit(solution)/shard_map/all_to_all | solution.py:224
  10.6 0.0 copy-start.5
  10.6 1.4 broadcast_in_dim.13
  12.0 0.0 copy-start.2
  12.0 0.0 copy-start.6
  12.0 0.0 copy-start.7
  12.0 0.0 copy-done.5
  12.0 5.1 %all-to-all-start.1 = ((bf16[8,2,14,16,256]{4,3,2,1,0:T(8,128)(2,1)}), bf16[8,2,14,16,256]{4,3,2,1,0:T(8,128)(2,1)S(1)}, u32[]{:S(2)}, u32[]{:S(2)}) async-start(bf16[8,2,14,16,256]{4,3,2,1,0:T(8,128)(2,1)} %broadcast_in_dim.13), calls=%async_computation.1 | async-start | bytes 3670016 | tf_op jit(solution)/shard_map/all_to_all | solution.py:226
  17.1 0.0 copy-done.2
  17.1 11.7 %collective-permute-start = (bf16[13,64,256]{2,1,0:T(8,128)(2,1)S(1)}, bf16[13,64,256]{2,1,0:T(8,128)(2,1)S(1)}, u32[]{:S(2)}, u32[]{:S(2)}) collective-permute-start(bf16[13,64,256]{2,1,0:T(8,128)(2,1)S(1)} %slice_bitcast_fusion), channel_id=1, source_target_pairs={{8,0},{16,8},{24,16},{32,24},{40,32},{48,40},{56,48},{64,56},{72,6... | collective-permute-start | bytes 1277960 | tf_op jit(solution)/shard_map/ppermute | solution.py:201
  28.8 0.0 copy-done.6
  28.8 0.7 copy.21.refs_3_.refs_1_
  29.5 0.0 copy-done.7
  29.5 0.7 copy.22.refs_4_.refs_2_
  30.2 8.0 %collective-permute-done.refs_6_ = bf16[13,64,256]{2,1,0:T(8,128)(2,1)S(1)} collective-permute-done((bf16[13,64,256]{2,1,0:T(8,128)(2,1)S(1)}, bf16[13,64,256]{2,1,0:T(8,128)(2,1)S(1)}, u32[]{:S(2)}, u32[]{:S(2)}) %collective-permute-start) | collective-permute-done | bytes 426016 | tf_op jit(solution)/shard_map/ppermute | solution.py:201
  38.1 0.0 copy-start.4
  38.1 1.9 %all-to-all-done.1.refs_7_ = bf16[8,2,14,16,256]{4,3,2,1,0:T(8,128)(2,1)S(1)} async-done(((bf16[8,2,14,16,256]{4,3,2,1,0:T(8,128)(2,1)}), bf16[8,2,14,16,256]{4,3,2,1,0:T(8,128)(2,1)S(1)}, u32[]{:S(2)}, u32[]{:S(2)}) %all-to-all-start.1) | async-done | bytes 1835040 | tf_op jit(solution)/shard_map/all_to_all | solution.py:226
  40.0 0.0 copy-done.4
  40.0 1.3 copy-done
  41.3 7.1 %forward.1 = (f32[288,2,8,128]{3,2,1,0:T(8,128)}, bf16[896,256]{1,0:T(8,128)(2,1)}) custom-call(s32[1]{0:T(128)} %bitcast.3.refs_0_, s32[8,8]{1,0:T(8,128)} %bitcast.27, s32[8]{0:T(128)} %bitcast.29, s32[8,2]{1,0:T(8,128)} %copy.21.refs_3_.refs_1_, s32[8,2]{1,0:T(8,128)} %copy.22.refs_4_.refs_2_, bf16[16,64,256]{2,1,0:T(8,128)(2,1)} %bitcast.24, ...), custom_call_target="tpu_custom_call" | custom-call | tf_op jit(solution)/shard_map/forward/pallas_call | solution.py:228
  48.4 1.8 %slice_select_fusion.1 = (f32[144,2,8,128]{3,2,1,0:T(8,128)S(1)}, f32[144,2,8,128]{3,2,1,0:T(8,128)S(1)}) fusion(f32[288,2,8,128]{3,2,1,0:T(8,128)} %get-tuple-element.9, pred[]{:T(512)S(6)} %eq.4), kind=kLoop, calls=%fused_computation.4 | loop fusion | flops 589824 | bytes 4718593 | tf_op jit(solution)/shard_map/jit(_where)/select_n | solution.py:270
  50.2 1.9 %collective-permute-start.2 = (f32[2304,128]{1,0:T(8,128)S(1)}, f32[2304,128]{1,0:T(8,128)S(1)}, u32[]{:S(2)}, u32[]{:S(2)}) collective-permute-start(f32[2304,128]{1,0:T(8,128)S(1)} %bitcast.25), channel_id=1, source_target_pairs={{0,1},{1,0},{2,3},{3,2},{4,5},{5,4},{6,7},{7,6},{8,9},{9,8},{10,11... | collective-permute-start | bytes 3538952 | tf_op jit(solution)/shard_map/ppermute | solution.py:272
  52.1 2.8 %collective-permute-done.2 = f32[2304,128]{1,0:T(8,128)S(1)} collective-permute-done((f32[2304,128]{1,0:T(8,128)S(1)}, f32[2304,128]{1,0:T(8,128)S(1)}, u32[]{:S(2)}, u32[]{:S(2)}) %collective-permute-start.2) | collective-permute-done | bytes 1179680 | tf_op jit(solution)/shard_map/ppermute | solution.py:272
  54.9 0.1 fusion
  55.0 13.1 %all_to_all.33 = bf16[4,576,128]{2,1,0:T(8,128)(2,1)S(1)} all-to-all(bf16[4,576,128]{2,1,0:T(8,128)(2,1)S(1)} %bitcast.21), channel_id=1, replica_groups={{0,2,4,6},{1,3,5,7},{8,10,12,14},{9,11,13,15},{16,18,20,22},{17,19,21,2..., dimensions={0} | all-to-all | bytes 1179648 | tf_op jit(solution)/shard_map/all_to_all | solution.py:274
  68.1 0.1 convert_reduce_fusion
  68.2 49.0 %all_to_all.34 = f32[64,9,128]{2,1,0:T(8,128)S(1)} all-to-all(f32[64,9,128]{2,1,0:T(8,128)S(1)} %reshape.48), channel_id=1, replica_groups=mesh['tile'=64,'dp'=8] {'tile'}, dimensions={0} | all-to-all | bytes 589824 | tf_op jit(solution)/shard_map/all_to_all | solution.py:278
  117.2 0.1 reduce_sum.19
  117.3 27.2 %all_to_all.35 = bf16[64,9,128]{2,1,0:T(8,128)(2,1)S(1)} all-to-all(bf16[64,9,128]{2,1,0:T(8,128)(2,1)S(1)} %broadcast_in_dim.30), channel_id=1, replica_groups=mesh['tile'=64,'dp'=8] {'tile'}, dimensions={0} | all-to-all | bytes 294912 | tf_op jit(solution)/shard_map/all_to_all | solution.py:280
  144.6 0.1 broadcast_in_dim.31
  144.6 0.9 broadcast_in_dim.32
  145.5 4.9 %all-to-all-start.5 = ((bf16[4,576,128]{2,1,0:T(8,128)(2,1)}), bf16[4,576,128]{2,1,0:T(8,128)(2,1)S(1)}, u32[]{:S(2)}, u32[]{:S(2)}) async-start(bf16[4,576,128]{2,1,0:T(8,128)(2,1)} %broadcast_in_dim.32), calls=%async_computation.5 | async-start | bytes 1179648 | tf_op jit(solution)/shard_map/all_to_all | solution.py:281
  150.4 4.6 %backward.1 = (f32[16,64,256]{2,1,0:T(8,128)}, bf16[13,64,256]{2,1,0:T(8,128)(2,1)}) custom-call(s32[8]{0:T(128)} %bitcast.30, s32[8,2]{1,0:T(8,128)} %copy.21.refs_3_.refs_1_, s32[8,2]{1,0:T(8,128)} %copy.22.refs_4_.refs_2_, bf16[896,256]{1,0:T(8,128)(2,1)} %get-tuple-element.6.refs_3_, bf16[9,256,256]{2,1,0:T(8,128)(2,1)} %refs_4_.1), custom_call_target="tpu_custom_call" | custom-call | tf_op jit(solution)/shard_map/backward/pallas_call | solution.py:245
  155.1 2.9 %collective-permute-start.1 = (bf16[13,64,256]{2,1,0:T(8,128)(2,1)}, bf16[13,64,256]{2,1,0:T(8,128)(2,1)S(1)}, u32[]{:S(2)}, u32[]{:S(2)}) collective-permute-start(bf16[13,64,256]{2,1,0:T(8,128)(2,1)} %get-tuple-element.8), channel_id=1, source_target_pairs={{0,8},{8,16},{16,24},{24,32},{32,40},{40,48},{48,56},{56,64},{64,7... | collective-permute-start | bytes 1277960 | tf_op jit(solution)/shard_map/ppermute | solution.py:201
  158.0 0.0 all-to-all-done.5
  158.0 0.0 copy-start.1
  158.0 1.9 %collective-permute-start.3 = (bf16[2304,128]{1,0:T(8,128)(2,1)S(1)}, bf16[2304,128]{1,0:T(8,128)(2,1)S(1)}, u32[]{:S(2)}, u32[]{:S(2)}) collective-permute-start(bf16[2304,128]{1,0:T(8,128)(2,1)S(1)} %bitcast.22), channel_id=1, source_target_pairs={{0,1},{1,0},{2,3},{3,2},{4,5},{5,4},{6,7},{7,6},{8,9},{9,8},{10,11... | collective-permute-start | bytes 1769480 | tf_op jit(solution)/shard_map/ppermute | solution.py:283
  159.9 0.9 slice.25
  160.9 7.5 %collective-permute-done.1 = bf16[13,64,256]{2,1,0:T(8,128)(2,1)S(1)} collective-permute-done((bf16[13,64,256]{2,1,0:T(8,128)(2,1)}, bf16[13,64,256]{2,1,0:T(8,128)(2,1)S(1)}, u32[]{:S(2)}, u32[]{:S(2)}) %collective-permute-start.1) | collective-permute-done | bytes 426016 | tf_op jit(solution)/shard_map/ppermute | solution.py:201
  168.4 1.3 convert_add_fusion
  169.6 0.0 copy-done.1
  169.6 1.1 maximum_bitcast_fusion
  170.7 0.0 collective-permute-done.3.other_ref
  170.7 0.8 copy-done.3
  171.5 2.9 %finish.1 = f32[2304,256]{1,0:T(8,128)} custom-call(s32[1]{0:T(128)} %bitcast.9.core_ref, bf16[2304,128]{1,0:T(8,128)(2,1)} %bitcast.23, bf16[2304,128]{1,0:T(8,128)(2,1)} %copy-done.3), custom_call_target="tpu_custom_call" | custom-call | tf_op jit(solution)/shard_map/finish/pallas_call | solution.py:284
  (7 shorter events, 0.1 us)
Async XLA Ops:
  1.9 8.7 %all-to-all-start = ((s32[8,1,8]{2,1,0:T(1,128)}), s32[8,1,8]{2,1,0:T(1,128)S(1)}, u32[]{:S(2)}, u32[]{:S(2)}) async-start(s32[8,1,8]{2,1,0:T(1,128)} %broadcast_in_dim.12), calls=%async_computation | async-start | bytes 8192 | tf_op jit(solution)/shard_map/all_to_all | solution.py:224
  10.6 1.4 copy-start.5
  12.0 5.1 %copy-start.2 = (bf16[1,16,64,256]{3,2,1,0:T(8,128)(2,1)S(1)}, bf16[1,16,64,256]{3,2,1,0:T(8,128)(2,1)}, u32[]{:S(2)}) copy-start(bf16[1,16,64,256]{3,2,1,0:T(8,128)(2,1)} %param.6) | copy-start | bytes 1572868
  12.0 16.8 %copy-start.6 = (s32[1,1,8,2]{2,3,1,0:T(2,128)S(1)}, s32[1,1,8,2]{2,3,1,0:T(2,128)}, u32[]{:S(2)}) copy-start(s32[1,1,8,2]{2,3,1,0:T(2,128)} %param.10) | copy-start | bytes 196
  12.0 17.5 %copy-start.7 = (s32[1,1,8,2]{2,3,1,0:T(2,128)S(1)}, s32[1,1,8,2]{2,3,1,0:T(2,128)}, u32[]{:S(2)}) copy-start(s32[1,1,8,2]{2,3,1,0:T(2,128)} %param.11) | copy-start | bytes 196
  12.0 28.0 %all-to-all-start.1 = ((bf16[8,2,14,16,256]{4,3,2,1,0:T(8,128)(2,1)}), bf16[8,2,14,16,256]{4,3,2,1,0:T(8,128)(2,1)S(1)}, u32[]{:S(2)}, u32[]{:S(2)}) async-start(bf16[8,2,14,16,256]{4,3,2,1,0:T(8,128)(2,1)} %broadcast_in_dim.13), calls=%async_computation.1 | async-start | bytes 3670016 | tf_op jit(solution)/shard_map/all_to_all | solution.py:226
  17.1 21.0 %collective-permute-start = (bf16[13,64,256]{2,1,0:T(8,128)(2,1)S(1)}, bf16[13,64,256]{2,1,0:T(8,128)(2,1)S(1)}, u32[]{:S(2)}, u32[]{:S(2)}) collective-permute-start(bf16[13,64,256]{2,1,0:T(8,128)(2,1)S(1)} %slice_bitcast_fusion), channel_id=1, source_target_pairs={{8,0},{16,8},{24,16},{32,24},{40,32},{48,40},{56,48},{64,56},{72,6... | collective-permute-start | bytes 1277960 | tf_op jit(solution)/shard_map/ppermute | solution.py:201
  38.1 1.9 %copy-start.4 = (bf16[13,64,256]{2,1,0:T(8,128)(2,1)}, bf16[13,64,256]{2,1,0:T(8,128)(2,1)S(1)}, u32[]{:S(2)}) copy-start(bf16[13,64,256]{2,1,0:T(8,128)(2,1)S(1)} %collective-permute-done.refs_6_) | copy-start | bytes 1277956
  40.0 1.3 copy-start
  50.2 4.7 %collective-permute-start.2 = (f32[2304,128]{1,0:T(8,128)S(1)}, f32[2304,128]{1,0:T(8,128)S(1)}, u32[]{:S(2)}, u32[]{:S(2)}) collective-permute-start(f32[2304,128]{1,0:T(8,128)S(1)} %bitcast.25), channel_id=1, source_target_pairs={{0,1},{1,0},{2,3},{3,2},{4,5},{5,4},{6,7},{7,6},{8,9},{9,8},{10,11... | collective-permute-start | bytes 3538952 | tf_op jit(solution)/shard_map/ppermute | solution.py:272
  145.5 12.5 %all-to-all-start.5 = ((bf16[4,576,128]{2,1,0:T(8,128)(2,1)}), bf16[4,576,128]{2,1,0:T(8,128)(2,1)S(1)}, u32[]{:S(2)}, u32[]{:S(2)}) async-start(bf16[4,576,128]{2,1,0:T(8,128)(2,1)} %broadcast_in_dim.32), calls=%async_computation.5 | async-start | bytes 1179648 | tf_op jit(solution)/shard_map/all_to_all | solution.py:281
  155.1 13.3 %collective-permute-start.1 = (bf16[13,64,256]{2,1,0:T(8,128)(2,1)}, bf16[13,64,256]{2,1,0:T(8,128)(2,1)S(1)}, u32[]{:S(2)}, u32[]{:S(2)}) collective-permute-start(bf16[13,64,256]{2,1,0:T(8,128)(2,1)} %get-tuple-element.8), channel_id=1, source_target_pairs={{0,8},{8,16},{16,24},{24,32},{32,40},{40,48},{48,56},{56,64},{64,7... | collective-permute-start | bytes 1277960 | tf_op jit(solution)/shard_map/ppermute | solution.py:201
  158.0 11.6 %copy-start.1 = (bf16[4,576,128]{2,1,0:T(8,128)(2,1)}, bf16[4,576,128]{2,1,0:T(8,128)(2,1)S(1)}, u32[]{:S(2)}) copy-start(bf16[4,576,128]{2,1,0:T(8,128)(2,1)S(1)} %all-to-all-done.5) | copy-start | bytes 1769476
  158.0 12.7 %collective-permute-start.3 = (bf16[2304,128]{1,0:T(8,128)(2,1)S(1)}, bf16[2304,128]{1,0:T(8,128)(2,1)S(1)}, u32[]{:S(2)}, u32[]{:S(2)}) collective-permute-start(bf16[2304,128]{1,0:T(8,128)(2,1)S(1)} %bitcast.22), channel_id=1, source_target_pairs={{0,1},{1,0},{2,3},{3,2},{4,5},{5,4},{6,7},{7,6},{8,9},{9,8},{10,11... | collective-permute-start | bytes 1769480 | tf_op jit(solution)/shard_map/ppermute | solution.py:283
  170.7 0.8 copy-start.3

commit v2 on v1

--- a/solution.py
+++ b/solution.py
@@ -26,54 +26,26 @@
     return 0.5 * (1.0 + tangent) + outer
 
 
-def column_iota(rows):
-    flat = lax.broadcasted_iota(jnp.int32, (rows, 1), 0)
-    return lax.rem(flat, XP)
-
-
-def forward_kernel(dims, me_ref, counts_ref, own_ref, row_ref, col_ref, map_ref, halo_ref, up_ref, weight_ref,
-                   wgrad_ref, slope_ref, wide, shifted, slid, slot):
-    side, slots, heads, cap, owners = dims
+def forward_kernel(dims, own_ref, row_ref, col_ref, map_ref, halo_ref, weight_ref,
+                   gelu_ref, shifted, wide, slot):
+    side, slots, heads, cap = dims
     high = map_ref.shape[0]
     halo = halo_ref.shape[0]
     width = map_ref.shape[1]
     channels = map_ref.shape[2]
     area = side * XP
     padded = (side + 2) * XP
-    me = me_ref[0]
-
-    for index in range(slots):
-        for field in range(4):
-            slot[field, index] = 0
-
-    def head(j, used):
-        before = lax.fori_loop(0, me, lambda i, total: total + counts_ref[i, j], 0)
-        count = own_ref[j]
-        for r in range(cap):
-            live = (r < count) & (used < slots)
-
-            @pl.when(live)
-            def _():
-                slot[0, used] = j
-                slot[1, used] = before + r
-                slot[2, used] = row_ref[j, r]
-                slot[3, used] = col_ref[j, r]
-
-            used = used + live.astype(jnp.int32)
-        return used
-
-    used = lax.fori_loop(0, heads, head, 0)
+    used = list_slots(dims, own_ref, slot, lambda j, r: (row_ref[j, r], col_ref[j, r]))
 
     wide[pl.ds(0, high), pl.ds(LEFT, width), :] = map_ref[...].astype(F32)
     wide[pl.ds(high, halo), pl.ds(LEFT, width), :] = halo_ref[...].astype(F32)
 
     columns = lax.broadcasted_iota(jnp.int32, (side, XP, channels), 1)
-    flat_columns = lax.broadcasted_iota(jnp.int32, (side, XP, channels), 1).reshape(area, channels)
     none = jnp.zeros((XP, channels), BF16)
     for s in range(slots):
         live = s < used
-        top = slot[2, s]
-        left = slot[3, s]
+        top = slot[0, s]
+        left = slot[1, s]
         base = pl.multiple_of(left // 8 * 8, 8)
         window_all = wide[pl.ds(top, side), pl.ds(base, 2 * XP), :]
         window_all = pltpu.roll(window_all, 2 * XP - (LEFT - 1) - lax.rem(left, 8), 1)
@@ -93,9 +65,63 @@
         ]
         lhs = jnp.concatenate(taps, axis=1)
         pre = jnp.dot(lhs, weight_ref[...].reshape(9 * channels, channels), preferred_element_type=F32)
-        upstream = up_ref[slot[0, s], slot[1, s]].astype(F32).reshape(area, channels)
+        gelu_ref[pl.ds(s * area, area), :] = gelu_slope(pre)
+
+
+def list_slots(dims, own_ref, slot, fields):
+    side, slots, heads, cap = dims
+    width = slot.shape[0]
+    for index in range(slots):
+        for field in range(width):
+            slot[field, index] = 0
+
+    def head(j, used):
+        count = own_ref[j]
+        for r in range(cap):
+            live = (r < count) & (used < slots)
+
+            @pl.when(live)
+            def _():
+                for field, value in enumerate(fields(j, r)):
+                    slot[field, used] = value
+
+            used = used + live.astype(jnp.int32)
+        return used
+
+    return lax.fori_loop(0, heads, head, 0)
+
+
+def slope_kernel(dims, me_ref, own_ref, ours_ref, across_ref, gelu_ref, shifted, mine_ref, theirs_ref, slope_ref,
+                 slid, prior, slot):
+    side, slots, heads, cap = dims
+    boxes = ours_ref.shape[1]
+    channels = gelu_ref.shape[1]
+    area = side * XP
+    padded = (side + 2) * XP
+    me = me_ref[0]
+    core = lax.rem(me, 2)
+
+    lane = lax.broadcasted_iota(jnp.int32, (8, channels), 1)
+    totals = jnp.zeros((8, channels), F32)
+    for i in range(heads):
+        row = jnp.where(core == i % 2, ours_ref[i // 2, 0, 0], across_ref[i // 2, 0, 0]).astype(F32)[8:16]
+        totals = totals + jnp.where(i < me, row, 0.0)
+    line = lax.broadcasted_iota(jnp.int32, (8, channels), 0)
+    totals = jnp.where(line == side - 8, totals, 0.0)
+    for j in range(heads):
+        prior[j] = jnp.sum(jnp.where(lane == j, totals, 0.0)).astype(jnp.int32)
+    used = list_slots(dims, own_ref, slot, lambda j, r: (j, jnp.minimum(prior[j] + r, boxes - 1)))
+
+    flat_columns = lax.broadcasted_iota(jnp.int32, (side, XP, channels), 1).reshape(area, channels)
+    for s in range(slots):
+        chip = slot[0, s] // 2
+        box = slot[1, s]
+        same = lax.rem(slot[0, s], 2) == core
+        upstream = jnp.where(same, ours_ref[chip, box].astype(F32), across_ref[chip, box].astype(F32))
+        upstream = upstream.reshape(area, channels)
         last = jnp.where(s < used, side, 0)
-        slope = jnp.where(flat_columns < last, upstream * gelu_slope(pre), 0.0).astype(BF16)
+        slope = upstream * gelu_ref[pl.ds(s * area, area), :]
+        slope = jnp.where(flat_columns < last, slope, 0.0).astype(BF16)
         slope_ref[pl.ds(s * area, area), :] = slope
         for a in range(3):
             if a > 0:
@@ -108,20 +134,35 @@
 
     half = channels // 2
     rows = channels // 8
+    split = 9 * rows // 2
     for b in range(3):
         rhs = jnp.concatenate([slid[a] for a in range(3)], axis=1)
         terms = lax.dot_general(
             shifted[b], rhs, (((0,), (0,)), ((), ())), preferred_element_type=F32
         )
         for a in range(3):
-            for part in range(2):
-                piece = terms[:, a * channels + part * half : a * channels + (part + 1) * half]
-                wgrad_ref[pl.ds((3 * a + b) * rows, rows), part] = piece.reshape(rows, 8, half)
+            first = (3 * a + b) * rows
+            for low, end, part in ((first, min(first + rows, split), 0), (max(first, split), first + rows, 1)):
+                if low >= end:
+                    continue
+                pieces = [
+                    terms[
+                        (low - first) * 8 : (end - first) * 8,
+                        a * channels + side_ * half : a * channels + (side_ + 1) * half,
+                    ].reshape(end - low, 8, half)
+                    for side_ in range(2)
+                ]
+                for ref, wanted in ((mine_ref, part), (theirs_ref, 1 - part)):
+
+                    @pl.when(core == wanted)
+                    def _():
+                        for side_ in range(2):
+                            ref[pl.ds(low - part * split, end - low), side_] = pieces[side_]
 
 
 def backward_kernel(dims, own_ref, row_ref, col_ref, slope_ref, weight_ref, main_ref, spill_ref, canvas, shifted,
                     slot):
-    side, slots, heads, cap, owners = dims
+    side, slots, heads, cap = dims
     high = main_ref.shape[0]
     width = main_ref.shape[1]
     channels = main_ref.shape[2]
@@ -129,25 +170,7 @@
     area = side * XP
     padded = (side + 2) * XP
 
-    for index in range(slots):
-        for field in range(2):
-            slot[field, index] = 0
-
-    def head(j, used):
-        count = own_ref[j]
-        for r in range(cap):
-            live = (r < count) & (used < slots)
-
-            @pl.when(live)
-            def _():
-                slot[0, used] = row_ref[j, r]
-                slot[1, used] = col_ref[j, r]
-
-            used = used + live.astype(jnp.int32)
-        return used
-
-    used = lax.fori_loop(0, heads, head, 0)
-
+    used = list_slots(dims, own_ref, slot, lambda j, r: (row_ref[j, r], col_ref[j, r]))
     canvas[...] = jnp.zeros(canvas.shape, F32)
     none = jnp.zeros((XP, channels), BF16)
     rhs = jnp.concatenate([weight_ref[k] for k in range(9)], axis=1)
@@ -215,32 +238,54 @@
     slots = boxes * cap
     halo = side - 1
     area, padded = side * XP, (side + 2) * XP
-    dims = (side, slots, heads, cap, owners)
+    dims = (side, slots, heads, cap)
     me = lax.axis_index("dp")
     me_array = me.reshape(1).astype(jnp.int32)
     own, top_rows, left_cols = send_count[0, 0], send_row[0, 0], send_col[0, 0]
+    partner = [(i, i ^ 1) for i in range(owners)]
+    chips = owners // 2
+    same_core = [[2 * i + c for i in range(chips)] for c in range(2)]
 
     below = shift(tile_map[:halo], "tile", -1)
-    counts = lax.all_to_all(repeated(own, owners), "dp", 0, 0, tiled=True)
-    up = jnp.pad(mask_grad[0, 0], ((0, 0), (0, 0), (0, XP - side), (0, 0)))
-    ups = lax.all_to_all(repeated(up, owners), "dp", 0, 0, tiled=True)
-
-    wgrad, slope = pl.pallas_call(
+    spare = jnp.pad(own.astype(BF16), (0, channels - heads))
+    spare = jnp.broadcast_to(spare, (boxes, side, XP - side, channels))
+    up = jnp.concatenate([mask_grad[0, 0], spare], 2)
+    ups = lax.all_to_all(
+        repeated(up, chips), "dp", 0, 0, axis_index_groups=same_core, tiled=True
+    )
+    partner_ups = lax.ppermute(ups, "dp", partner)
+    core = lax.rem(me, 2)
+
+    gelu, shifted = pl.pallas_call(
         lambda *refs: forward_kernel(dims, *refs),
         out_shape=(
-            jax.ShapeDtypeStruct((9 * channels // 8, 2, 8, channels // 2), F32),
-            jax.ShapeDtypeStruct((slots * area, channels), BF16),
+            jax.ShapeDtypeStruct((slots * area, channels), F32),
+            jax.ShapeDtypeStruct((3, slots * padded, channels), BF16),
         ),
-        in_specs=[smem()] * 5 + [vmem()] * 4,
+        in_specs=[smem()] * 3 + [vmem()] * 3,
         out_specs=(vmem(), vmem()),
         scratch_shapes=[
             pltpu.VMEM((high + halo, width + 2 * LEFT, channels), F32),
-            pltpu.VMEM((3, slots * padded, channels), BF16),
-            pltpu.VMEM((3, slots * padded, channels), BF16),
-            pltpu.SMEM((4, slots), jnp.int32),
+            pltpu.SMEM((2, slots), jnp.int32),
         ],
         name="forward",
-    )(me_array, counts, own, top_rows, left_cols, tile_map, below, ups, weight)
+    )(own, top_rows, left_cols, tile_map, below, weight)
+
+    lanes = channels // 2
+    total = 9 * channels * 2
+    split = jax.ShapeDtypeStruct((total // 32, 2, 8, lanes), F32)
+    mine, theirs, slope = pl.pallas_call(
+        lambda *refs: slope_kernel(dims, *refs),
+        out_shape=(split, split, jax.ShapeDtypeStruct((slots * area, channels), BF16)),
+        in_specs=[smem()] * 2 + [vmem()] * 4,
+        out_specs=(vmem(), vmem(), vmem()),
+        scratch_shapes=[
+            pltpu.VMEM((3, slots * padded, channels), BF16),
+            pltpu.SMEM((heads,), jnp.int32),
+            pltpu.SMEM((2, slots), jnp.int32),
+        ],
+        name="slope",
+    )(me_array, own, ups, partner_ups, gelu, shifted)
 
     main, spill = pl.pallas_call(
         lambda *refs: backward_kernel(dims, *refs),
@@ -260,26 +305,29 @@
     arriving = shift(spill, "tile", 1).astype(F32)
     map_grad = jnp.concatenate([main[:halo] + arriving, main[halo:]], 0)
 
-    core = lax.rem(me, 2)
-    partner = [(i, i ^ 1) for i in range(owners)]
-    chips = owners // 2
-    same_core = [[2 * i + c for i in range(chips)] for c in range(2)]
-    lanes = channels // 2
-    total = 9 * channels * 2
-    halves = wgrad.reshape(2, total // 2, lanes)
-    mine = jnp.where(core == 0, halves[0], halves[1])
-    theirs = jnp.where(core == 0, halves[1], halves[0])
-    pair = (mine + lax.ppermute(theirs, "dp", partner)).astype(BF16)
-    quarter = total // 2 // chips
+    part = total // 2
+    deep = 16 if tiles % 16 == 0 else 1
+    wide = tiles // deep
+    plane = [
+        [(x * deep + z) * owners + 2 * y + c for x in range(wide) for y in range(chips)]
+        for z in range(deep)
+        for c in range(2)
+    ]
+    stick = [[x * deep + z for z in range(deep)] for x in range(wide)]
+    near = wide * chips
+    pair = (mine.reshape(part, lanes) + lax.ppermute(theirs, "dp", partner).reshape(part, lanes)).astype(BF16)
     got = lax.all_to_all(
-        pair.reshape(chips, quarter, lanes), "dp", 0, 0, axis_index_groups=same_core, tiled=True
+        pair.reshape(near, part // near, lanes), ("tile", "dp"), 0, 0, axis_index_groups=plane, tiled=True
     )
     column = got.astype(F32).sum(0)
-    got = lax.all_to_all(column.reshape(tiles, quarter // tiles, lanes), "tile", 0, 0, tiled=True)
+    got = lax.all_to_all(
+        column.reshape(deep, part // near // deep, lanes), "tile", 0, 0, axis_index_groups=stick, tiled=True
+    )
     chunk = (got.sum(0) / (boxes * tiles * owners)).astype(BF16)
-    got = lax.all_to_all(repeated(chunk, tiles), "tile", 0, 0, tiled=True).reshape(quarter, lanes)
-    got = lax.all_to_all(repeated(got, chips), "dp", 0, 0, axis_index_groups=same_core, tiled=True)
-    got = got.reshape(total // 2, lanes)
+    got = lax.all_to_all(repeated(chunk, deep), "tile", 0, 0, axis_index_groups=stick, tiled=True)
+    got = got.reshape(part // near, lanes)
+    got = lax.all_to_all(repeated(got, near), ("tile", "dp"), 0, 0, axis_index_groups=plane, tiled=True)
+    got = got.reshape(part, lanes)
     other = lax.ppermute(got, "dp", partner)
     weight_grad = pl.pallas_call(
         finish_kernel,

time: 175 us -> 148 us (0.85)
  the two profiles are of different devices: /device:TPU:14 before, /device:TPU:2 now
where the time goes in v2:
time: 148 us; the launch traced here: 147 us
  blocking collectives  72.4 us (49%)
  starting transfers between devices  25 us (17%)
  Pallas kernels  18.6 us (13%)
  waiting for transfers between devices  18.4 us (12%)
  local copies, waits for them, and re-layouts  5.93 us (4%)
  other arithmetic  5.77 us (4%)
    all_to_all x1, blocking collectives, on_device(): lax.all_to_all(column.reshape(deep, part // near // deep, lanes), 'tile',...  21.9 us
    all_to_all x1, blocking collectives, on_device(): lax.all_to_all(repeated(up, chips), 'dp', 0, 0, axis_index_groups=same_co...  18.1 us
    all_to_all x1, blocking collectives, on_device(): lax.all_to_all(pair.reshape(near, part // near, lanes), ('tile', 'dp'), 0...  16.4 us
    all_to_all x1, blocking collectives, on_device(): lax.all_to_all(repeated(chunk, deep), 'tile', 0, 0, axis_index_groups=sti...  16 us
    ppermute x2, waiting for transfers between devices, shift(): return lax.ppermute(array, axis, pairs)  14.5 us
    ppermute x2, starting transfers between devices, shift(): return lax.ppermute(array, axis, pairs)  14.1 us
    pallas_call x1, Pallas kernels, on_device(): pl.pallas_call(lambda *refs: slope_kernel(dims, *refs), out_shape=(split,...  6.4 us
    all_to_all x1, starting transfers between devices, on_device(): lax.all_to_all(repeated(got, near), ('tile', 'dp'), 0, 0, axis_index_grou...  5.17 us
  transfers between devices with their start and end apart: 6, of which 4 were waited for; matrix products, arithmetic and copies ran while one was open for 3% of the time, Pallas kernels for 6%

profile of v2, /device:TPU:2, one launch (start us, length us, event | category | flops | bytes accessed | tf_op | source)
XLA Modules:
  0.0 147.0 jit_solution(12195609233592383261)
XLA Ops:
  0.6 0.7 bitcast_convert_fusion
  1.3 1.2 pad_maximum_fusion
  2.6 0.1 broadcast_in_dim.26
  2.7 0.0 copy-start.2
  2.7 0.0 copy-start.6
  2.7 0.0 copy-start.7
  2.7 18.1 %all_to_all.25.refs_2_ = bf16[4,2,14,16,256]{4,3,2,1,0:T(8,128)(2,1)S(1)} all-to-all(bf16[4,2,14,16,256]{4,3,2,1,0:T(8,128)(2,1)S(1)} %broadcast_in_dim.26), channel_id=1, replica_groups={{0,2,4,6},{1,3,5,7},{8,10,12,14},{9,11,13,15},{16,18,20,22},{17,19,21,2..., dimensions={0} | all-to-all | bytes 1835008 | tf_op jit(solution)/shard_map/all_to_all | solution.py:253
  20.8 0.0 copy-start
  20.8 1.9 %collective-permute-start = (bf16[4,2,14,16,256]{4,3,2,1,0:T(8,128)(2,1)S(1)}, bf16[4,2,14,16,256]{4,3,2,1,0:T(8,128)(2,1)S(1)}, u32[]{:S(2)}, u32[]{:S(2)}) collective-permute-start(bf16[4,2,14,16,256]{4,3,2,1,0:T(8,128)(2,1)S(1)} %all_to_all.25.refs_2_), channel_id=1, source_target_pairs={{0,1},{1,0},{2,3},{3,2},{4,5},{5,4},{6,7},{7,6},{8,9},{9,8},{10,11... | collective-permute-start | bytes 2752520 | tf_op jit(solution)/shard_map/ppermute | solution.py:256
  22.7 0.0 copy-done.2
  22.8 11.4 %collective-permute-start.1 = (bf16[13,64,256]{2,1,0:T(8,128)(2,1)S(1)}, bf16[13,64,256]{2,1,0:T(8,128)(2,1)S(1)}, u32[]{:S(2)}, u32[]{:S(2)}) collective-permute-start(bf16[13,64,256]{2,1,0:T(8,128)(2,1)S(1)} %slice_bitcast_fusion), channel_id=1, source_target_pairs={{8,0},{16,8},{24,16},{32,24},{40,32},{48,40},{56,48},{64,56},{72,6... | collective-permute-start | bytes 1277960 | tf_op jit(solution)/shard_map/ppermute | solution.py:224
  34.1 0.0 copy-done.6
  34.2 0.7 copy.16.refs_1_
  34.8 0.0 copy-done.7
  34.8 0.7 copy.17.refs_2_
  35.5 8.4 %collective-permute-done.1.refs_4_ = bf16[13,64,256]{2,1,0:T(8,128)(2,1)S(1)} collective-permute-done((bf16[13,64,256]{2,1,0:T(8,128)(2,1)S(1)}, bf16[13,64,256]{2,1,0:T(8,128)(2,1)S(1)}, u32[]{:S(2)}, u32[]{:S(2)}) %collective-permute-start.1) | collective-permute-done | bytes 426016 | tf_op jit(solution)/shard_map/ppermute | solution.py:224
  43.9 0.0 copy-start.5
  43.9 0.8 copy-done.5
  44.6 4.7 %forward.1 = (f32[896,256]{1,0:T(8,128)}, bf16[3,1024,256]{2,1,0:T(8,128)(2,1)}) custom-call(s32[8]{0:T(128)} %bitcast.21, s32[8,2]{1,0:T(8,128)} %copy.16.refs_1_, s32[8,2]{1,0:T(8,128)} %copy.17.refs_2_, bf16[16,64,256]{2,1,0:T(8,128)(2,1)} %bitcast.19, bf16[13,64,256]{2,1,0:T(8,128)(2,1)} %copy-done.5, bf16[9,256,256]{2,1,0:T(8,128)(2,1)} %refs_4_.1), custom_call_target="tpu_custom_call" | custom-call | tf_op jit(solution)/shard_map/forward/pallas_call | solution.py:259
  49.3 0.0 copy-done
  49.3 0.0 collective-permute-done.refs_3_
  49.3 0.0 copy-start.3
  49.3 0.9 copy-done.3
  50.3 6.4 %slope.1 = (f32[144,2,8,128]{3,2,1,0:T(8,128)}, f32[144,2,8,128]{3,2,1,0:T(8,128)}, bf16[896,256]{1,0:T(8,128)(2,1)}) custom-call(s32[1]{0:T(128)} %bitcast.3.refs_0_, s32[8]{0:T(128)} %bitcast.22, bf16[4,2,14,16,256]{4,3,2,1,0:T(8,128)(2,1)} %copy-done, bf16[4,2,14,16,256]{4,3,2,1,0:T(8,128)(2,1)} %copy-done.3, f32[896,256]{1,0:T(8,128)} %get-tuple-element.9.refs_4_, ...), custom_call_target="tpu_custom_call" | custom-call | tf_op jit(solution)/shard_map/slope/pallas_call | solution.py:277
  56.7 1.9 %collective-permute-start.3 = (f32[144,2,8,128]{3,2,1,0:T(8,128)}, f32[144,2,8,128]{3,2,1,0:T(8,128)S(1)}, u32[]{:S(2)}, u32[]{:S(2)}) collective-permute-start(f32[144,2,8,128]{3,2,1,0:T(8,128)} %get-tuple-element.15), channel_id=1, source_target_pairs={{0,1},{1,0},{2,3},{3,2},{4,5},{5,4},{6,7},{7,6},{8,9},{9,8},{10,11... | collective-permute-start | bytes 3538952 | tf_op jit(solution)/shard_map/ppermute | solution.py:318
  58.6 3.0 %collective-permute-done.3 = f32[144,2,8,128]{3,2,1,0:T(8,128)S(1)} collective-permute-done((f32[144,2,8,128]{3,2,1,0:T(8,128)}, f32[144,2,8,128]{3,2,1,0:T(8,128)S(1)}, u32[]{:S(2)}, u32[]{:S(2)}) %collective-permute-start.3) | collective-permute-done | bytes 1179680 | tf_op jit(solution)/shard_map/ppermute | solution.py:318
  61.6 1.4 add_convert_fusion
  63.1 16.4 %all_to_all.26 = bf16[16,144,128]{2,1,0:T(8,128)(2,1)S(1)} all-to-all(bf16[16,144,128]{2,1,0:T(8,128)(2,1)S(1)} %bitcast.16), channel_id=1, replica_groups={{0,2,4,6,128,130,132,134,256,258,260,262,384,386,388,390},{1,3,5,7,129,..., dimensions={0} | all-to-all | bytes 1179648 | tf_op jit(solution)/shard_map/all_to_all | solution.py:319
  79.5 0.1 convert_reduce_fusion
  79.6 21.9 %all_to_all.27 = f32[16,9,128]{2,1,0:T(8,128)S(1)} all-to-all(f32[16,9,128]{2,1,0:T(8,128)S(1)} %reshape.35), channel_id=1, replica_groups={{0,8,16,24,32,40,48,56,64,72,80,88,96,104,112,120},{128,136,144,152,160..., dimensions={0} | all-to-all | bytes 147456 | tf_op jit(solution)/shard_map/all_to_all | solution.py:323
  101.5 16.0 %all_to_all.28 = bf16[16,9,128]{2,1,0:T(8,128)(2,1)S(1)} all-to-all(bf16[16,9,128]{2,1,0:T(8,128)(2,1)S(1)} %broadcast_in_dim.28), channel_id=1, replica_groups={{0,8,16,24,32,40,48,56,64,72,80,88,96,104,112,120},{128,136,144,152,160..., dimensions={0} | all-to-all | bytes 73728 | tf_op jit(solution)/shard_map/all_to_all | solution.py:327
  117.6 0.9 broadcast_in_dim.30
  118.4 5.2 %all-to-all-start.4 = ((bf16[16,144,128]{2,1,0:T(8,128)(2,1)}), bf16[16,144,128]{2,1,0:T(8,128)(2,1)S(1)}, u32[]{:S(2)}, u32[]{:S(2)}) async-start(bf16[16,144,128]{2,1,0:T(8,128)(2,1)} %broadcast_in_dim.30), calls=%async_computation.4 | async-start | bytes 1179648 | tf_op jit(solution)/shard_map/all_to_all | solution.py:329
  123.6 4.6 %backward.1 = (f32[16,64,256]{2,1,0:T(8,128)}, bf16[13,64,256]{2,1,0:T(8,128)(2,1)}) custom-call(s32[8]{0:T(128)} %bitcast.23, s32[8,2]{1,0:T(8,128)} %copy.16.refs_1_, s32[8,2]{1,0:T(8,128)} %copy.17.refs_2_, bf16[896,256]{1,0:T(8,128)(2,1)} %get-tuple-element.11.refs_3_, bf16[9,256,256]{2,1,0:T(8,128)(2,1)} %refs_4_.1), custom_call_target="tpu_custom_call" | custom-call | tf_op jit(solution)/shard_map/backward/pallas_call | solution.py:290
  128.2 2.7 %collective-permute-start.2 = (bf16[13,64,256]{2,1,0:T(8,128)(2,1)}, bf16[13,64,256]{2,1,0:T(8,128)(2,1)S(1)}, u32[]{:S(2)}, u32[]{:S(2)}) collective-permute-start(bf16[13,64,256]{2,1,0:T(8,128)(2,1)} %get-tuple-element.13), channel_id=1, source_target_pairs={{0,8},{8,16},{16,24},{24,32},{32,40},{40,48},{48,56},{56,64},{64,7... | collective-permute-start | bytes 1277960 | tf_op jit(solution)/shard_map/ppermute | solution.py:224
  131.0 0.9 all-to-all-done.4
  131.9 0.0 copy-start.1
  131.9 1.9 %collective-permute-start.4 = (bf16[2304,128]{1,0:T(8,128)(2,1)S(1)}, bf16[2304,128]{1,0:T(8,128)(2,1)S(1)}, u32[]{:S(2)}, u32[]{:S(2)}) collective-permute-start(bf16[2304,128]{1,0:T(8,128)(2,1)S(1)} %bitcast.17), channel_id=1, source_target_pairs={{0,1},{1,0},{2,3},{3,2},{4,5},{5,4},{6,7},{7,6},{8,9},{9,8},{10,11... | collective-permute-start | bytes 1769480 | tf_op jit(solution)/shard_map/ppermute | solution.py:331
  133.8 0.9 slice.15
  134.8 6.1 %collective-permute-done.2 = bf16[13,64,256]{2,1,0:T(8,128)(2,1)S(1)} collective-permute-done((bf16[13,64,256]{2,1,0:T(8,128)(2,1)}, bf16[13,64,256]{2,1,0:T(8,128)(2,1)S(1)}, u32[]{:S(2)}, u32[]{:S(2)}) %collective-permute-start.2) | collective-permute-done | bytes 426016 | tf_op jit(solution)/shard_map/ppermute | solution.py:224
  140.9 1.3 convert_add_fusion
  142.2 0.0 copy-done.1
  142.2 1.1 maximum_bitcast_fusion
  143.2 0.0 collective-permute-done.4.other_ref
  143.2 0.0 copy-start.4
  143.2 0.8 copy-done.4
  144.1 2.9 %finish.1 = f32[2304,256]{1,0:T(8,128)} custom-call(s32[1]{0:T(128)} %bitcast.8.core_ref, bf16[2304,128]{1,0:T(8,128)(2,1)} %bitcast.18, bf16[2304,128]{1,0:T(8,128)(2,1)} %copy-done.4), custom_call_target="tpu_custom_call" | custom-call | tf_op jit(solution)/shard_map/finish/pallas_call | solution.py:332
  (9 shorter events, 0.2 us)
Async XLA Ops:
  2.7 20.0 %copy-start.2 = (bf16[1,16,64,256]{3,2,1,0:T(8,128)(2,1)S(1)}, bf16[1,16,64,256]{3,2,1,0:T(8,128)(2,1)}, u32[]{:S(2)}) copy-start(bf16[1,16,64,256]{3,2,1,0:T(8,128)(2,1)} %param.6) | copy-start | bytes 1572868
  2.7 31.5 %copy-start.6 = (s32[1,1,8,2]{2,3,1,0:T(2,128)S(1)}, s32[1,1,8,2]{2,3,1,0:T(2,128)}, u32[]{:S(2)}) copy-start(s32[1,1,8,2]{2,3,1,0:T(2,128)} %param.10) | copy-start | bytes 196
  2.7 32.1 %copy-start.7 = (s32[1,1,8,2]{2,3,1,0:T(2,128)S(1)}, s32[1,1,8,2]{2,3,1,0:T(2,128)}, u32[]{:S(2)}) copy-start(s32[1,1,8,2]{2,3,1,0:T(2,128)} %param.11) | copy-start | bytes 196
  20.8 28.5 %copy-start = (bf16[4,2,14,16,256]{4,3,2,1,0:T(8,128)(2,1)}, bf16[4,2,14,16,256]{4,3,2,1,0:T(8,128)(2,1)S(1)}, u32[]{:S(2)}) copy-start(bf16[4,2,14,16,256]{4,3,2,1,0:T(8,128)(2,1)S(1)} %all_to_all.25.refs_2_) | copy-start | bytes 2752516
  20.8 28.5 %collective-permute-start = (bf16[4,2,14,16,256]{4,3,2,1,0:T(8,128)(2,1)S(1)}, bf16[4,2,14,16,256]{4,3,2,1,0:T(8,128)(2,1)S(1)}, u32[]{:S(2)}, u32[]{:S(2)}) collective-permute-start(bf16[4,2,14,16,256]{4,3,2,1,0:T(8,128)(2,1)S(1)} %all_to_all.25.refs_2_), channel_id=1, source_target_pairs={{0,1},{1,0},{2,3},{3,2},{4,5},{5,4},{6,7},{7,6},{8,9},{9,8},{10,11... | collective-permute-start | bytes 2752520 | tf_op jit(solution)/shard_map/ppermute | solution.py:256
  22.8 21.1 %collective-permute-start.1 = (bf16[13,64,256]{2,1,0:T(8,128)(2,1)S(1)}, bf16[13,64,256]{2,1,0:T(8,128)(2,1)S(1)}, u32[]{:S(2)}, u32[]{:S(2)}) collective-permute-start(bf16[13,64,256]{2,1,0:T(8,128)(2,1)S(1)} %slice_bitcast_fusion), channel_id=1, source_target_pairs={{8,0},{16,8},{24,16},{32,24},{40,32},{48,40},{56,48},{64,56},{72,6... | collective-permute-start | bytes 1277960 | tf_op jit(solution)/shard_map/ppermute | solution.py:224
  43.9 0.8 copy-start.5
  49.3 1.0 copy-start.3
  56.7 4.9 %collective-permute-start.3 = (f32[144,2,8,128]{3,2,1,0:T(8,128)}, f32[144,2,8,128]{3,2,1,0:T(8,128)S(1)}, u32[]{:S(2)}, u32[]{:S(2)}) collective-permute-start(f32[144,2,8,128]{3,2,1,0:T(8,128)} %get-tuple-element.15), channel_id=1, source_target_pairs={{0,1},{1,0},{2,3},{3,2},{4,5},{5,4},{6,7},{7,6},{8,9},{9,8},{10,11... | collective-permute-start | bytes 3538952 | tf_op jit(solution)/shard_map/ppermute | solution.py:318
  118.4 13.5 %all-to-all-start.4 = ((bf16[16,144,128]{2,1,0:T(8,128)(2,1)}), bf16[16,144,128]{2,1,0:T(8,128)(2,1)S(1)}, u32[]{:S(2)}, u32[]{:S(2)}) async-start(bf16[16,144,128]{2,1,0:T(8,128)(2,1)} %broadcast_in_dim.30), calls=%async_computation.4 | async-start | bytes 1179648 | tf_op jit(solution)/shard_map/all_to_all | solution.py:329
  128.2 12.6 %collective-permute-start.2 = (bf16[13,64,256]{2,1,0:T(8,128)(2,1)}, bf16[13,64,256]{2,1,0:T(8,128)(2,1)S(1)}, u32[]{:S(2)}, u32[]{:S(2)}) collective-permute-start(bf16[13,64,256]{2,1,0:T(8,128)(2,1)} %get-tuple-element.13), channel_id=1, source_target_pairs={{0,8},{8,16},{16,24},{24,32},{32,40},{40,48},{48,56},{56,64},{64,7... | collective-permute-start | bytes 1277960 | tf_op jit(solution)/shard_map/ppermute | solution.py:224
  131.9 10.3 %copy-start.1 = (bf16[16,144,128]{2,1,0:T(8,128)(2,1)}, bf16[16,144,128]{2,1,0:T(8,128)(2,1)S(1)}, u32[]{:S(2)}) copy-start(bf16[16,144,128]{2,1,0:T(8,128)(2,1)S(1)} %all-to-all-done.4) | copy-start | bytes 1769476
  131.9 11.3 %collective-permute-start.4 = (bf16[2304,128]{1,0:T(8,128)(2,1)S(1)}, bf16[2304,128]{1,0:T(8,128)(2,1)S(1)}, u32[]{:S(2)}, u32[]{:S(2)}) collective-permute-start(bf16[2304,128]{1,0:T(8,128)(2,1)S(1)} %bitcast.17), channel_id=1, source_target_pairs={{0,1},{1,0},{2,3},{3,2},{4,5},{5,4},{6,7},{7,6},{8,9},{9,8},{10,11... | collective-permute-start | bytes 1769480 | tf_op jit(solution)/shard_map/ppermute | solution.py:331
  143.2 0.8 copy-start.4

commit v3 on v2

--- a/solution.py
+++ b/solution.py
@@ -5,10 +5,12 @@
 from jax.experimental.pallas import tpu as pltpu
 from jax.sharding import PartitionSpec as P
 
+
 GELU_SCALE = 0.7978845608
 GELU_CUBIC = 0.044715
 F32 = jnp.float32
 BF16 = jnp.bfloat16
+VMEM_BYTES = 20 * 2**20
 XP = 16
 LEFT = 8
 
@@ -28,7 +30,7 @@
 
 def forward_kernel(dims, own_ref, row_ref, col_ref, map_ref, halo_ref, weight_ref,
                    gelu_ref, shifted, wide, slot):
-    side, slots, heads, cap = dims
+    side, slots, _, _ = dims
     high = map_ref.shape[0]
     halo = halo_ref.shape[0]
     width = map_ref.shape[1]
@@ -69,7 +71,7 @@
 
 
 def list_slots(dims, own_ref, slot, fields):
-    side, slots, heads, cap = dims
+    _, slots, heads, cap = dims
     width = slot.shape[0]
     for index in range(slots):
         for field in range(width):
@@ -93,7 +95,7 @@
 
 def slope_kernel(dims, me_ref, own_ref, ours_ref, across_ref, gelu_ref, shifted, mine_ref, theirs_ref, slope_ref,
                  slid, prior, slot):
-    side, slots, heads, cap = dims
+    side, slots, heads, _ = dims
     boxes = ours_ref.shape[1]
     channels = gelu_ref.shape[1]
     area = side * XP
@@ -162,13 +164,12 @@
 
 def backward_kernel(dims, own_ref, row_ref, col_ref, slope_ref, weight_ref, main_ref, spill_ref, canvas, shifted,
                     slot):
-    side, slots, heads, cap = dims
+    side, slots, _, _ = dims
     high = main_ref.shape[0]
     width = main_ref.shape[1]
     channels = main_ref.shape[2]
     halo = spill_ref.shape[0]
     area = side * XP
-    padded = (side + 2) * XP
 
     used = list_slots(dims, own_ref, slot, lambda j, r: (row_ref[j, r], col_ref[j, r]))
     canvas[...] = jnp.zeros(canvas.shape, F32)
@@ -250,17 +251,16 @@
     spare = jnp.pad(own.astype(BF16), (0, channels - heads))
     spare = jnp.broadcast_to(spare, (boxes, side, XP - side, channels))
     up = jnp.concatenate([mask_grad[0, 0], spare], 2)
-    ups = lax.all_to_all(
-        repeated(up, chips), "dp", 0, 0, axis_index_groups=same_core, tiled=True
-    )
+    sent = repeated(up, chips)
+    ups = lax.all_to_all(sent, "dp", 0, 0, axis_index_groups=same_core, tiled=True)
     partner_ups = lax.ppermute(ups, "dp", partner)
     core = lax.rem(me, 2)
 
     gelu, shifted = pl.pallas_call(
         lambda *refs: forward_kernel(dims, *refs),
         out_shape=(
-            jax.ShapeDtypeStruct((slots * area, channels), F32),
-            jax.ShapeDtypeStruct((3, slots * padded, channels), BF16),
+            pltpu.VMEM((slots * area, channels), F32),
+            pltpu.VMEM((3, slots * padded, channels), BF16),
         ),
         in_specs=[smem()] * 3 + [vmem()] * 3,
         out_specs=(vmem(), vmem()),
@@ -269,6 +269,7 @@
             pltpu.SMEM((2, slots), jnp.int32),
         ],
         name="forward",
+        compiler_params=pltpu.CompilerParams(vmem_limit_bytes=VMEM_BYTES),
     )(own, top_rows, left_cols, tile_map, below, weight)
 
     lanes = channels // 2
@@ -285,6 +286,7 @@
             pltpu.SMEM((2, slots), jnp.int32),
         ],
         name="slope",
+        compiler_params=pltpu.CompilerParams(vmem_limit_bytes=VMEM_BYTES),
     )(me_array, own, ups, partner_ups, gelu, shifted)
 
     main, spill = pl.pallas_call(
@@ -301,6 +303,7 @@
             pltpu.SMEM((2, slots), jnp.int32),
         ],
         name="backward",
+        compiler_params=pltpu.CompilerParams(vmem_limit_bytes=VMEM_BYTES),
     )(own, top_rows, left_cols, slope, weight)
     arriving = shift(spill, "tile", 1).astype(F32)
     map_grad = jnp.concatenate([main[:halo] + arriving, main[halo:]], 0)
@@ -335,6 +338,7 @@
         in_specs=[smem(), vmem(), vmem()],
         out_specs=vmem(),
         name="finish",
+        compiler_params=pltpu.CompilerParams(vmem_limit_bytes=VMEM_BYTES),
     )(core.reshape(1), got, other)
     return map_grad[None], weight_grad.reshape(9, channels, channels)
 
@@ -349,6 +353,5 @@
         P("dp", "tile", None, None),
     )
     out_specs = (P("dp", "tile", None, None), P())
-    return jax.shard_map(
-        on_device, mesh=mesh, in_specs=in_specs, out_specs=out_specs, check_vma=False
-    )
+
+    return jax.shard_map(on_device, mesh=mesh, in_specs=in_specs, out_specs=out_specs, check_vma=False)

time: 148 us -> 137 us (0.926)
  the two profiles are of different devices: /device:TPU:2 before, /device:TPU:4 now
where the time goes in v3:
time: 137 us; the launch traced here: 136 us
  blocking collectives  72.2 us (53%)
  starting transfers between devices  25.4 us (19%)
  waiting for transfers between devices  20.7 us (15%)
  Pallas kernels  11.7 us (9%)
  other arithmetic  3.39 us (2%)
  local copies, waits for them, and re-layouts  2.07 us (2%)
    all_to_all x1, blocking collectives, on_device(): lax.all_to_all(column.reshape(deep, part // near // deep, lanes), 'tile',...  22 us
    all_to_all x1, blocking collectives, on_device(): lax.all_to_all(sent, 'dp', 0, 0, axis_index_groups=same_core, tiled=True)  18.1 us
    all_to_all x1, blocking collectives, on_device(): lax.all_to_all(repeated(chunk, deep), 'tile', 0, 0, axis_index_groups=sti...  16.5 us
    ppermute x2, waiting for transfers between devices, shift(): return lax.ppermute(array, axis, pairs)  16 us
    all_to_all x1, blocking collectives, on_device(): lax.all_to_all(pair.reshape(near, part // near, lanes), ('tile', 'dp'), 0...  15.5 us
    ppermute x2, starting transfers between devices, shift(): return lax.ppermute(array, axis, pairs)  14.1 us
    all_to_all x1, starting transfers between devices, on_device(): lax.all_to_all(repeated(got, near), ('tile', 'dp'), 0, 0, axis_index_grou...  5.54 us
    pallas_call x1, Pallas kernels, on_device(): pl.pallas_call(lambda *refs: backward_kernel(dims, *refs), out_shape=(jax...  3.58 us
  transfers between devices with their start and end apart: 6, of which 4 were waited for; matrix products, arithmetic and copies ran while one was open for 2% of the time, Pallas kernels for 5%

profile of v3, /device:TPU:4, one launch (start us, length us, event | category | flops | bytes accessed | tf_op | source)
XLA Modules:
  0.0 136.1 jit_solution(16068582884321283288)
XLA Ops:
  0.6 0.7 bitcast_convert_fusion
  1.3 1.2 pad_maximum_fusion
  2.6 0.1 broadcast_in_dim.26
  2.7 0.0 copy-start.1
  2.7 0.0 copy-start.5
  2.7 0.0 copy-start.6
  2.7 0.0 copy-start
  2.7 0.0 copy-start.4
  2.7 18.1 %all_to_all.25.refs_2_ = bf16[4,2,14,16,256]{4,3,2,1,0:T(8,128)(2,1)S(1)} all-to-all(bf16[4,2,14,16,256]{4,3,2,1,0:T(8,128)(2,1)S(1)} %broadcast_in_dim.26), channel_id=1, replica_groups={{0,2,4,6},{1,3,5,7},{8,10,12,14},{9,11,13,15},{16,18,20,22},{17,19,21,2..., dimensions={0} | all-to-all | bytes 1835008 | tf_op jit(solution)/shard_map/all_to_all | solution.py:255
  20.8 1.9 %collective-permute-start = (bf16[4,2,14,16,256]{4,3,2,1,0:T(8,128)(2,1)S(1)}, bf16[4,2,14,16,256]{4,3,2,1,0:T(8,128)(2,1)S(1)}, u32[]{:S(2)}, u32[]{:S(2)}) collective-permute-start(bf16[4,2,14,16,256]{4,3,2,1,0:T(8,128)(2,1)S(1)} %all_to_all.25.refs_2_), channel_id=1, source_target_pairs={{0,1},{1,0},{2,3},{3,2},{4,5},{5,4},{6,7},{7,6},{8,9},{9,8},{10,11... | collective-permute-start | bytes 2752520 | tf_op jit(solution)/shard_map/ppermute | solution.py:256
  22.7 0.0 copy-done.1
  22.7 0.8 slice_bitcast_fusion
  23.5 11.4 %collective-permute-start.1 = (bf16[13,64,256]{2,1,0:T(8,128)(2,1)}, bf16[13,64,256]{2,1,0:T(8,128)(2,1)}, u32[]{:S(2)}, u32[]{:S(2)}) collective-permute-start(bf16[13,64,256]{2,1,0:T(8,128)(2,1)} %slice_bitcast_fusion), channel_id=1, source_target_pairs={{8,0},{16,8},{24,16},{32,24},{40,32},{48,40},{56,48},{64,56},{72,6... | collective-permute-start | bytes 1277960 | tf_op jit(solution)/shard_map/ppermute | solution.py:225
  34.9 0.0 copy-done.5
  34.9 0.1 copy.16.refs_1_
  35.0 0.0 copy-done.6
  35.0 0.1 copy.17.refs_2_
  35.1 9.9 %collective-permute-done.1.refs_4_ = bf16[13,64,256]{2,1,0:T(8,128)(2,1)} collective-permute-done((bf16[13,64,256]{2,1,0:T(8,128)(2,1)}, bf16[13,64,256]{2,1,0:T(8,128)(2,1)}, u32[]{:S(2)}, u32[]{:S(2)}) %collective-permute-start.1) | collective-permute-done | bytes 426016 | tf_op jit(solution)/shard_map/ppermute | solution.py:225
  44.9 0.0 copy-done
  44.9 0.0 copy-done.4
  44.9 3.2 %forward.1 = (f32[896,256]{1,0:T(8,128)S(1)}, bf16[3,1024,256]{2,1,0:T(8,128)(2,1)S(1)}) custom-call(s32[8]{0:T(128)S(1)} %bitcast.18, s32[8,2]{1,0:T(8,128)S(1)} %copy.16.refs_1_, s32[8,2]{1,0:T(8,128)S(1)} %copy.17.refs_2_, bf16[16,64,256]{2,1,0:T(8,128)(2,1)S(1)} %bitcast.17, bf16[13,64,256]{2,1,0:T(8,128)(2,1)} %collective-permute-done.1.refs_4_, ...), custom_call_target="tpu_custom_call" | custom-call | tf_op jit(solution)/shard_map/forward/pallas_call | solution.py:259
  48.1 0.0 collective-permute-done.refs_3_
  48.2 3.2 %slope.1 = (f32[144,2,8,128]{3,2,1,0:T(8,128)S(1)}, f32[144,2,8,128]{3,2,1,0:T(8,128)S(1)}, bf16[896,256]{1,0:T(8,128)(2,1)S(1)}) custom-call(s32[1]{0:T(128)} %bitcast.3.refs_0_, s32[8]{0:T(128)S(1)} %bitcast.19, bf16[4,2,14,16,256]{4,3,2,1,0:T(8,128)(2,1)S(1)} %all_to_all.25.refs_2_, bf16[4,2,14,16,256]{4,3,2,1,0:T(8,128)(2,1)S(1)} %collective-permute-done.refs_3_, ...), custom_call_target="tpu_custom_call" | custom-call | tf_op jit(solution)/shard_map/slope/pallas_call | solution.py:278
  51.4 0.0 copy-start.2
  51.4 1.9 %collective-permute-start.3 = (f32[144,2,8,128]{3,2,1,0:T(8,128)S(1)}, f32[144,2,8,128]{3,2,1,0:T(8,128)S(1)}, u32[]{:S(2)}, u32[]{:S(2)}) collective-permute-start(f32[144,2,8,128]{3,2,1,0:T(8,128)S(1)} %get-tuple-element.15), channel_id=1, source_target_pairs={{0,1},{1,0},{2,3},{3,2},{4,5},{5,4},{6,7},{7,6},{8,9},{9,8},{10,11... | collective-permute-start | bytes 3538952 | tf_op jit(solution)/shard_map/ppermute | solution.py:321
  53.3 2.8 %collective-permute-done.3 = f32[144,2,8,128]{3,2,1,0:T(8,128)S(1)} collective-permute-done((f32[144,2,8,128]{3,2,1,0:T(8,128)S(1)}, f32[144,2,8,128]{3,2,1,0:T(8,128)S(1)}, u32[]{:S(2)}, u32[]{:S(2)}) %collective-permute-start.3) | collective-permute-done | bytes 1179680 | tf_op jit(solution)/shard_map/ppermute | solution.py:321
  56.1 0.2 add_convert_fusion
  56.4 0.0 copy-done.2
  56.4 15.5 %all_to_all.26 = bf16[16,144,128]{2,1,0:T(8,128)(2,1)S(1)} all-to-all(bf16[16,144,128]{2,1,0:T(8,128)(2,1)S(1)} %bitcast.22), channel_id=1, replica_groups={{0,2,4,6,128,130,132,134,256,258,260,262,384,386,388,390},{1,3,5,7,129,..., dimensions={0} | all-to-all | bytes 1179648 | tf_op jit(solution)/shard_map/all_to_all | solution.py:322
  71.9 0.1 convert_reduce_fusion
  72.0 22.0 %all_to_all.27 = f32[16,9,128]{2,1,0:T(8,128)S(1)} all-to-all(f32[16,9,128]{2,1,0:T(8,128)S(1)} %reshape.35), channel_id=1, replica_groups={{0,8,16,24,32,40,48,56,64,72,80,88,96,104,112,120},{128,136,144,152,160..., dimensions={0} | all-to-all | bytes 147456 | tf_op jit(solution)/shard_map/all_to_all | solution.py:326
  94.0 0.0 copy-start.3
  94.1 16.5 %all_to_all.28 = bf16[16,9,128]{2,1,0:T(8,128)(2,1)S(1)} all-to-all(bf16[16,9,128]{2,1,0:T(8,128)(2,1)S(1)} %broadcast_in_dim.28), channel_id=1, replica_groups={{0,8,16,24,32,40,48,56,64,72,80,88,96,104,112,120},{128,136,144,152,160..., dimensions={0} | all-to-all | bytes 73728 | tf_op jit(solution)/shard_map/all_to_all | solution.py:330
  110.6 0.9 broadcast_in_dim.30
  111.5 5.5 %all-to-all-start.4 = ((bf16[16,144,128]{2,1,0:T(8,128)(2,1)}), bf16[16,144,128]{2,1,0:T(8,128)(2,1)S(1)}, u32[]{:S(2)}, u32[]{:S(2)}) async-start(bf16[16,144,128]{2,1,0:T(8,128)(2,1)} %broadcast_in_dim.30), calls=%async_computation.4 | async-start | bytes 1179648 | tf_op jit(solution)/shard_map/all_to_all | solution.py:332
  117.0 0.0 copy-done.3
  117.1 3.6 %backward.1 = (f32[16,64,256]{2,1,0:T(8,128)S(1)}, bf16[13,64,256]{2,1,0:T(8,128)(2,1)}) custom-call(s32[8]{0:T(128)S(1)} %bitcast.20, s32[8,2]{1,0:T(8,128)S(1)} %copy.16.refs_1_, s32[8,2]{1,0:T(8,128)S(1)} %copy.17.refs_2_, bf16[896,256]{1,0:T(8,128)(2,1)S(1)} %copy-done.3, bf16[9,256,256]{2,1,0:T(8,128)(2,1)S(1)} %copy-done), custom_call_target="tpu_custom_call" | custom-call | tf_op jit(solution)/shard_map/backward/pallas_call | solution.py:292
  120.6 2.7 %collective-permute-start.2 = (bf16[13,64,256]{2,1,0:T(8,128)(2,1)}, bf16[13,64,256]{2,1,0:T(8,128)(2,1)S(1)}, u32[]{:S(2)}, u32[]{:S(2)}) collective-permute-start(bf16[13,64,256]{2,1,0:T(8,128)(2,1)} %get-tuple-element.13), channel_id=1, source_target_pairs={{0,8},{8,16},{16,24},{24,32},{32,40},{40,48},{48,56},{56,64},{64,7... | collective-permute-start | bytes 1277960 | tf_op jit(solution)/shard_map/ppermute | solution.py:225
  123.4 1.8 %all-to-all-done.4 = bf16[16,144,128]{2,1,0:T(8,128)(2,1)S(1)} async-done(((bf16[16,144,128]{2,1,0:T(8,128)(2,1)}), bf16[16,144,128]{2,1,0:T(8,128)(2,1)S(1)}, u32[]{:S(2)}, u32[]{:S(2)}) %all-to-all-start.4) | async-done | bytes 589856 | tf_op jit(solution)/shard_map/all_to_all | solution.py:332
  125.2 1.9 %collective-permute-start.4 = (bf16[2304,128]{1,0:T(8,128)(2,1)S(1)}, bf16[2304,128]{1,0:T(8,128)(2,1)S(1)}, u32[]{:S(2)}, u32[]{:S(2)}) collective-permute-start(bf16[2304,128]{1,0:T(8,128)(2,1)S(1)} %bitcast.15), channel_id=1, source_target_pairs={{0,1},{1,0},{2,3},{3,2},{4,5},{5,4},{6,7},{7,6},{8,9},{9,8},{10,11... | collective-permute-start | bytes 1769480 | tf_op jit(solution)/shard_map/ppermute | solution.py:334
  127.1 6.2 %collective-permute-done.2 = bf16[13,64,256]{2,1,0:T(8,128)(2,1)S(1)} collective-permute-done((bf16[13,64,256]{2,1,0:T(8,128)(2,1)}, bf16[13,64,256]{2,1,0:T(8,128)(2,1)S(1)}, u32[]{:S(2)}, u32[]{:S(2)}) %collective-permute-start.2) | collective-permute-done | bytes 426016 | tf_op jit(solution)/shard_map/ppermute | solution.py:225
  133.3 0.1 convert_add_fusion
  133.4 1.1 maximum_bitcast_fusion
  134.5 0.0 collective-permute-done.4.other_ref
  134.5 1.7 %finish.1 = f32[2304,256]{1,0:T(8,128)} custom-call(s32[1]{0:T(128)} %bitcast.8.core_ref, bf16[2304,128]{1,0:T(8,128)(2,1)S(1)} %bitcast.16, bf16[2304,128]{1,0:T(8,128)(2,1)S(1)} %collective-permute-done.4.other_ref), custom_call_target="tpu_custom_call" | custom-call | tf_op jit(solution)/shard_map/finish/pallas_call | solution.py:335
  (9 shorter events, 0.1 us)
Async XLA Ops:
  2.7 20.1 %copy-start.1 = (bf16[1,16,64,256]{3,2,1,0:T(8,128)(2,1)S(1)}, bf16[1,16,64,256]{3,2,1,0:T(8,128)(2,1)}, u32[]{:S(2)}) copy-start(bf16[1,16,64,256]{3,2,1,0:T(8,128)(2,1)} %param.6) | copy-start | bytes 1572868
  2.7 32.2 %copy-start.5 = (s32[1,1,8,2]{2,3,1,0:T(2,128)S(1)}, s32[1,1,8,2]{2,3,1,0:T(2,128)}, u32[]{:S(2)}) copy-start(s32[1,1,8,2]{2,3,1,0:T(2,128)} %param.10) | copy-start | bytes 196
  2.7 32.3 %copy-start.6 = (s32[1,1,8,2]{2,3,1,0:T(2,128)S(1)}, s32[1,1,8,2]{2,3,1,0:T(2,128)}, u32[]{:S(2)}) copy-start(s32[1,1,8,2]{2,3,1,0:T(2,128)} %param.11) | copy-start | bytes 196
  2.7 42.2 %copy-start = (bf16[9,256,256]{2,1,0:T(8,128)(2,1)S(1)}, bf16[9,256,256]{2,1,0:T(8,128)(2,1)}, u32[]{:S(2)}) copy-start(bf16[9,256,256]{2,1,0:T(8,128)(2,1)} %refs_4_.1) | copy-start | bytes 3538948
  2.7 42.2 %copy-start.4 = (s32[1,1,8]{2,1,0:T(1,128)S(1)}, s32[1,1,8]{2,1,0:T(1,128)}, u32[]{:S(2)}) copy-start(s32[1,1,8]{2,1,0:T(1,128)} %param.9) | copy-start | bytes 100
  20.8 27.3 %collective-permute-start = (bf16[4,2,14,16,256]{4,3,2,1,0:T(8,128)(2,1)S(1)}, bf16[4,2,14,16,256]{4,3,2,1,0:T(8,128)(2,1)S(1)}, u32[]{:S(2)}, u32[]{:S(2)}) collective-permute-start(bf16[4,2,14,16,256]{4,3,2,1,0:T(8,128)(2,1)S(1)} %all_to_all.25.refs_2_), channel_id=1, source_target_pairs={{0,1},{1,0},{2,3},{3,2},{4,5},{5,4},{6,7},{7,6},{8,9},{9,8},{10,11... | collective-permute-start | bytes 2752520 | tf_op jit(solution)/shard_map/ppermute | solution.py:256
  23.5 21.4 %collective-permute-start.1 = (bf16[13,64,256]{2,1,0:T(8,128)(2,1)}, bf16[13,64,256]{2,1,0:T(8,128)(2,1)}, u32[]{:S(2)}, u32[]{:S(2)}) collective-permute-start(bf16[13,64,256]{2,1,0:T(8,128)(2,1)} %slice_bitcast_fusion), channel_id=1, source_target_pairs={{8,0},{16,8},{24,16},{32,24},{40,32},{48,40},{56,48},{64,56},{72,6... | collective-permute-start | bytes 1277960 | tf_op jit(solution)/shard_map/ppermute | solution.py:225
  51.4 5.0 %copy-start.2 = (bf16[896,256]{1,0:T(8,128)(2,1)}, bf16[896,256]{1,0:T(8,128)(2,1)S(1)}, u32[]{:S(2)}) copy-start(bf16[896,256]{1,0:T(8,128)(2,1)S(1)} %get-tuple-element.11.refs_3_) | copy-start | bytes 1376260
  51.4 4.7 %collective-permute-start.3 = (f32[144,2,8,128]{3,2,1,0:T(8,128)S(1)}, f32[144,2,8,128]{3,2,1,0:T(8,128)S(1)}, u32[]{:S(2)}, u32[]{:S(2)}) collective-permute-start(f32[144,2,8,128]{3,2,1,0:T(8,128)S(1)} %get-tuple-element.15), channel_id=1, source_target_pairs={{0,1},{1,0},{2,3},{3,2},{4,5},{5,4},{6,7},{7,6},{8,9},{9,8},{10,11... | collective-permute-start | bytes 3538952 | tf_op jit(solution)/shard_map/ppermute | solution.py:321
  94.0 23.0 %copy-start.3 = (bf16[896,256]{1,0:T(8,128)(2,1)S(1)}, bf16[896,256]{1,0:T(8,128)(2,1)}, u32[]{:S(2)}) copy-start(bf16[896,256]{1,0:T(8,128)(2,1)} %copy-done.2) | copy-start | bytes 1376260
  111.5 13.7 %all-to-all-start.4 = ((bf16[16,144,128]{2,1,0:T(8,128)(2,1)}), bf16[16,144,128]{2,1,0:T(8,128)(2,1)S(1)}, u32[]{:S(2)}, u32[]{:S(2)}) async-start(bf16[16,144,128]{2,1,0:T(8,128)(2,1)} %broadcast_in_dim.30), calls=%async_computation.4 | async-start | bytes 1179648 | tf_op jit(solution)/shard_map/all_to_all | solution.py:332
  120.6 12.7 %collective-permute-start.2 = (bf16[13,64,256]{2,1,0:T(8,128)(2,1)}, bf16[13,64,256]{2,1,0:T(8,128)(2,1)S(1)}, u32[]{:S(2)}, u32[]{:S(2)}) collective-permute-start(bf16[13,64,256]{2,1,0:T(8,128)(2,1)} %get-tuple-element.13), channel_id=1, source_target_pairs={{0,8},{8,16},{16,24},{24,32},{32,40},{40,48},{48,56},{56,64},{64,7... | collective-permute-start | bytes 1277960 | tf_op jit(solution)/shard_map/ppermute | solution.py:225
  125.2 9.3 %collective-permute-start.4 = (bf16[2304,128]{1,0:T(8,128)(2,1)S(1)}, bf16[2304,128]{1,0:T(8,128)(2,1)S(1)}, u32[]{:S(2)}, u32[]{:S(2)}) collective-permute-start(bf16[2304,128]{1,0:T(8,128)(2,1)S(1)} %bitcast.15), channel_id=1, source_target_pairs={{0,1},{1,0},{2,3},{3,2},{4,5},{5,4},{6,7},{7,6},{8,9},{9,8},{10,11... | collective-permute-start | bytes 1769480 | tf_op jit(solution)/shard_map/ppermute | solution.py:334

commit v4 on v3

v4 whole, which is shorter than its diff:
```python
import jax
import jax.numpy as jnp
from jax import lax
from jax.experimental import pallas as pl
from jax.experimental.pallas import tpu as pltpu
from jax.sharding import PartitionSpec as P


GELU_SCALE = 0.7978845608
GELU_CUBIC = 0.044715
F32 = jnp.float32
BF16 = jnp.bfloat16
VMEM_BYTES = 20 * 2**20
XP = 16
LEFT = 8


def gelu_slope(values):
    inner = GELU_SCALE * (values + GELU_CUBIC * values * values * values)
    tangent = jnp.tanh(inner)
    outer = (
        0.5
        * values
        * (1.0 - tangent * tangent)
        * GELU_SCALE
        * (1.0 + 3.0 * GELU_CUBIC * values * values)
    )
    return 0.5 * (1.0 + tangent) + outer


def list_slots(dims, count_of, slot, fields):
    _, slots, heads, cap = dims
    width = slot.shape[0]
    for index in range(slots):
        for field in range(width):
            slot[field, index] = 0

    def head(j, used):
        count = count_of(j)
        for r in range(cap):
            live = (r < count) & (used < slots)

            @pl.when(live)
            def _():
                for field, value in enumerate(fields(j, r)):
                    slot[field, used] = value

            used = used + live.astype(jnp.int32)
        return used

    return lax.fori_loop(0, heads, head, 0)


def crop_kernel(dims, own_ref, row_ref, col_ref, map_ref, below_ref, crop_ref, wide, slot):
    side, slots, _, _ = dims
    high, width, channels = map_ref.shape
    halo = side - 1
    area = side * XP
    used = list_slots(dims, lambda j: own_ref[j], slot, lambda j, r: (row_ref[j, r], col_ref[j, r]))

    wide[pl.ds(0, high), pl.ds(LEFT, width), :] = map_ref[...].astype(F32)
    wide[pl.ds(high, halo), pl.ds(LEFT, width), :] = below_ref[pl.ds(0, halo)].astype(F32)

    columns = lax.broadcasted_iota(jnp.int32, (side, XP, channels), 1)
    for s in range(slots):
        left = slot[1, s]
        base = pl.multiple_of(left // 8 * 8, 8)
        window = wide[pl.ds(slot[0, s], side), pl.ds(base + LEFT, 3 * XP // 2), :]
        window = pltpu.roll(window, lax.rem(3 * XP // 2 - lax.rem(left, 8), 3 * XP // 2), 1)[:, :XP]
        last = jnp.where(s < used, side, 0)
        window = jnp.where(columns < last, window, 0.0).astype(BF16)
        crop_ref[pl.ds(s * area, area), :] = window.reshape(area, channels)


def forward_kernel(dims, me_ref, own_ref, other_ref, weight_ref, gelu_ref, gelu_other_ref, shifted):
    side, slots, _, _ = dims
    channels = own_ref.shape[1]
    half = channels // 2
    area = side * XP
    padded = (side + 2) * XP
    core = lax.rem(me_ref[0], 2)
    lanes = pl.ds(pl.multiple_of(core * half, half), half)

    none = jnp.zeros((XP, channels), BF16)
    for s in range(2 * slots):
        source = own_ref if s < slots else other_ref
        crop = source[pl.ds(s % slots * area, area), :]
        loose = crop.astype(F32)
        for b in range(3):
            moved = crop if b == 1 else pltpu.roll(loose, (area + 1 - b) % area, 0).astype(BF16)
            shifted[b, pl.ds(s * padded, XP), :] = none
            shifted[b, pl.ds(s * padded + XP, area), :] = moved
            shifted[b, pl.ds(s * padded + XP + area, XP), :] = none

    for s in range(2 * slots):
        taps = [
            shifted[b, pl.ds(s * padded + a * XP, area), :] for a in range(3) for b in range(3)
        ]
        lhs = jnp.concatenate(taps, axis=1)
        rows = pl.ds(s % slots * area, area)
        if s < slots:
            matrix = weight_ref[...].reshape(9 * channels, channels)
            gelu_ref[rows, :] = gelu_slope(jnp.dot(lhs, matrix, preferred_element_type=F32))
        else:
            matrix = weight_ref[:, :, lanes].reshape(9 * channels, half)
            gelu_other_ref[rows, :] = gelu_slope(jnp.dot(lhs, matrix, preferred_element_type=F32))


def slope_kernel(dims, me_ref, own_ref, ours_ref, across_ref, gelu_ref, gelu_other_ref, shifted,
                 terms_ref, slope_ref, slid, prior, partner_count, slot, partner_slot):
    side, slots, heads, _ = dims
    boxes = ours_ref.shape[1]
    channels = gelu_ref.shape[1]
    half = channels // 2
    area = side * XP
    padded = (side + 2) * XP
    me = me_ref[0]
    core = lax.rem(me, 2)
    even = me - core
    partner = even + 1 - core
    lanes = pl.ds(pl.multiple_of(core * half, half), half)

    lane = lax.broadcasted_iota(jnp.int32, (8, channels), 1)
    line = lax.broadcasted_iota(jnp.int32, (8, channels), 0)
    totals = jnp.zeros((8, channels), F32)
    counts = jnp.zeros((8, channels), F32)
    for i in range(heads):
        row = jnp.where(core == i % 2, ours_ref[i // 2, 0, 0], across_ref[i // 2, 0, 0]).astype(F32)[8:16]
        totals = totals + jnp.where(i < even, row, 0.0)
        counts = counts + jnp.where(i == partner, row, 0.0)
    totals = jnp.where(line == side - 8, totals, 0.0)
    counts = jnp.where(line == side - 8, counts, 0.0)
    for j in range(heads):
        prior[j] = jnp.sum(jnp.where(lane == j, totals, 0.0)).astype(jnp.int32)
        partner_count[j] = jnp.sum(jnp.where(lane == j, counts, 0.0)).astype(jnp.int32)

    def box(j, r, ahead):
        return j, jnp.minimum(prior[j] + ahead + r, boxes - 1)

    used = list_slots(
        dims, lambda j: own_ref[j], slot, lambda j, r: box(j, r, core * partner_count[j])
    )
    partner_used = list_slots(
        dims, lambda j: partner_count[j], partner_slot, lambda j, r: box(j, r, (1 - core) * own_ref[j])
    )

    def masked(slope, last, width):
        columns = lax.broadcasted_iota(jnp.int32, (side, XP, width), 1).reshape(area, width)
        return jnp.where(columns < last, slope, 0.0).astype(BF16)

    for s in range(2 * slots):
        table, number, count = (slot, s, used) if s < slots else (partner_slot, s - slots, partner_used)
        chip = table[0, number] // 2
        index = table[1, number]
        same = lax.rem(table[0, number], 2) == core
        last = jnp.where(number < count, side, 0)
        rows = pl.ds(number * area, area)
        if s < slots:
            upstream = jnp.where(same, ours_ref[chip, index], across_ref[chip, index]).astype(F32)
            slope = masked(upstream.reshape(area, channels) * gelu_ref[rows, :], last, channels)
            slope_ref[rows, :] = slope
            slope = jnp.where(core == 0, slope[:, :half], slope[:, half:])
        else:
            upstream = jnp.where(
                same, ours_ref[chip, index, :, :, lanes], across_ref[chip, index, :, :, lanes]
            ).astype(F32)
            slope = masked(upstream.reshape(area, half) * gelu_other_ref[rows, :], last, half)
        for a in range(3):
            if a > 0:
                slid[a, pl.ds(s * padded, a * XP), :] = jnp.zeros((a * XP, half), BF16)
            slid[a, pl.ds(s * padded + a * XP, area), :] = slope
            if a < 2:
                slid[a, pl.ds(s * padded + a * XP + area, (2 - a) * XP), :] = jnp.zeros(
                    ((2 - a) * XP, half), BF16
                )

    rhs = jnp.concatenate([slid[a] for a in range(3)], axis=1)
    for b in range(3):
        terms = lax.dot_general(
            shifted[b], rhs, (((0,), (0,)), ((), ())), preferred_element_type=F32
        )
        for a in range(3):
            terms_ref[pl.ds((3 * a + b) * channels, channels), :] = (
                terms[:, a * half : (a + 1) * half].astype(BF16)
            )


def backward_kernel(dims, own_ref, row_ref, col_ref, slope_ref, weight_ref, main_ref, spill_ref, canvas, shifted,
                    slot):
    side, slots, _, _ = dims
    high = main_ref.shape[0]
    width = main_ref.shape[1]
    channels = main_ref.shape[2]
    halo = spill_ref.shape[0]
    area = side * XP

    used = list_slots(dims, lambda j: own_ref[j], slot, lambda j, r: (row_ref[j, r], col_ref[j, r]))
    canvas[...] = jnp.zeros(canvas.shape, F32)
    none = jnp.zeros((XP, channels), BF16)
    rhs = jnp.concatenate([weight_ref[k] for k in range(9)], axis=1)
    columns = lax.broadcasted_iota(jnp.int32, (side, XP, channels), 1)
    for s in range(slots):
        slope = slope_ref[pl.ds(s * area, area), :].astype(F32)
        for b in range(3):
            moved = slope if b == 1 else pltpu.roll(slope, (area + b - 1) % area, 0)
            shifted[b, pl.ds(0, XP), :] = none
            shifted[b, pl.ds(XP, area), :] = moved.astype(BF16)
            shifted[b, pl.ds(XP + area, XP), :] = none
        taps = [shifted[b, pl.ds((2 - a) * XP, area), :] for a in range(3) for b in range(3)]
        lhs = jnp.concatenate(taps, axis=1)
        grad = lax.dot_general(lhs, rhs, (((1,), (1,)), ((), ())), preferred_element_type=F32)
        grad = grad.astype(BF16).astype(F32).reshape(side, XP, channels)
        last = jnp.where(s < used, side, 0)
        grad = jnp.where(columns < last, grad, 0.0)
        left = slot[1, s]
        grad = jnp.concatenate([grad, jnp.zeros((side, XP // 2, channels), F32)], axis=1)
        grad = pltpu.roll(grad, lax.rem(left, 8), 1)
        base = pl.multiple_of(left // 8 * 8, 8)
        place = (pl.ds(slot[0, s], side), pl.ds(base, XP + XP // 2), slice(None))
        canvas[place] = canvas[place] + grad
    main_ref[...] = canvas[pl.ds(0, high), pl.ds(0, width), :]
    spill_ref[...] = canvas[pl.ds(high, halo), pl.ds(0, width), :].astype(spill_ref.dtype)


def finish_kernel(core_ref, mine_ref, other_ref, out_ref):
    half = mine_ref.shape[1]
    core = core_ref[0]
    for part in range(2):
        source = jnp.where(core == part, mine_ref[...], other_ref[...])
        out_ref[:, pl.ds(part * half, half)] = source.astype(F32)


def smem():
    return pl.BlockSpec(memory_space=pltpu.SMEM)


def vmem():
    return pl.BlockSpec(memory_space=pltpu.VMEM)


def kernel(body, dims, out_shape, in_specs, scratch_shapes):
    return pl.pallas_call(
        lambda *refs: body(dims, *refs),
        out_shape=out_shape,
        in_specs=in_specs,
        out_specs=jax.tree.map(lambda _: vmem(), out_shape),
        scratch_shapes=scratch_shapes,
        compiler_params=pltpu.CompilerParams(vmem_limit_bytes=VMEM_BYTES),
    )


def shift(array, axis, by):
    length = lax.axis_size(axis)
    pairs = [(i, i + by) for i in range(length) if 0 <= i + by < length]
    return lax.ppermute(array, axis, pairs)


def repeated(array, times):
    return jnp.broadcast_to(array[None], (times,) + array.shape)


def on_device(feature_map, weight, mask_grad, send_count, send_row, send_col):
    tile_map = feature_map[0]
    high, width, channels = tile_map.shape
    boxes, side = mask_grad.shape[2], mask_grad.shape[3]
    heads, cap = send_row.shape[2], send_row.shape[3]
    owners = lax.axis_size("dp")
    tiles = lax.axis_size("tile")
    slots = boxes * cap
    halo = side - 1
    area, padded = side * XP, (side + 2) * XP
    dims = (side, slots, heads, cap)
    me = lax.axis_index("dp")
    me_array = me.reshape(1).astype(jnp.int32)
    own, top_rows, left_cols = send_count[0, 0], send_row[0, 0], send_col[0, 0]
    partner = [(i, i ^ 1) for i in range(owners)]
    chips = owners // 2
    same_core = [[2 * i + c for i in range(chips)] for c in range(2)]

    half = channels // 2
    core = lax.rem(me, 2)

    below = shift(tile_map, "tile", -1)
    spare = jnp.pad(own.astype(BF16), (0, channels - heads))
    spare = jnp.broadcast_to(spare, (boxes, side, XP - side, channels))
    up = jnp.concatenate([mask_grad[0, 0], spare], 2)
    sent = repeated(up, chips)
    ups = lax.all_to_all(sent, "dp", 0, 0, axis_index_groups=same_core, tiled=True)
    partner_ups = lax.ppermute(ups, "dp", partner)

    crops = kernel(
        crop_kernel,
        dims,
        jax.ShapeDtypeStruct((slots * area, channels), BF16),
        [smem()] * 3 + [vmem()] * 2,
        [
            pltpu.VMEM((high + halo, width + 2 * LEFT, channels), F32),
            pltpu.SMEM((2, slots), jnp.int32),
        ],
    )(own, top_rows, left_cols, tile_map, below)
    partner_crops = lax.ppermute(crops, "dp", partner)

    gelu, gelu_other, shifted = kernel(
        forward_kernel,
        dims,
        (
            pltpu.VMEM((slots * area, channels), F32),
            pltpu.VMEM((slots * area, half), F32),
            pltpu.VMEM((3, 2 * slots * padded, channels), BF16),
        ),
        [smem()] + [vmem()] * 3,
        [],
    )(me_array, crops, partner_crops, weight)

    terms, slope = kernel(
        slope_kernel,
        dims,
        (
            jax.ShapeDtypeStruct((9 * channels, half), BF16),
            jax.ShapeDtypeStruct((slots * area, channels), BF16),
        ),
        [smem()] * 2 + [vmem()] * 5,
        [
            pltpu.VMEM((3, 2 * slots * padded, half), BF16),
            pltpu.SMEM((heads,), jnp.int32),
            pltpu.SMEM((heads,), jnp.int32),
            pltpu.SMEM((2, slots), jnp.int32),
            pltpu.SMEM((2, slots), jnp.int32),
        ],
    )(me_array, own, ups, partner_ups, gelu, gelu_other, shifted)

    main, spill = pl.pallas_call(
        lambda *refs: backward_kernel(dims, *refs),
        out_shape=(
            jax.ShapeDtypeStruct((high, width, channels), F32),
            jax.ShapeDtypeStruct((halo, width, channels), BF16),
        ),
        in_specs=[smem()] * 3 + [vmem()] * 2,
        out_specs=(vmem(), vmem()),
        scratch_shapes=[
            pltpu.VMEM((high + halo, width + XP, channels), F32),
            pltpu.VMEM((3, padded, channels), BF16),
            pltpu.SMEM((2, slots), jnp.int32),
        ],
        name="backward",
        compiler_params=pltpu.CompilerParams(vmem_limit_bytes=VMEM_BYTES),
    )(own, top_rows, left_cols, slope, weight)
    arriving = shift(spill, "tile", 1)
    arriving = arriving.astype(F32)
    map_grad = jnp.concatenate([main[:halo] + arriving, main[halo:]], 0)

    part = 9 * channels
    deep = 16 if tiles % 16 == 0 else 1
    wide = tiles // deep
    plane = [
        [(x * deep + z) * owners + 2 * y + c for x in range(wide) for y in range(chips)]
        for z in range(deep)
        for c in range(2)
    ]
    stick = [[x * deep + z for z in range(deep)] for x in range(wide)]
    near = wide * chips
    got = lax.all_to_all(
        terms.reshape(near, part // near, half), ("tile", "dp"), 0, 0, axis_index_groups=plane, tiled=True
    )
    column = got.astype(F32).sum(0)
    got = lax.all_to_all(
        column.reshape(deep, part // near // deep, half), "tile", 0, 0, axis_index_groups=stick, tiled=True
    )
    chunk = (got.sum(0) / (boxes * tiles * owners)).astype(BF16)
    got = lax.all_to_all(repeated(chunk, deep), "tile", 0, 0, axis_index_groups=stick, tiled=True)
    got = got.reshape(part // near, half)
    got = lax.all_to_all(repeated(got, near), ("tile", "dp"), 0, 0, axis_index_groups=plane, tiled=True)
    got = got.reshape(part, half)
    other = lax.ppermute(got, "dp", partner)
    weight_grad = pl.pallas_call(
        finish_kernel,
        out_shape=jax.ShapeDtypeStruct((9 * channels, channels), F32),
        in_specs=[smem(), vmem(), vmem()],
        out_specs=vmem(),
        name="finish",
        compiler_params=pltpu.CompilerParams(vmem_limit_bytes=VMEM_BYTES),
    )(core.reshape(1), got, other)
    return map_grad[None], weight_grad.reshape(9, channels, channels)


def solution(mesh):
    in_specs = (
        P("dp", "tile", None, None),
        P(),
        P("dp", "tile", None, None, None, None),
        P("dp", "tile", None),
        P("dp", "tile", None, None),
        P("dp", "tile", None, None),
    )
    out_specs = (P("dp", "tile", None, None), P())

    return jax.shard_map(
        on_device, mesh=mesh, in_specs=in_specs, out_specs=out_specs, check_vma=False
    )
```

time: 137 us -> 127 us (0.927)
  the two profiles are of different devices: /device:TPU:4 before, /device:TPU:6 now
where the time goes in v4:
time: 127 us; the launch traced here: 126 us
  blocking collectives  55.6 us (44%)
  starting transfers between devices  30.2 us (24%)
  waiting for transfers between devices  19 us (15%)
  Pallas kernels  13.3 us (10%)
  other arithmetic  4.21 us (3%)
  local copies, waits for them, and re-layouts  3.21 us (3%)
    all_to_all x1, blocking collectives, on_device(): lax.all_to_all(column.reshape(deep, part // near // deep, half), 'tile',...  21.9 us
    all_to_all x1, blocking collectives, on_device(): lax.all_to_all(terms.reshape(near, part // near, half), ('tile', 'dp'), 0...  17.5 us
    all_to_all x1, blocking collectives, on_device(): lax.all_to_all(repeated(chunk, deep), 'tile', 0, 0, axis_index_groups=sti...  16.1 us
    ppermute x2, starting transfers between devices, shift(): return lax.ppermute(array, axis, pairs)  14.4 us
    ppermute x2, waiting for transfers between devices, shift(): return lax.ppermute(array, axis, pairs)  13.2 us
    all_to_all x1, starting transfers between devices, on_device(): lax.all_to_all(repeated(got, near), ('tile', 'dp'), 0, 0, axis_index_grou...  5.66 us
    all_to_all x1, starting transfers between devices, on_device(): lax.all_to_all(sent, 'dp', 0, 0, axis_index_groups=same_core, tiled=True)  4.46 us
    pallas_call x1, Pallas kernels, on_device(): kernel(forward_kernel, dims, (pltpu.VMEM((slots * area, channels), F32),...  3.99 us
  transfers between devices with their start and end apart: 7, of which 5 were waited for; matrix products, arithmetic and copies ran while one was open for 2% of the time, Pallas kernels for 7%

profile of v4, /device:TPU:6, one launch (start us, length us, event | category | flops | bytes accessed | tf_op | source)
XLA Modules:
  0.0 126.3 jit_solution(15660809924191704082)
XLA Ops:
  0.6 0.0 copy-start.3
  0.6 0.0 copy-start.4
  0.7 0.0 copy-start.5
  0.7 0.7 bitcast_convert_fusion
  1.4 1.2 pad_maximum_fusion
  2.7 0.0 copy-start
  2.7 1.0 broadcast_in_dim.26
  3.7 4.5 %all-to-all-start = ((bf16[4,2,14,16,256]{4,3,2,1,0:T(8,128)(2,1)}), bf16[4,2,14,16,256]{4,3,2,1,0:T(8,128)(2,1)S(1)}, u32[]{:S(2)}, u32[]{:S(2)}) async-start(bf16[4,2,14,16,256]{4,3,2,1,0:T(8,128)(2,1)} %broadcast_in_dim.26), calls=%async_computation | async-start | bytes 1835008 | tf_op jit(solution)/shard_map/all_to_all | solution.py:288
  8.1 11.7 %collective-permute-start.1 = (bf16[16,64,256]{2,1,0:T(8,128)(2,1)}, bf16[16,64,256]{2,1,0:T(8,128)(2,1)}, u32[]{:S(2)}, u32[]{:S(2)}) collective-permute-start(bf16[16,64,256]{2,1,0:T(8,128)(2,1)} %bitcast.5.refs_3_), channel_id=1, source_target_pairs={{8,0},{16,8},{24,16},{32,24},{40,32},{48,40},{56,48},{64,56},{72,6... | collective-permute-start | bytes 1572872 | tf_op jit(solution)/shard_map/ppermute | solution.py:255
  19.8 2.0 %all-to-all-done.refs_2_ = bf16[4,2,14,16,256]{4,3,2,1,0:T(8,128)(2,1)S(1)} async-done(((bf16[4,2,14,16,256]{4,3,2,1,0:T(8,128)(2,1)}), bf16[4,2,14,16,256]{4,3,2,1,0:T(8,128)(2,1)S(1)}, u32[]{:S(2)}, u32[]{:S(2)}) %all-to-all-start) | async-done | bytes 917536 | tf_op jit(solution)/shard_map/all_to_all | solution.py:288
  21.8 1.9 %collective-permute-start = (bf16[4,2,14,16,256]{4,3,2,1,0:T(8,128)(2,1)S(1)}, bf16[4,2,14,16,256]{4,3,2,1,0:T(8,128)(2,1)S(1)}, u32[]{:S(2)}, u32[]{:S(2)}) collective-permute-start(bf16[4,2,14,16,256]{4,3,2,1,0:T(8,128)(2,1)S(1)} %all-to-all-done.refs_2_), channel_id=1, source_target_pairs={{0,1},{1,0},{2,3},{3,2},{4,5},{5,4},{6,7},{7,6},{8,9},{9,8},{10,11... | collective-permute-start | bytes 2752520 | tf_op jit(solution)/shard_map/ppermute | solution.py:289
  23.8 0.0 copy-done.4
  23.8 0.1 copy.16.refs_1_
  23.8 0.0 copy-done.5
  23.8 0.1 copy.17.refs_2_
  23.9 7.1 %collective-permute-done.1.refs_4_ = bf16[16,64,256]{2,1,0:T(8,128)(2,1)} collective-permute-done((bf16[16,64,256]{2,1,0:T(8,128)(2,1)}, bf16[16,64,256]{2,1,0:T(8,128)(2,1)}, u32[]{:S(2)}, u32[]{:S(2)}) %collective-permute-start.1) | collective-permute-done | bytes 524320 | tf_op jit(solution)/shard_map/ppermute | solution.py:255
  31.0 0.0 copy-done.3
  31.0 1.8 %shard_map.77.refs_1_ = bf16[896,256]{1,0:T(8,128)(2,1)S(1)} custom-call(s32[8]{0:T(128)S(1)} %bitcast.16, s32[8,2]{1,0:T(8,128)S(1)} %copy.16.refs_1_, s32[8,2]{1,0:T(8,128)S(1)} %copy.17.refs_2_, bf16[16,64,256]{2,1,0:T(8,128)(2,1)} %bitcast.5.refs_3_, bf16[16,64,256]{2,1,0:T(8,128)(2,1)} %collective-permute-done.1.refs_4_), custom_call_target="tpu_custom_call" | custom-call | tf_op jit(solution)/shard_map/pallas_call | solution.py:291
  32.8 1.9 %collective-permute-start.2 = (bf16[896,256]{1,0:T(8,128)(2,1)S(1)}, bf16[896,256]{1,0:T(8,128)(2,1)}, u32[]{:S(2)}, u32[]{:S(2)}) collective-permute-start(bf16[896,256]{1,0:T(8,128)(2,1)S(1)} %shard_map.77.refs_1_), channel_id=1, source_target_pairs={{0,1},{1,0},{2,3},{3,2},{4,5},{5,4},{6,7},{7,6},{8,9},{9,8},{10,11... | collective-permute-start | bytes 1376264 | tf_op jit(solution)/shard_map/ppermute | solution.py:301
  34.7 1.9 %collective-permute-done.2.refs_2_ = bf16[896,256]{1,0:T(8,128)(2,1)} collective-permute-done((bf16[896,256]{1,0:T(8,128)(2,1)S(1)}, bf16[896,256]{1,0:T(8,128)(2,1)}, u32[]{:S(2)}, u32[]{:S(2)}) %collective-permute-start.2) | collective-permute-done | bytes 458784 | tf_op jit(solution)/shard_map/ppermute | solution.py:301
  36.6 0.0 copy-done
  36.6 4.0 %shard_map.78 = (f32[896,256]{1,0:T(8,128)S(1)}, f32[896,128]{1,0:T(8,128)S(1)}, bf16[3,2048,256]{2,1,0:T(8,128)(2,1)S(1)}) custom-call(s32[1]{0:T(128)} %bitcast.3.refs_0_, bf16[896,256]{1,0:T(8,128)(2,1)S(1)} %shard_map.77.refs_1_, bf16[896,256]{1,0:T(8,128)(2,1)} %collective-permute-done.2.refs_2_, bf16[9,256,256]{2,1,0:T(8,128)(2,1)S(1)} %copy-done), custom_call_target="tpu_custom_call" | custom-call | tf_op jit(solution)/shard_map/pallas_call | solution.py:303
  40.6 0.0 collective-permute-done.refs_3_
  40.6 3.0 %shard_map.79 = (bf16[2304,128]{1,0:T(8,128)(2,1)S(1)}, bf16[896,256]{1,0:T(8,128)(2,1)S(1)}) custom-call(s32[1]{0:T(128)} %bitcast.3.refs_0_, s32[8]{0:T(128)S(1)} %bitcast.17, bf16[4,2,14,16,256]{4,3,2,1,0:T(8,128)(2,1)S(1)} %all-to-all-done.refs_2_, bf16[4,2,14,16,256]{4,3,2,1,0:T(8,128)(2,1)S(1)} %collective-permute-done.refs_3_, ...), custom_call_target="tpu_custom_call" | custom-call | tf_op jit(solution)/shard_map/pallas_call | solution.py:315
  43.7 0.0 copy-start.1
  43.7 17.5 %all_to_all.25 = bf16[16,144,128]{2,1,0:T(8,128)(2,1)S(1)} all-to-all(bf16[16,144,128]{2,1,0:T(8,128)(2,1)S(1)} %bitcast.15), channel_id=1, replica_groups={{0,2,4,6,128,130,132,134,256,258,260,262,384,386,388,390},{1,3,5,7,129,..., dimensions={0} | all-to-all | bytes 1179648 | tf_op jit(solution)/shard_map/all_to_all | solution.py:362
  61.2 0.1 convert_reduce_fusion
  61.3 21.9 %all_to_all.26 = f32[16,9,128]{2,1,0:T(8,128)S(1)} all-to-all(f32[16,9,128]{2,1,0:T(8,128)S(1)} %reshape.31), channel_id=1, replica_groups={{0,8,16,24,32,40,48,56,64,72,80,88,96,104,112,120},{128,136,144,152,160..., dimensions={0} | all-to-all | bytes 147456 | tf_op jit(solution)/shard_map/all_to_all | solution.py:366
  83.3 16.1 %all_to_all.27 = bf16[16,9,128]{2,1,0:T(8,128)(2,1)S(1)} all-to-all(bf16[16,9,128]{2,1,0:T(8,128)(2,1)S(1)} %broadcast_in_dim.28), channel_id=1, replica_groups={{0,8,16,24,32,40,48,56,64,72,80,88,96,104,112,120},{128,136,144,152,160..., dimensions={0} | all-to-all | bytes 73728 | tf_op jit(solution)/shard_map/all_to_all | solution.py:370
  99.5 0.9 broadcast_in_dim.30
  100.4 5.7 %all-to-all-start.4 = ((bf16[16,144,128]{2,1,0:T(8,128)(2,1)}), bf16[16,144,128]{2,1,0:T(8,128)(2,1)S(1)}, u32[]{:S(2)}, u32[]{:S(2)}) async-start(bf16[16,144,128]{2,1,0:T(8,128)(2,1)} %broadcast_in_dim.30), calls=%async_computation.4 | async-start | bytes 1179648 | tf_op jit(solution)/shard_map/all_to_all | solution.py:372
  106.0 0.0 copy-done.1
  106.0 0.0 copy-start.2
  106.0 1.0 copy-done.2
  107.0 2.8 %backward.1 = (f32[16,64,256]{2,1,0:T(8,128)S(1)}, bf16[13,64,256]{2,1,0:T(8,128)(2,1)S(1)}) custom-call(s32[8]{0:T(128)S(1)} %bitcast.18, s32[8,2]{1,0:T(8,128)S(1)} %copy.16.refs_1_, s32[8,2]{1,0:T(8,128)S(1)} %copy.17.refs_2_, bf16[896,256]{1,0:T(8,128)(2,1)S(1)} %copy-done.2, bf16[9,256,256]{2,1,0:T(8,128)(2,1)S(1)} %copy-done), custom_call_target="tpu_custom_call" | custom-call | tf_op jit(solution)/shard_map/backward/pallas_call | solution.py:332
  109.9 2.7 %collective-permute-start.3 = (bf16[13,64,256]{2,1,0:T(8,128)(2,1)S(1)}, bf16[13,64,256]{2,1,0:T(8,128)(2,1)}, u32[]{:S(2)}, u32[]{:S(2)}) collective-permute-start(bf16[13,64,256]{2,1,0:T(8,128)(2,1)S(1)} %get-tuple-element.14), channel_id=1, source_target_pairs={{0,8},{8,16},{16,24},{24,32},{32,40},{40,48},{48,56},{56,64},{64,7... | collective-permute-start | bytes 1277960 | tf_op jit(solution)/shard_map/ppermute | solution.py:255
  112.6 1.8 %all-to-all-done.4 = bf16[16,144,128]{2,1,0:T(8,128)(2,1)S(1)} async-done(((bf16[16,144,128]{2,1,0:T(8,128)(2,1)}), bf16[16,144,128]{2,1,0:T(8,128)(2,1)S(1)}, u32[]{:S(2)}, u32[]{:S(2)}) %all-to-all-start.4) | async-done | bytes 589856 | tf_op jit(solution)/shard_map/all_to_all | solution.py:372
  114.4 1.9 %collective-permute-start.4 = (bf16[2304,128]{1,0:T(8,128)(2,1)S(1)}, bf16[2304,128]{1,0:T(8,128)(2,1)S(1)}, u32[]{:S(2)}, u32[]{:S(2)}) collective-permute-start(bf16[2304,128]{1,0:T(8,128)(2,1)S(1)} %bitcast.13), channel_id=1, source_target_pairs={{0,1},{1,0},{2,3},{3,2},{4,5},{5,4},{6,7},{7,6},{8,9},{9,8},{10,11... | collective-permute-start | bytes 1769480 | tf_op jit(solution)/shard_map/ppermute | solution.py:374
  116.3 6.1 %collective-permute-done.3 = bf16[13,64,256]{2,1,0:T(8,128)(2,1)} collective-permute-done((bf16[13,64,256]{2,1,0:T(8,128)(2,1)S(1)}, bf16[13,64,256]{2,1,0:T(8,128)(2,1)}, u32[]{:S(2)}, u32[]{:S(2)}) %collective-permute-start.3) | collective-permute-done | bytes 426016 | tf_op jit(solution)/shard_map/ppermute | solution.py:255
  122.5 1.1 convert_add_fusion
  123.6 1.1 maximum_bitcast_fusion
  124.6 0.0 collective-permute-done.4.other_ref
  124.6 1.7 %finish.1 = f32[2304,256]{1,0:T(8,128)} custom-call(s32[1]{0:T(128)} %bitcast.7.core_ref, bf16[2304,128]{1,0:T(8,128)(2,1)S(1)} %bitcast.14, bf16[2304,128]{1,0:T(8,128)(2,1)S(1)} %collective-permute-done.4.other_ref), custom_call_target="tpu_custom_call" | custom-call | tf_op jit(solution)/shard_map/finish/pallas_call | solution.py:375
  (9 shorter events, 0.1 us)
Async XLA Ops:
  0.6 30.4 %copy-start.3 = (s32[1,1,8]{2,1,0:T(1,128)S(1)}, s32[1,1,8]{2,1,0:T(1,128)}, u32[]{:S(2)}) copy-start(s32[1,1,8]{2,1,0:T(1,128)} %param.9) | copy-start | bytes 100
  0.6 23.1 %copy-start.4 = (s32[1,1,8,2]{2,3,1,0:T(2,128)S(1)}, s32[1,1,8,2]{2,3,1,0:T(2,128)}, u32[]{:S(2)}) copy-start(s32[1,1,8,2]{2,3,1,0:T(2,128)} %param.10) | copy-start | bytes 196
  0.7 23.2 %copy-start.5 = (s32[1,1,8,2]{2,3,1,0:T(2,128)S(1)}, s32[1,1,8,2]{2,3,1,0:T(2,128)}, u32[]{:S(2)}) copy-start(s32[1,1,8,2]{2,3,1,0:T(2,128)} %param.11) | copy-start | bytes 196
  2.7 34.0 %copy-start = (bf16[9,256,256]{2,1,0:T(8,128)(2,1)S(1)}, bf16[9,256,256]{2,1,0:T(8,128)(2,1)}, u32[]{:S(2)}) copy-start(bf16[9,256,256]{2,1,0:T(8,128)(2,1)} %refs_4_.1) | copy-start | bytes 3538948
  3.7 18.2 %all-to-all-start = ((bf16[4,2,14,16,256]{4,3,2,1,0:T(8,128)(2,1)}), bf16[4,2,14,16,256]{4,3,2,1,0:T(8,128)(2,1)S(1)}, u32[]{:S(2)}, u32[]{:S(2)}) async-start(bf16[4,2,14,16,256]{4,3,2,1,0:T(8,128)(2,1)} %broadcast_in_dim.26), calls=%async_computation | async-start | bytes 1835008 | tf_op jit(solution)/shard_map/all_to_all | solution.py:288
  8.1 22.9 %collective-permute-start.1 = (bf16[16,64,256]{2,1,0:T(8,128)(2,1)}, bf16[16,64,256]{2,1,0:T(8,128)(2,1)}, u32[]{:S(2)}, u32[]{:S(2)}) collective-permute-start(bf16[16,64,256]{2,1,0:T(8,128)(2,1)} %bitcast.5.refs_3_), channel_id=1, source_target_pairs={{8,0},{16,8},{24,16},{32,24},{40,32},{48,40},{56,48},{64,56},{72,6... | collective-permute-start | bytes 1572872 | tf_op jit(solution)/shard_map/ppermute | solution.py:255
  21.8 18.8 %collective-permute-start = (bf16[4,2,14,16,256]{4,3,2,1,0:T(8,128)(2,1)S(1)}, bf16[4,2,14,16,256]{4,3,2,1,0:T(8,128)(2,1)S(1)}, u32[]{:S(2)}, u32[]{:S(2)}) collective-permute-start(bf16[4,2,14,16,256]{4,3,2,1,0:T(8,128)(2,1)S(1)} %all-to-all-done.refs_2_), channel_id=1, source_target_pairs={{0,1},{1,0},{2,3},{3,2},{4,5},{5,4},{6,7},{7,6},{8,9},{9,8},{10,11... | collective-permute-start | bytes 2752520 | tf_op jit(solution)/shard_map/ppermute | solution.py:289
  32.8 3.8 %collective-permute-start.2 = (bf16[896,256]{1,0:T(8,128)(2,1)S(1)}, bf16[896,256]{1,0:T(8,128)(2,1)}, u32[]{:S(2)}, u32[]{:S(2)}) collective-permute-start(bf16[896,256]{1,0:T(8,128)(2,1)S(1)} %shard_map.77.refs_1_), channel_id=1, source_target_pairs={{0,1},{1,0},{2,3},{3,2},{4,5},{5,4},{6,7},{7,6},{8,9},{9,8},{10,11... | collective-permute-start | bytes 1376264 | tf_op jit(solution)/shard_map/ppermute | solution.py:301
  43.7 62.3 %copy-start.1 = (bf16[896,256]{1,0:T(8,128)(2,1)}, bf16[896,256]{1,0:T(8,128)(2,1)S(1)}, u32[]{:S(2)}) copy-start(bf16[896,256]{1,0:T(8,128)(2,1)S(1)} %get-tuple-element.12.refs_3_) | copy-start | bytes 1376260
  100.4 14.0 %all-to-all-start.4 = ((bf16[16,144,128]{2,1,0:T(8,128)(2,1)}), bf16[16,144,128]{2,1,0:T(8,128)(2,1)S(1)}, u32[]{:S(2)}, u32[]{:S(2)}) async-start(bf16[16,144,128]{2,1,0:T(8,128)(2,1)} %broadcast_in_dim.30), calls=%async_computation.4 | async-start | bytes 1179648 | tf_op jit(solution)/shard_map/all_to_all | solution.py:372
  106.0 1.0 copy-start.2
  109.9 12.6 %collective-permute-start.3 = (bf16[13,64,256]{2,1,0:T(8,128)(2,1)S(1)}, bf16[13,64,256]{2,1,0:T(8,128)(2,1)}, u32[]{:S(2)}, u32[]{:S(2)}) collective-permute-start(bf16[13,64,256]{2,1,0:T(8,128)(2,1)S(1)} %get-tuple-element.14), channel_id=1, source_target_pairs={{0,8},{8,16},{16,24},{24,32},{32,40},{40,48},{48,56},{56,64},{64,7... | collective-permute-start | bytes 1277960 | tf_op jit(solution)/shard_map/ppermute | solution.py:255
  114.4 10.3 %collective-permute-start.4 = (bf16[2304,128]{1,0:T(8,128)(2,1)S(1)}, bf16[2304,128]{1,0:T(8,128)(2,1)S(1)}, u32[]{:S(2)}, u32[]{:S(2)}) collective-permute-start(bf16[2304,128]{1,0:T(8,128)(2,1)S(1)} %bitcast.13), channel_id=1, source_target_pairs={{0,1},{1,0},{2,3},{3,2},{4,5},{5,4},{6,7},{7,6},{8,9},{9,8},{10,11... | collective-permute-start | bytes 1769480 | tf_op jit(solution)/shard_map/ppermute | solution.py:374

commit v5 on v4

--- a/solution.py
+++ b/solution.py
@@ -72,7 +72,7 @@
         crop_ref[pl.ds(s * area, area), :] = window.reshape(area, channels)
 
 
-def forward_kernel(dims, me_ref, own_ref, other_ref, weight_ref, gelu_ref, gelu_other_ref, shifted):
+def forward_kernel(dims, me_ref, own_ref, other_ref, weight_ref, gelu_ref, shifted):
     side, slots, _, _ = dims
     channels = own_ref.shape[1]
     half = channels // 2
@@ -92,26 +92,23 @@
             shifted[b, pl.ds(s * padded + XP, area), :] = moved
             shifted[b, pl.ds(s * padded + XP + area, XP), :] = none
 
+    matrix = weight_ref[:, :, lanes].reshape(9 * channels, half)
     for s in range(2 * slots):
         taps = [
             shifted[b, pl.ds(s * padded + a * XP, area), :] for a in range(3) for b in range(3)
         ]
         lhs = jnp.concatenate(taps, axis=1)
-        rows = pl.ds(s % slots * area, area)
-        if s < slots:
-            matrix = weight_ref[...].reshape(9 * channels, channels)
-            gelu_ref[rows, :] = gelu_slope(jnp.dot(lhs, matrix, preferred_element_type=F32))
-        else:
-            matrix = weight_ref[:, :, lanes].reshape(9 * channels, half)
-            gelu_other_ref[rows, :] = gelu_slope(jnp.dot(lhs, matrix, preferred_element_type=F32))
-
-
-def slope_kernel(dims, me_ref, own_ref, ours_ref, across_ref, gelu_ref, gelu_other_ref, shifted,
-                 terms_ref, slope_ref, slid, prior, partner_count, slot, partner_slot):
+        gelu_ref[pl.ds(s * area, area), :] = gelu_slope(
+            jnp.dot(lhs, matrix, preferred_element_type=F32)
+        )
+
+
+def slope_kernel(dims, me_ref, own_ref, ours_ref, across_ref, gelu_ref, shifted,
+                 terms_ref, slope_ref, lent_ref, slid, prior, partner_count, slot, partner_slot, staged, sems):
     side, slots, heads, _ = dims
     boxes = ours_ref.shape[1]
-    channels = gelu_ref.shape[1]
-    half = channels // 2
+    half = gelu_ref.shape[1]
+    channels = 2 * half
     area = side * XP
     padded = (side + 2) * XP
     me = me_ref[0]
@@ -120,12 +117,14 @@
     partner = even + 1 - core
     lanes = pl.ds(pl.multiple_of(core * half, half), half)
 
-    lane = lax.broadcasted_iota(jnp.int32, (8, channels), 1)
-    line = lax.broadcasted_iota(jnp.int32, (8, channels), 0)
-    totals = jnp.zeros((8, channels), F32)
-    counts = jnp.zeros((8, channels), F32)
+    lane = lax.broadcasted_iota(jnp.int32, (8, half), 1)
+    line = lax.broadcasted_iota(jnp.int32, (8, half), 0)
+    totals = jnp.zeros((8, half), F32)
+    counts = jnp.zeros((8, half), F32)
     for i in range(heads):
-        row = jnp.where(core == i % 2, ours_ref[i // 2, 0, 0], across_ref[i // 2, 0, 0]).astype(F32)[8:16]
+        row = jnp.where(
+            core == i % 2, ours_ref[i // 2, 0, 0, :, :half], across_ref[i // 2, 0, 0, :, :half]
+        ).astype(F32)[8:16]
         totals = totals + jnp.where(i < even, row, 0.0)
         counts = counts + jnp.where(i == partner, row, 0.0)
     totals = jnp.where(line == side - 8, totals, 0.0)
@@ -144,27 +143,18 @@
         dims, lambda j: partner_count[j], partner_slot, lambda j, r: box(j, r, (1 - core) * own_ref[j])
     )
 
-    def masked(slope, last, width):
-        columns = lax.broadcasted_iota(jnp.int32, (side, XP, width), 1).reshape(area, width)
-        return jnp.where(columns < last, slope, 0.0).astype(BF16)
-
+    columns = lax.broadcasted_iota(jnp.int32, (side, XP, half), 1).reshape(area, half)
     for s in range(2 * slots):
-        table, number, count = (slot, s, used) if s < slots else (partner_slot, s - slots, partner_used)
-        chip = table[0, number] // 2
-        index = table[1, number]
-        same = lax.rem(table[0, number], 2) == core
+        table, number, count, ref = (
+            (slot, s, used, slope_ref) if s < slots else (partner_slot, s - slots, partner_used, lent_ref)
+        )
+        head = table[0, number]
+        where = (head // 2, table[1, number], slice(None), slice(None), lanes)
+        upstream = jnp.where(lax.rem(head, 2) == core, ours_ref[where], across_ref[where]).astype(F32)
         last = jnp.where(number < count, side, 0)
-        rows = pl.ds(number * area, area)
-        if s < slots:
-            upstream = jnp.where(same, ours_ref[chip, index], across_ref[chip, index]).astype(F32)
-            slope = masked(upstream.reshape(area, channels) * gelu_ref[rows, :], last, channels)
-            slope_ref[rows, :] = slope
-            slope = jnp.where(core == 0, slope[:, :half], slope[:, half:])
-        else:
-            upstream = jnp.where(
-                same, ours_ref[chip, index, :, :, lanes], across_ref[chip, index, :, :, lanes]
-            ).astype(F32)
-            slope = masked(upstream.reshape(area, half) * gelu_other_ref[rows, :], last, half)
+        slope = upstream.reshape(area, half) * gelu_ref[pl.ds(s * area, area), :]
+        slope = jnp.where(columns < last, slope, 0.0).astype(BF16)
+        ref[pl.ds(number * area, area), :] = slope
         for a in range(3):
             if a > 0:
                 slid[a, pl.ds(s * padded, a * XP), :] = jnp.zeros((a * XP, half), BF16)
@@ -175,17 +165,23 @@
                 )
 
     rhs = jnp.concatenate([slid[a] for a in range(3)], axis=1)
+    copies = []
     for b in range(3):
         terms = lax.dot_general(
             shifted[b], rhs, (((0,), (0,)), ((), ())), preferred_element_type=F32
         )
         for a in range(3):
-            terms_ref[pl.ds((3 * a + b) * channels, channels), :] = (
-                terms[:, a * half : (a + 1) * half].astype(BF16)
-            )
-
-
-def backward_kernel(dims, own_ref, row_ref, col_ref, slope_ref, weight_ref, main_ref, spill_ref, canvas, shifted,
+            tap = 3 * a + b
+            rows = pl.ds(tap * channels, channels)
+            staged[rows, :] = terms[:, a * half : (a + 1) * half].astype(BF16)
+            copy = pltpu.make_async_copy(staged.at[rows], terms_ref.at[rows], sems.at[tap])
+            copy.start()
+            copies.append(copy)
+    for copy in copies:
+        copy.wait()
+
+
+def backward_kernel(dims, me_ref, own_ref, row_ref, col_ref, slope_ref, back_ref, weight_ref, main_ref, spill_ref, canvas, shifted,
                     slot):
     side, slots, _, _ = dims
     high = main_ref.shape[0]
@@ -195,12 +191,17 @@
     area = side * XP
 
     used = list_slots(dims, lambda j: own_ref[j], slot, lambda j, r: (row_ref[j, r], col_ref[j, r]))
+    core = lax.rem(me_ref[0], 2)
     canvas[...] = jnp.zeros(canvas.shape, F32)
     none = jnp.zeros((XP, channels), BF16)
     rhs = jnp.concatenate([weight_ref[k] for k in range(9)], axis=1)
     columns = lax.broadcasted_iota(jnp.int32, (side, XP, channels), 1)
     for s in range(slots):
-        slope = slope_ref[pl.ds(s * area, area), :].astype(F32)
+        ours = slope_ref[pl.ds(s * area, area), :].astype(F32)
+        theirs = back_ref[pl.ds(s * area, area), :].astype(F32)
+        slope = jnp.concatenate(
+            [jnp.where(core == 0, ours, theirs), jnp.where(core == 0, theirs, ours)], axis=1
+        )
         for b in range(3):
             moved = slope if b == 1 else pltpu.roll(slope, (area + b - 1) % area, 0)
             shifted[b, pl.ds(0, XP), :] = none
@@ -238,12 +239,12 @@
     return pl.BlockSpec(memory_space=pltpu.VMEM)
 
 
-def kernel(body, dims, out_shape, in_specs, scratch_shapes):
+def kernel(body, dims, out_shape, in_specs, scratch_shapes, out_specs=None):
     return pl.pallas_call(
         lambda *refs: body(dims, *refs),
         out_shape=out_shape,
         in_specs=in_specs,
-        out_specs=jax.tree.map(lambda _: vmem(), out_shape),
+        out_specs=out_specs or jax.tree.map(lambda _: vmem(), out_shape),
         scratch_shapes=scratch_shapes,
         compiler_params=pltpu.CompilerParams(vmem_limit_bytes=VMEM_BYTES),
     )
@@ -280,11 +281,10 @@
     half = channels // 2
     core = lax.rem(me, 2)
 
-    below = shift(tile_map, "tile", -1)
+    below = shift(tile_map[:halo], "tile", -1)
     spare = jnp.pad(own.astype(BF16), (0, channels - heads))
     spare = jnp.broadcast_to(spare, (boxes, side, XP - side, channels))
-    up = jnp.concatenate([mask_grad[0, 0], spare], 2)
-    sent = repeated(up, chips)
+    sent = repeated(jnp.concatenate([mask_grad[0, 0], spare], 2), chips)
     ups = lax.all_to_all(sent, "dp", 0, 0, axis_index_groups=same_core, tiled=True)
     partner_ups = lax.ppermute(ups, "dp", partner)
 
@@ -300,54 +300,52 @@
     )(own, top_rows, left_cols, tile_map, below)
     partner_crops = lax.ppermute(crops, "dp", partner)
 
-    gelu, gelu_other, shifted = kernel(
+    gelu, shifted = kernel(
         forward_kernel,
         dims,
         (
-            pltpu.VMEM((slots * area, channels), F32),
-            pltpu.VMEM((slots * area, half), F32),
+            pltpu.VMEM((2 * slots * area, half), F32),
             pltpu.VMEM((3, 2 * slots * padded, channels), BF16),
         ),
         [smem()] + [vmem()] * 3,
         [],
     )(me_array, crops, partner_crops, weight)
 
-    terms, slope = kernel(
+    strip = jax.ShapeDtypeStruct((slots * area, half), BF16)
+    terms, slope, lent = kernel(
         slope_kernel,
         dims,
-        (
-            jax.ShapeDtypeStruct((9 * channels, half), BF16),
-            jax.ShapeDtypeStruct((slots * area, channels), BF16),
-        ),
-        [smem()] * 2 + [vmem()] * 5,
+        (jax.ShapeDtypeStruct((9 * channels, half), BF16), strip, strip),
+        [smem()] * 2 + [vmem()] * 4,
         [
             pltpu.VMEM((3, 2 * slots * padded, half), BF16),
             pltpu.SMEM((heads,), jnp.int32),
             pltpu.SMEM((heads,), jnp.int32),
             pltpu.SMEM((2, slots), jnp.int32),
             pltpu.SMEM((2, slots), jnp.int32),
+            pltpu.VMEM((9 * channels, half), BF16),
+            pltpu.SemaphoreType.DMA((9,)),
         ],
-    )(me_array, own, ups, partner_ups, gelu, gelu_other, shifted)
-
-    main, spill = pl.pallas_call(
-        lambda *refs: backward_kernel(dims, *refs),
-        out_shape=(
+        out_specs=(pl.BlockSpec(memory_space=pltpu.HBM), vmem(), vmem()),
+    )(me_array, own, ups, partner_ups, gelu, shifted)
+    returned = lax.ppermute(lent, "dp", partner)
+
+    main, spill = kernel(
+        backward_kernel,
+        dims,
+        (
             jax.ShapeDtypeStruct((high, width, channels), F32),
             jax.ShapeDtypeStruct((halo, width, channels), BF16),
         ),
-        in_specs=[smem()] * 3 + [vmem()] * 2,
-        out_specs=(vmem(), vmem()),
-        scratch_shapes=[
+        [smem()] * 4 + [vmem()] * 3,
+        [
             pltpu.VMEM((high + halo, width + XP, channels), F32),
             pltpu.VMEM((3, padded, channels), BF16),
             pltpu.SMEM((2, slots), jnp.int32),
         ],
-        name="backward",
-        compiler_params=pltpu.CompilerParams(vmem_limit_bytes=VMEM_BYTES),
-    )(own, top_rows, left_cols, slope, weight)
+    )(me_array, own, top_rows, left_cols, slope, returned, weight)
     arriving = shift(spill, "tile", 1)
-    arriving = arriving.astype(F32)
-    map_grad = jnp.concatenate([main[:halo] + arriving, main[halo:]], 0)
+    map_grad = jnp.concatenate([main[:halo] + arriving.astype(F32), main[halo:]], 0)
 
     part = 9 * channels
     deep = 16 if tiles % 16 == 0 else 1
@@ -362,14 +360,16 @@
     got = lax.all_to_all(
         terms.reshape(near, part // near, half), ("tile", "dp"), 0, 0, axis_index_groups=plane, tiled=True
     )
-    column = got.astype(F32).sum(0)
+    column = (got.astype(F32).sum(0) / boxes).astype(BF16)
     got = lax.all_to_all(
         column.reshape(deep, part // near // deep, half), "tile", 0, 0, axis_index_groups=stick, tiled=True
     )
-    chunk = (got.sum(0) / (boxes * tiles * owners)).astype(BF16)
+    chunk = (got.astype(F32).sum(0) / (tiles * owners)).astype(BF16)
     got = lax.all_to_all(repeated(chunk, deep), "tile", 0, 0, axis_index_groups=stick, tiled=True)
     got = got.reshape(part // near, half)
-    got = lax.all_to_all(repeated(got, near), ("tile", "dp"), 0, 0, axis_index_groups=plane, tiled=True)
+    got = lax.all_to_all(
+        repeated(got, near), ("tile", "dp"), 0, 0, axis_index_groups=plane, tiled=True
+    )
     got = got.reshape(part, half)
     other = lax.ppermute(got, "dp", partner)
     weight_grad = pl.pallas_call(

time: 127 us -> 141 us (1.11)
  the two profiles are of different devices: /device:TPU:6 before, /device:TPU:2 now
where the time goes in v5:
time: 141 us; the launch traced here: 140 us
  blocking collectives  70.9 us (50%)
  starting transfers between devices  26.7 us (19%)
  waiting for transfers between devices  23.8 us (17%)
  Pallas kernels  13.3 us (9%)
  other arithmetic  3.23 us (2%)
    all_to_all x1, blocking collectives, on_device(): lax.all_to_all(column.reshape(deep, part // near // deep, half), 'tile',...  20.8 us
    ppermute x2, waiting for transfers between devices, shift(): return lax.ppermute(array, axis, pairs)  20.5 us
    all_to_all x1, blocking collectives, on_device(): lax.all_to_all(sent, 'dp', 0, 0, axis_index_groups=same_core, tiled=True)  18.1 us
    all_to_all x1, blocking collectives, on_device(): lax.all_to_all(terms.reshape(near, part // near, half), ('tile', 'dp'), 0...  16.4 us
    all_to_all x1, blocking collectives, on_device(): lax.all_to_all(repeated(chunk, deep), 'tile', 0, 0, axis_index_groups=sti...  15.5 us
    ppermute x2, starting transfers between devices, shift(): return lax.ppermute(array, axis, pairs)  14.3 us
    pallas_call x1, Pallas kernels, on_device(): kernel(slope_kernel, dims, (jax.ShapeDtypeStruct((9 * channels, half), BF...  4.93 us
    all_to_all x1, starting transfers between devices, on_device(): lax.all_to_all(repeated(got, near), ('tile', 'dp'), 0, 0, axis_index_grou...  4.81 us
  transfers between devices with their start and end apart: 7, of which 4 were waited for; matrix products, arithmetic and copies ran while one was open for 1% of the time, Pallas kernels for 5%

profile of v5, /device:TPU:2, one launch (start us, length us, event | category | flops | bytes accessed | tf_op | source)
XLA Modules:
  0.0 140.1 jit_solution(12110712700824806579)
XLA Ops:
  0.6 0.0 copy-start.1
  0.6 0.7 bitcast_convert_fusion
  1.4 0.0 copy-start.3
  1.4 0.0 copy-start.4
  1.4 0.0 copy-start.2
  1.4 1.2 pad_maximum_fusion
  2.7 0.0 copy-start
  2.7 0.1 broadcast_in_dim.26
  2.8 18.1 %all_to_all.25.refs_2_ = bf16[4,2,14,16,256]{4,3,2,1,0:T(8,128)(2,1)S(1)} all-to-all(bf16[4,2,14,16,256]{4,3,2,1,0:T(8,128)(2,1)S(1)} %broadcast_in_dim.26), channel_id=1, replica_groups={{0,2,4,6},{1,3,5,7},{8,10,12,14},{9,11,13,15},{16,18,20,22},{17,19,21,2..., dimensions={0} | all-to-all | bytes 1835008 | tf_op jit(solution)/shard_map/all_to_all | solution.py:288
  20.9 1.9 %collective-permute-start = (bf16[4,2,14,16,256]{4,3,2,1,0:T(8,128)(2,1)S(1)}, bf16[4,2,14,16,256]{4,3,2,1,0:T(8,128)(2,1)}, u32[]{:S(2)}, u32[]{:S(2)}) collective-permute-start(bf16[4,2,14,16,256]{4,3,2,1,0:T(8,128)(2,1)S(1)} %all_to_all.25.refs_2_), channel_id=1, source_target_pairs={{0,1},{1,0},{2,3},{3,2},{4,5},{5,4},{6,7},{7,6},{8,9},{9,8},{10,11... | collective-permute-start | bytes 2752520 | tf_op jit(solution)/shard_map/ppermute | solution.py:289
  22.8 0.0 copy-done.1
  22.8 11.4 %collective-permute-start.1 = (bf16[13,64,256]{2,1,0:T(8,128)(2,1)S(1)}, bf16[13,64,256]{2,1,0:T(8,128)(2,1)S(1)}, u32[]{:S(2)}, u32[]{:S(2)}) collective-permute-start(bf16[13,64,256]{2,1,0:T(8,128)(2,1)S(1)} %slice_bitcast_fusion), channel_id=1, source_target_pairs={{8,0},{16,8},{24,16},{32,24},{40,32},{48,40},{56,48},{64,56},{72,6... | collective-permute-start | bytes 1277960 | tf_op jit(solution)/shard_map/ppermute | solution.py:256
  34.2 0.0 copy-done.3
  34.2 0.1 copy.16.refs_1_.refs_2_
  34.3 0.0 copy-done.4
  34.3 0.1 copy.17.refs_2_.refs_3_
  34.4 9.5 %collective-permute-done.1.refs_4_ = bf16[13,64,256]{2,1,0:T(8,128)(2,1)S(1)} collective-permute-done((bf16[13,64,256]{2,1,0:T(8,128)(2,1)S(1)}, bf16[13,64,256]{2,1,0:T(8,128)(2,1)S(1)}, u32[]{:S(2)}, u32[]{:S(2)}) %collective-permute-start.1) | collective-permute-done | bytes 426016 | tf_op jit(solution)/shard_map/ppermute | solution.py:256
  43.9 0.0 copy-done.2
  44.0 1.2 shard_map.77.refs_1_
  45.2 1.9 %collective-permute-start.2 = (bf16[896,256]{1,0:T(8,128)(2,1)S(1)}, bf16[896,256]{1,0:T(8,128)(2,1)S(1)}, u32[]{:S(2)}, u32[]{:S(2)}) collective-permute-start(bf16[896,256]{1,0:T(8,128)(2,1)S(1)} %shard_map.77.refs_1_), channel_id=1, source_target_pairs={{0,1},{1,0},{2,3},{3,2},{4,5},{5,4},{6,7},{7,6},{8,9},{9,8},{10,11... | collective-permute-start | bytes 1376264 | tf_op jit(solution)/shard_map/ppermute | solution.py:301
  47.1 1.8 %collective-permute-done.2.refs_2_ = bf16[896,256]{1,0:T(8,128)(2,1)S(1)} collective-permute-done((bf16[896,256]{1,0:T(8,128)(2,1)S(1)}, bf16[896,256]{1,0:T(8,128)(2,1)S(1)}, u32[]{:S(2)}, u32[]{:S(2)}) %collective-permute-start.2) | collective-permute-done | bytes 458784 | tf_op jit(solution)/shard_map/ppermute | solution.py:301
  48.9 0.0 copy-done
  48.9 2.7 %shard_map.78 = (f32[1792,128]{1,0:T(8,128)S(1)}, bf16[3,2048,256]{2,1,0:T(8,128)(2,1)S(1)}) custom-call(s32[1]{0:T(128)} %bitcast.refs_0_, bf16[896,256]{1,0:T(8,128)(2,1)S(1)} %shard_map.77.refs_1_, bf16[896,256]{1,0:T(8,128)(2,1)S(1)} %collective-permute-done.2.refs_2_, bf16[9,256,256]{2,1,0:T(8,128)(2,1)S(1)} %copy-done), custom_call_target="tpu_custom_call" | custom-call | tf_op jit(solution)/shard_map/pallas_call | solution.py:303
  51.6 0.0 collective-permute-done.refs_3_
  51.6 4.9 %shard_map.79 = (bf16[2304,128]{1,0:T(8,128)(2,1)S(1)}, bf16[896,128]{1,0:T(8,128)(2,1)S(1)}, bf16[896,128]{1,0:T(8,128)(2,1)S(1)}) custom-call(s32[1]{0:T(128)} %bitcast.refs_0_, s32[8]{0:T(128)S(1)} %bitcast.20, bf16[4,2,14,16,256]{4,3,2,1,0:T(8,128)(2,1)S(1)} %all_to_all.25.refs_2_, bf16[4,2,14,16,256]{4,3,2,1,0:T(8,128)(2,1)} %collective-permute-done.refs_3_, ...), custom_call_target="tpu_custom_call" | custom-call | tf_op jit(solution)/shard_map/pallas_call | solution.py:315
  56.5 16.4 %all_to_all.26 = bf16[16,144,128]{2,1,0:T(8,128)(2,1)S(1)} all-to-all(bf16[16,144,128]{2,1,0:T(8,128)(2,1)S(1)} %bitcast.18), channel_id=1, replica_groups={{0,2,4,6,128,130,132,134,256,258,260,262,384,386,388,390},{1,3,5,7,129,..., dimensions={0} | all-to-all | bytes 1179648 | tf_op jit(solution)/shard_map/all_to_all | solution.py:360
  72.9 0.1 convert_reduce_fusion
  73.0 20.8 %all_to_all.27 = bf16[16,9,128]{2,1,0:T(8,128)(2,1)S(1)} all-to-all(bf16[16,9,128]{2,1,0:T(8,128)(2,1)S(1)} %convert_element_type.32), channel_id=1, replica_groups={{0,8,16,24,32,40,48,56,64,72,80,88,96,104,112,120},{128,136,144,152,160..., dimensions={0} | all-to-all | bytes 73728 | tf_op jit(solution)/shard_map/all_to_all | solution.py:364
  93.9 15.5 %all_to_all.28 = bf16[16,9,128]{2,1,0:T(8,128)(2,1)S(1)} all-to-all(bf16[16,9,128]{2,1,0:T(8,128)(2,1)S(1)} %broadcast_in_dim.28), channel_id=1, replica_groups={{0,8,16,24,32,40,48,56,64,72,80,88,96,104,112,120},{128,136,144,152,160..., dimensions={0} | all-to-all | bytes 73728 | tf_op jit(solution)/shard_map/all_to_all | solution.py:368
  109.5 0.9 broadcast_in_dim.30
  110.4 4.8 %all-to-all-start.4 = ((bf16[16,144,128]{2,1,0:T(8,128)(2,1)}), bf16[16,144,128]{2,1,0:T(8,128)(2,1)S(1)}, u32[]{:S(2)}, u32[]{:S(2)}) async-start(bf16[16,144,128]{2,1,0:T(8,128)(2,1)} %broadcast_in_dim.30), calls=%async_computation.4 | async-start | bytes 1179648 | tf_op jit(solution)/shard_map/all_to_all | solution.py:370
  115.2 1.9 %collective-permute-start.3 = (bf16[896,128]{1,0:T(8,128)(2,1)S(1)}, bf16[896,128]{1,0:T(8,128)(2,1)S(1)}, u32[]{:S(2)}, u32[]{:S(2)}) collective-permute-start(bf16[896,128]{1,0:T(8,128)(2,1)S(1)} %get-tuple-element.12), channel_id=1, source_target_pairs={{0,1},{1,0},{2,3},{3,2},{4,5},{5,4},{6,7},{7,6},{8,9},{9,8},{10,11... | collective-permute-start | bytes 688136 | tf_op jit(solution)/shard_map/ppermute | solution.py:331
  117.1 1.5 %collective-permute-done.3.refs_5_ = bf16[896,128]{1,0:T(8,128)(2,1)S(1)} collective-permute-done((bf16[896,128]{1,0:T(8,128)(2,1)S(1)}, bf16[896,128]{1,0:T(8,128)(2,1)S(1)}, u32[]{:S(2)}, u32[]{:S(2)}) %collective-permute-start.3) | collective-permute-done | bytes 229408 | tf_op jit(solution)/shard_map/ppermute | solution.py:331
  118.6 2.8 %shard_map.80 = (f32[16,64,256]{2,1,0:T(8,128)S(1)}, bf16[13,64,256]{2,1,0:T(8,128)(2,1)S(1)}) custom-call(s32[1]{0:T(128)} %bitcast.refs_0_, s32[8]{0:T(128)S(1)} %bitcast.21, s32[8,2]{1,0:T(8,128)S(1)} %copy.16.refs_1_.refs_2_, s32[8,2]{1,0:T(8,128)S(1)} %copy.17.refs_2_.refs_3_, bf16[896,128]{1,0:T(8,128)(2,1)S(1)} %get-tuple-element.11.refs_4_, ...), custom_call_target="tpu_custom_call" | custom-call | tf_op jit(solution)/shard_map/pallas_call | solution.py:333
  121.4 2.9 %collective-permute-start.4 = (bf16[13,64,256]{2,1,0:T(8,128)(2,1)S(1)}, bf16[13,64,256]{2,1,0:T(8,128)(2,1)S(1)}, u32[]{:S(2)}, u32[]{:S(2)}) collective-permute-start(bf16[13,64,256]{2,1,0:T(8,128)(2,1)S(1)} %get-tuple-element.14), channel_id=1, source_target_pairs={{0,8},{8,16},{16,24},{24,32},{32,40},{40,48},{48,56},{56,64},{64,7... | collective-permute-start | bytes 1277960 | tf_op jit(solution)/shard_map/ppermute | solution.py:256
  124.3 0.0 all-to-all-done.4
  124.3 1.9 %collective-permute-start.5 = (bf16[2304,128]{1,0:T(8,128)(2,1)S(1)}, bf16[2304,128]{1,0:T(8,128)(2,1)S(1)}, u32[]{:S(2)}, u32[]{:S(2)}) collective-permute-start(bf16[2304,128]{1,0:T(8,128)(2,1)S(1)} %bitcast.15), channel_id=1, source_target_pairs={{0,1},{1,0},{2,3},{3,2},{4,5},{5,4},{6,7},{7,6},{8,9},{9,8},{10,11... | collective-permute-start | bytes 1769480 | tf_op jit(solution)/shard_map/ppermute | solution.py:374
  126.3 11.0 %collective-permute-done.4 = bf16[13,64,256]{2,1,0:T(8,128)(2,1)S(1)} collective-permute-done((bf16[13,64,256]{2,1,0:T(8,128)(2,1)S(1)}, bf16[13,64,256]{2,1,0:T(8,128)(2,1)S(1)}, u32[]{:S(2)}, u32[]{:S(2)}) %collective-permute-start.4) | collective-permute-done | bytes 426016 | tf_op jit(solution)/shard_map/ppermute | solution.py:256
  137.2 0.1 convert_add_fusion
  137.3 1.1 maximum_bitcast_fusion
  138.4 0.0 collective-permute-done.5.other_ref
  138.4 1.7 %finish.1 = f32[2304,256]{1,0:T(8,128)} custom-call(s32[1]{0:T(128)} %bitcast.8.core_ref, bf16[2304,128]{1,0:T(8,128)(2,1)S(1)} %bitcast.16, bf16[2304,128]{1,0:T(8,128)(2,1)S(1)} %collective-permute-done.5.other_ref), custom_call_target="tpu_custom_call" | custom-call | tf_op jit(solution)/shard_map/finish/pallas_call | solution.py:375
  (11 shorter events, 0.2 us)
Async XLA Ops:
  0.6 22.2 %copy-start.1 = (bf16[1,16,64,256]{3,2,1,0:T(8,128)(2,1)S(1)}, bf16[1,16,64,256]{3,2,1,0:T(8,128)(2,1)}, u32[]{:S(2)}) copy-start(bf16[1,16,64,256]{3,2,1,0:T(8,128)(2,1)} %param.6) | copy-start | bytes 1572868
  1.4 32.8 %copy-start.3 = (s32[1,1,8,2]{2,3,1,0:T(2,128)S(1)}, s32[1,1,8,2]{2,3,1,0:T(2,128)}, u32[]{:S(2)}) copy-start(s32[1,1,8,2]{2,3,1,0:T(2,128)} %param.10) | copy-start | bytes 196
  1.4 32.9 %copy-start.4 = (s32[1,1,8,2]{2,3,1,0:T(2,128)S(1)}, s32[1,1,8,2]{2,3,1,0:T(2,128)}, u32[]{:S(2)}) copy-start(s32[1,1,8,2]{2,3,1,0:T(2,128)} %param.11) | copy-start | bytes 196
  1.4 42.5 %copy-start.2 = (s32[1,1,8]{2,1,0:T(1,128)S(1)}, s32[1,1,8]{2,1,0:T(1,128)}, u32[]{:S(2)}) copy-start(s32[1,1,8]{2,1,0:T(1,128)} %param.9) | copy-start | bytes 100
  2.7 46.2 %copy-start = (bf16[9,256,256]{2,1,0:T(8,128)(2,1)S(1)}, bf16[9,256,256]{2,1,0:T(8,128)(2,1)}, u32[]{:S(2)}) copy-start(bf16[9,256,256]{2,1,0:T(8,128)(2,1)} %refs_6_.1) | copy-start | bytes 3538948
  20.9 30.7 %collective-permute-start = (bf16[4,2,14,16,256]{4,3,2,1,0:T(8,128)(2,1)S(1)}, bf16[4,2,14,16,256]{4,3,2,1,0:T(8,128)(2,1)}, u32[]{:S(2)}, u32[]{:S(2)}) collective-permute-start(bf16[4,2,14,16,256]{4,3,2,1,0:T(8,128)(2,1)S(1)} %all_to_all.25.refs_2_), channel_id=1, source_target_pairs={{0,1},{1,0},{2,3},{3,2},{4,5},{5,4},{6,7},{7,6},{8,9},{9,8},{10,11... | collective-permute-start | bytes 2752520 | tf_op jit(solution)/shard_map/ppermute | solution.py:289
  22.8 21.1 %collective-permute-start.1 = (bf16[13,64,256]{2,1,0:T(8,128)(2,1)S(1)}, bf16[13,64,256]{2,1,0:T(8,128)(2,1)S(1)}, u32[]{:S(2)}, u32[]{:S(2)}) collective-permute-start(bf16[13,64,256]{2,1,0:T(8,128)(2,1)S(1)} %slice_bitcast_fusion), channel_id=1, source_target_pairs={{8,0},{16,8},{24,16},{32,24},{40,32},{48,40},{56,48},{64,56},{72,6... | collective-permute-start | bytes 1277960 | tf_op jit(solution)/shard_map/ppermute | solution.py:256
  45.2 3.7 %collective-permute-start.2 = (bf16[896,256]{1,0:T(8,128)(2,1)S(1)}, bf16[896,256]{1,0:T(8,128)(2,1)S(1)}, u32[]{:S(2)}, u32[]{:S(2)}) collective-permute-start(bf16[896,256]{1,0:T(8,128)(2,1)S(1)} %shard_map.77.refs_1_), channel_id=1, source_target_pairs={{0,1},{1,0},{2,3},{3,2},{4,5},{5,4},{6,7},{7,6},{8,9},{9,8},{10,11... | collective-permute-start | bytes 1376264 | tf_op jit(solution)/shard_map/ppermute | solution.py:301
  110.4 13.9 %all-to-all-start.4 = ((bf16[16,144,128]{2,1,0:T(8,128)(2,1)}), bf16[16,144,128]{2,1,0:T(8,128)(2,1)S(1)}, u32[]{:S(2)}, u32[]{:S(2)}) async-start(bf16[16,144,128]{2,1,0:T(8,128)(2,1)} %broadcast_in_dim.30), calls=%async_computation.4 | async-start | bytes 1179648 | tf_op jit(solution)/shard_map/all_to_all | solution.py:370
  115.2 3.4 %collective-permute-start.3 = (bf16[896,128]{1,0:T(8,128)(2,1)S(1)}, bf16[896,128]{1,0:T(8,128)(2,1)S(1)}, u32[]{:S(2)}, u32[]{:S(2)}) collective-permute-start(bf16[896,128]{1,0:T(8,128)(2,1)S(1)} %get-tuple-element.12), channel_id=1, source_target_pairs={{0,1},{1,0},{2,3},{3,2},{4,5},{5,4},{6,7},{7,6},{8,9},{9,8},{10,11... | collective-permute-start | bytes 688136 | tf_op jit(solution)/shard_map/ppermute | solution.py:331
  121.4 15.8 %collective-permute-start.4 = (bf16[13,64,256]{2,1,0:T(8,128)(2,1)S(1)}, bf16[13,64,256]{2,1,0:T(8,128)(2,1)S(1)}, u32[]{:S(2)}, u32[]{:S(2)}) collective-permute-start(bf16[13,64,256]{2,1,0:T(8,128)(2,1)S(1)} %get-tuple-element.14), channel_id=1, source_target_pairs={{0,8},{8,16},{16,24},{24,32},{32,40},{40,48},{48,56},{56,64},{64,7... | collective-permute-start | bytes 1277960 | tf_op jit(solution)/shard_map/ppermute | solution.py:256
  124.3 14.1 %collective-permute-start.5 = (bf16[2304,128]{1,0:T(8,128)(2,1)S(1)}, bf16[2304,128]{1,0:T(8,128)(2,1)S(1)}, u32[]{:S(2)}, u32[]{:S(2)}) collective-permute-start(bf16[2304,128]{1,0:T(8,128)(2,1)S(1)} %bitcast.15), channel_id=1, source_target_pairs={{0,1},{1,0},{2,3},{3,2},{4,5},{5,4},{6,7},{7,6},{8,9},{9,8},{10,11... | collective-permute-start | bytes 1769480 | tf_op jit(solution)/shard_map/ppermute | solution.py:374

commit v6 on v4

--- a/solution.py
+++ b/solution.py
@@ -107,7 +107,7 @@
 
 
 def slope_kernel(dims, me_ref, own_ref, ours_ref, across_ref, gelu_ref, gelu_other_ref, shifted,
-                 terms_ref, slope_ref, slid, prior, partner_count, slot, partner_slot):
+                 terms_ref, slope_ref, slid, prior, partner_count, slot, partner_slot, staged, sems):
     side, slots, heads, _ = dims
     boxes = ours_ref.shape[1]
     channels = gelu_ref.shape[1]
@@ -175,14 +175,20 @@
                 )
 
     rhs = jnp.concatenate([slid[a] for a in range(3)], axis=1)
+    copies = []
     for b in range(3):
         terms = lax.dot_general(
             shifted[b], rhs, (((0,), (0,)), ((), ())), preferred_element_type=F32
         )
         for a in range(3):
-            terms_ref[pl.ds((3 * a + b) * channels, channels), :] = (
-                terms[:, a * half : (a + 1) * half].astype(BF16)
-            )
+            tap = 3 * a + b
+            rows = pl.ds(tap * channels, channels)
+            staged[rows, :] = terms[:, a * half : (a + 1) * half].astype(BF16)
+            copy = pltpu.make_async_copy(staged.at[rows], terms_ref.at[rows], sems.at[tap])
+            copy.start()
+            copies.append(copy)
+    for copy in copies:
+        copy.wait()
 
 
 def backward_kernel(dims, own_ref, row_ref, col_ref, slope_ref, weight_ref, main_ref, spill_ref, canvas, shifted,
@@ -222,12 +228,34 @@
     spill_ref[...] = canvas[pl.ds(high, halo), pl.ds(0, width), :].astype(spill_ref.dtype)
 
 
-def finish_kernel(core_ref, mine_ref, other_ref, out_ref):
-    half = mine_ref.shape[1]
-    core = core_ref[0]
-    for part in range(2):
-        source = jnp.where(core == part, mine_ref[...], other_ref[...])
-        out_ref[:, pl.ds(part * half, half)] = source.astype(F32)
+def merge_kernel(dims, main_ref, arriving_ref, out_ref):
+    halo = arriving_ref.shape[0]
+    out_ref[pl.ds(0, halo)] = main_ref[pl.ds(0, halo)] + arriving_ref[...].astype(F32)
+    out_ref[pl.ds(halo, main_ref.shape[0] - halo)] = main_ref[pl.ds(halo, main_ref.shape[0] - halo)]
+
+
+def write_half(part, source_ref, out_ref, staged, sems):
+    half = source_ref.shape[1]
+    pieces = sems.shape[0]
+    rows = source_ref.shape[0] // pieces
+    lanes = pl.ds(pl.multiple_of(part * half, half), half)
+    copies = []
+    for piece in range(pieces):
+        block = pl.ds(piece * rows, rows)
+        staged[block, :] = source_ref[block, :].astype(F32)
+        copy = pltpu.make_async_copy(staged.at[block], out_ref.at[block, lanes], sems.at[piece])
+        copy.start()
+        copies.append(copy)
+    for copy in copies:
+        copy.wait()
+
+
+def first_kernel(dims, core_ref, mine_ref, out_ref, staged, sems):
+    write_half(core_ref[0], mine_ref, out_ref, staged, sems)
+
+
+def finish_kernel(dims, core_ref, other_ref, begun_ref, out_ref, staged, sems):
+    write_half(1 - core_ref[0], other_ref, out_ref, staged, sems)
 
 
 def smem():
@@ -238,12 +266,13 @@
     return pl.BlockSpec(memory_space=pltpu.VMEM)
 
 
-def kernel(body, dims, out_shape, in_specs, scratch_shapes):
+def kernel(body, dims, out_shape, in_specs, scratch_shapes, out_specs=None, aliases=None):
     return pl.pallas_call(
         lambda *refs: body(dims, *refs),
         out_shape=out_shape,
         in_specs=in_specs,
-        out_specs=jax.tree.map(lambda _: vmem(), out_shape),
+        out_specs=out_specs or jax.tree.map(lambda _: vmem(), out_shape),
+        input_output_aliases=aliases or {},
         scratch_shapes=scratch_shapes,
         compiler_params=pltpu.CompilerParams(vmem_limit_bytes=VMEM_BYTES),
     )
@@ -316,7 +345,7 @@
         slope_kernel,
         dims,
         (
-            jax.ShapeDtypeStruct((9 * channels, half), BF16),
+            pltpu.HBM((9 * channels, half), BF16),
             jax.ShapeDtypeStruct((slots * area, channels), BF16),
         ),
         [smem()] * 2 + [vmem()] * 5,
@@ -326,7 +355,10 @@
             pltpu.SMEM((heads,), jnp.int32),
             pltpu.SMEM((2, slots), jnp.int32),
             pltpu.SMEM((2, slots), jnp.int32),
+            pltpu.VMEM((9 * channels, half), BF16),
+            pltpu.SemaphoreType.DMA((9,)),
         ],
+        out_specs=(pl.BlockSpec(memory_space=pltpu.HBM), vmem()),
     )(me_array, own, ups, partner_ups, gelu, gelu_other, shifted)
 
     main, spill = pl.pallas_call(
@@ -346,8 +378,9 @@
         compiler_params=pltpu.CompilerParams(vmem_limit_bytes=VMEM_BYTES),
     )(own, top_rows, left_cols, slope, weight)
     arriving = shift(spill, "tile", 1)
-    arriving = arriving.astype(F32)
-    map_grad = jnp.concatenate([main[:halo] + arriving, main[halo:]], 0)
+    map_grad = kernel(
+        merge_kernel, dims, jax.ShapeDtypeStruct((high, width, channels), F32), [vmem()] * 2, []
+    )(main, arriving)
 
     part = 9 * channels
     deep = 16 if tiles % 16 == 0 else 1
@@ -372,14 +405,13 @@
     got = lax.all_to_all(repeated(got, near), ("tile", "dp"), 0, 0, axis_index_groups=plane, tiled=True)
     got = got.reshape(part, half)
     other = lax.ppermute(got, "dp", partner)
-    weight_grad = pl.pallas_call(
-        finish_kernel,
-        out_shape=jax.ShapeDtypeStruct((9 * channels, channels), F32),
-        in_specs=[smem(), vmem(), vmem()],
-        out_specs=vmem(),
-        name="finish",
-        compiler_params=pltpu.CompilerParams(vmem_limit_bytes=VMEM_BYTES),
-    )(core.reshape(1), got, other)
+    whole = pltpu.HBM((part, channels), F32)
+    room = [pltpu.VMEM((part, half), F32), pltpu.SemaphoreType.DMA((4,))]
+    hbm = pl.BlockSpec(memory_space=pltpu.HBM)
+    begun = kernel(first_kernel, dims, whole, [smem(), vmem()], room, hbm)(core.reshape(1), got)
+    weight_grad = kernel(
+        finish_kernel, dims, whole, [smem(), vmem(), hbm], room, hbm, {2: 0}
+    )(core.reshape(1), other, begun)
     return map_grad[None], weight_grad.reshape(9, channels, channels)
 
 
@@ -394,6 +426,4 @@
     )
     out_specs = (P("dp", "tile", None, None), P())
 
-    return jax.shard_map(
-        on_device, mesh=mesh, in_specs=in_specs, out_specs=out_specs, check_vma=False
-    )
+    return jax.shard_map(on_device, mesh=mesh, in_specs=in_specs, out_specs=out_specs, check_vma=False)

time: 127 us -> 142 us (1.12)
  the two profiles are of different devices: /device:TPU:6 before, /device:TPU:2 now
where the time goes in v6:
time: 142 us; the launch traced here: 141 us
  blocking collectives  70.7 us (50%)
  waiting for transfers between devices  24.7 us (17%)
  starting transfers between devices  24.3 us (17%)
  Pallas kernels  16.3 us (11%)
  local copies, waits for them, and re-layouts  2.39 us (2%)
  other arithmetic  2.05 us (1%)
    all_to_all x1, blocking collectives, on_device(): lax.all_to_all(column.reshape(deep, part // near // deep, half), 'tile',...  21.9 us
    ppermute x2, waiting for transfers between devices, shift(): return lax.ppermute(array, axis, pairs)  20.5 us
    all_to_all x1, blocking collectives, on_device(): lax.all_to_all(terms.reshape(near, part // near, half), ('tile', 'dp'), 0...  18.7 us
    all_to_all x1, blocking collectives, on_device(): lax.all_to_all(repeated(chunk, deep), 'tile', 0, 0, axis_index_groups=sti...  16 us
    ppermute x2, starting transfers between devices, shift(): return lax.ppermute(array, axis, pairs)  14.1 us
    all_to_all x1, blocking collectives, on_device(): lax.all_to_all(repeated(got, near), ('tile', 'dp'), 0, 0, axis_index_grou...  14 us
    all_to_all x1, starting transfers between devices, on_device(): lax.all_to_all(sent, 'dp', 0, 0, axis_index_groups=same_core, tiled=True)  4.46 us
    pallas_call x1, Pallas kernels, on_device(): kernel(forward_kernel, dims, (pltpu.VMEM((slots * area, channels), F32),...  3.99 us
  transfers between devices with their start and end apart: 6, of which 4 were waited for; matrix products, arithmetic and copies ran while one was open for 0% of the time, Pallas kernels for 8%

profile of v6, /device:TPU:2, one launch (start us, length us, event | category | flops | bytes accessed | tf_op | source)
XLA Modules:
  0.0 141.2 jit_solution(17544605379641294072)
XLA Ops:
  0.6 0.0 copy-start.3
  0.6 0.0 copy-start.4
  0.7 0.0 copy-start.5
  0.7 0.7 bitcast_convert_fusion
  1.4 1.2 pad_maximum_fusion
  2.7 0.0 copy-start
  2.7 1.0 broadcast_in_dim.26
  3.7 4.5 %all-to-all-start = ((bf16[4,2,14,16,256]{4,3,2,1,0:T(8,128)(2,1)}), bf16[4,2,14,16,256]{4,3,2,1,0:T(8,128)(2,1)S(1)}, u32[]{:S(2)}, u32[]{:S(2)}) async-start(bf16[4,2,14,16,256]{4,3,2,1,0:T(8,128)(2,1)} %broadcast_in_dim.26), calls=%async_computation | async-start | bytes 1835008 | tf_op jit(solution)/shard_map/all_to_all | solution.py:317
  8.1 11.4 %collective-permute-start.1 = (bf16[16,64,256]{2,1,0:T(8,128)(2,1)}, bf16[16,64,256]{2,1,0:T(8,128)(2,1)}, u32[]{:S(2)}, u32[]{:S(2)}) collective-permute-start(bf16[16,64,256]{2,1,0:T(8,128)(2,1)} %bitcast.5.refs_3_), channel_id=1, source_target_pairs={{8,0},{16,8},{24,16},{32,24},{40,32},{48,40},{56,48},{64,56},{72,6... | collective-permute-start | bytes 1572872 | tf_op jit(solution)/shard_map/ppermute | solution.py:284
  19.5 2.3 %all-to-all-done.refs_2_ = bf16[4,2,14,16,256]{4,3,2,1,0:T(8,128)(2,1)S(1)} async-done(((bf16[4,2,14,16,256]{4,3,2,1,0:T(8,128)(2,1)}), bf16[4,2,14,16,256]{4,3,2,1,0:T(8,128)(2,1)S(1)}, u32[]{:S(2)}, u32[]{:S(2)}) %all-to-all-start) | async-done | bytes 917536 | tf_op jit(solution)/shard_map/all_to_all | solution.py:317
  21.8 1.9 %collective-permute-start = (bf16[4,2,14,16,256]{4,3,2,1,0:T(8,128)(2,1)S(1)}, bf16[4,2,14,16,256]{4,3,2,1,0:T(8,128)(2,1)S(1)}, u32[]{:S(2)}, u32[]{:S(2)}) collective-permute-start(bf16[4,2,14,16,256]{4,3,2,1,0:T(8,128)(2,1)S(1)} %all-to-all-done.refs_2_), channel_id=1, source_target_pairs={{0,1},{1,0},{2,3},{3,2},{4,5},{5,4},{6,7},{7,6},{8,9},{9,8},{10,11... | collective-permute-start | bytes 2752520 | tf_op jit(solution)/shard_map/ppermute | solution.py:318
  23.8 0.0 copy-done.4
  23.8 0.1 copy.17.refs_1_
  23.8 0.0 copy-done.5
  23.8 0.1 copy.18.refs_2_
  23.9 6.8 %collective-permute-done.1.refs_4_ = bf16[16,64,256]{2,1,0:T(8,128)(2,1)} collective-permute-done((bf16[16,64,256]{2,1,0:T(8,128)(2,1)}, bf16[16,64,256]{2,1,0:T(8,128)(2,1)}, u32[]{:S(2)}, u32[]{:S(2)}) %collective-permute-start.1) | collective-permute-done | bytes 524320 | tf_op jit(solution)/shard_map/ppermute | solution.py:284
  30.7 0.0 copy-done.3
  30.7 1.8 %shard_map.77.refs_1_ = bf16[896,256]{1,0:T(8,128)(2,1)S(1)} custom-call(s32[8]{0:T(128)S(1)} %bitcast.14, s32[8,2]{1,0:T(8,128)S(1)} %copy.17.refs_1_, s32[8,2]{1,0:T(8,128)S(1)} %copy.18.refs_2_, bf16[16,64,256]{2,1,0:T(8,128)(2,1)} %bitcast.5.refs_3_, bf16[16,64,256]{2,1,0:T(8,128)(2,1)} %collective-permute-done.1.refs_4_), custom_call_target="tpu_custom_call" | custom-call | tf_op jit(solution)/shard_map/pallas_call | solution.py:320
  32.5 1.9 %collective-permute-start.2 = (bf16[896,256]{1,0:T(8,128)(2,1)S(1)}, bf16[896,256]{1,0:T(8,128)(2,1)}, u32[]{:S(2)}, u32[]{:S(2)}) collective-permute-start(bf16[896,256]{1,0:T(8,128)(2,1)S(1)} %shard_map.77.refs_1_), channel_id=1, source_target_pairs={{0,1},{1,0},{2,3},{3,2},{4,5},{5,4},{6,7},{7,6},{8,9},{9,8},{10,11... | collective-permute-start | bytes 1376264 | tf_op jit(solution)/shard_map/ppermute | solution.py:330
  34.4 1.9 %collective-permute-done.2.refs_2_ = bf16[896,256]{1,0:T(8,128)(2,1)} collective-permute-done((bf16[896,256]{1,0:T(8,128)(2,1)S(1)}, bf16[896,256]{1,0:T(8,128)(2,1)}, u32[]{:S(2)}, u32[]{:S(2)}) %collective-permute-start.2) | collective-permute-done | bytes 458784 | tf_op jit(solution)/shard_map/ppermute | solution.py:330
  36.3 0.0 copy-done
  36.3 4.0 %shard_map.78 = (f32[896,256]{1,0:T(8,128)S(1)}, f32[896,128]{1,0:T(8,128)S(1)}, bf16[3,2048,256]{2,1,0:T(8,128)(2,1)S(1)}) custom-call(s32[1]{0:T(128)} %bitcast.3.refs_0_, bf16[896,256]{1,0:T(8,128)(2,1)S(1)} %shard_map.77.refs_1_, bf16[896,256]{1,0:T(8,128)(2,1)} %collective-permute-done.2.refs_2_, bf16[9,256,256]{2,1,0:T(8,128)(2,1)S(1)} %copy-done), custom_call_target="tpu_custom_call" | custom-call | tf_op jit(solution)/shard_map/pallas_call | solution.py:332
  40.3 0.0 collective-permute-done.refs_3_
  40.3 3.8 %shard_map.79 = (bf16[2304,128]{1,0:T(8,128)(2,1)}, bf16[896,256]{1,0:T(8,128)(2,1)S(1)}) custom-call(s32[1]{0:T(128)} %bitcast.3.refs_0_, s32[8]{0:T(128)S(1)} %bitcast.15, bf16[4,2,14,16,256]{4,3,2,1,0:T(8,128)(2,1)S(1)} %all-to-all-done.refs_2_, bf16[4,2,14,16,256]{4,3,2,1,0:T(8,128)(2,1)S(1)} %collective-permute-done.refs_3_, ...), custom_call_target="tpu_custom_call" | custom-call | tf_op jit(solution)/shard_map/pallas_call | solution.py:344
  44.1 0.0 copy-start.1
  44.1 18.7 %all_to_all.25 = bf16[16,144,128]{2,1,0:T(8,128)(2,1)S(1)} all-to-all(bf16[16,144,128]{2,1,0:T(8,128)(2,1)} %bitcast.19), channel_id=1, replica_groups={{0,2,4,6,128,130,132,134,256,258,260,262,384,386,388,390},{1,3,5,7,129,..., dimensions={0} | all-to-all | bytes 1179648 | tf_op jit(solution)/shard_map/all_to_all | solution.py:395
  62.8 0.1 convert_reduce_fusion
  62.9 21.9 %all_to_all.26 = f32[16,9,128]{2,1,0:T(8,128)S(1)} all-to-all(f32[16,9,128]{2,1,0:T(8,128)S(1)} %reshape.32), channel_id=1, replica_groups={{0,8,16,24,32,40,48,56,64,72,80,88,96,104,112,120},{128,136,144,152,160..., dimensions={0} | all-to-all | bytes 147456 | tf_op jit(solution)/shard_map/all_to_all | solution.py:399
  84.9 16.0 %all_to_all.27 = bf16[16,9,128]{2,1,0:T(8,128)(2,1)S(1)} all-to-all(bf16[16,9,128]{2,1,0:T(8,128)(2,1)S(1)} %broadcast_in_dim.28), channel_id=1, replica_groups={{0,8,16,24,32,40,48,56,64,72,80,88,96,104,112,120},{128,136,144,152,160..., dimensions={0} | all-to-all | bytes 73728 | tf_op jit(solution)/shard_map/all_to_all | solution.py:403
  100.9 0.1 broadcast_in_dim.30
  101.0 14.0 %all_to_all.28 = bf16[16,144,128]{2,1,0:T(8,128)(2,1)S(1)} all-to-all(bf16[16,144,128]{2,1,0:T(8,128)(2,1)S(1)} %broadcast_in_dim.30), channel_id=1, replica_groups={{0,2,4,6,128,130,132,134,256,258,260,262,384,386,388,390},{1,3,5,7,129,..., dimensions={0} | all-to-all | bytes 1179648 | tf_op jit(solution)/shard_map/all_to_all | solution.py:405
  115.1 1.9 %collective-permute-start.4 = (bf16[2304,128]{1,0:T(8,128)(2,1)S(1)}, bf16[2304,128]{1,0:T(8,128)(2,1)S(1)}, u32[]{:S(2)}, u32[]{:S(2)}) collective-permute-start(bf16[2304,128]{1,0:T(8,128)(2,1)S(1)} %bitcast.12), channel_id=1, source_target_pairs={{0,1},{1,0},{2,3},{3,2},{4,5},{5,4},{6,7},{7,6},{8,9},{9,8},{10,11... | collective-permute-start | bytes 1769480 | tf_op jit(solution)/shard_map/ppermute | solution.py:407
  117.0 0.0 copy-done.1
  117.0 0.0 copy-start.2
  117.0 1.0 copy-done.2
  118.0 3.6 %backward.1 = (f32[16,64,256]{2,1,0:T(8,128)S(1)}, bf16[13,64,256]{2,1,0:T(8,128)(2,1)}) custom-call(s32[8]{0:T(128)S(1)} %bitcast.16, s32[8,2]{1,0:T(8,128)S(1)} %copy.17.refs_1_, s32[8,2]{1,0:T(8,128)S(1)} %copy.18.refs_2_, bf16[896,256]{1,0:T(8,128)(2,1)S(1)} %copy-done.2, bf16[9,256,256]{2,1,0:T(8,128)(2,1)S(1)} %copy-done), custom_call_target="tpu_custom_call" | custom-call | tf_op jit(solution)/shard_map/backward/pallas_call | solution.py:364
  121.6 2.7 %collective-permute-start.3 = (bf16[13,64,256]{2,1,0:T(8,128)(2,1)}, bf16[13,64,256]{2,1,0:T(8,128)(2,1)S(1)}, u32[]{:S(2)}, u32[]{:S(2)}) collective-permute-start(bf16[13,64,256]{2,1,0:T(8,128)(2,1)} %get-tuple-element.14), channel_id=1, source_target_pairs={{0,8},{8,16},{16,24},{24,32},{32,40},{40,48},{48,56},{56,64},{64,7... | collective-permute-start | bytes 1277960 | tf_op jit(solution)/shard_map/ppermute | solution.py:284
  124.3 13.7 %collective-permute-done.3.refs_1_ = bf16[13,64,256]{2,1,0:T(8,128)(2,1)S(1)} collective-permute-done((bf16[13,64,256]{2,1,0:T(8,128)(2,1)}, bf16[13,64,256]{2,1,0:T(8,128)(2,1)S(1)}, u32[]{:S(2)}, u32[]{:S(2)}) %collective-permute-start.3) | collective-permute-done | bytes 426016 | tf_op jit(solution)/shard_map/ppermute | solution.py:284
  138.0 1.1 shard_map.80
  139.1 1.1 shard_map.81.refs_2_
  140.1 0.0 collective-permute-done.4.refs_1_
  140.1 1.1 shard_map.82
  (8 shorter events, 0.1 us)
Async XLA Ops:
  0.6 30.1 %copy-start.3 = (s32[1,1,8]{2,1,0:T(1,128)S(1)}, s32[1,1,8]{2,1,0:T(1,128)}, u32[]{:S(2)}) copy-start(s32[1,1,8]{2,1,0:T(1,128)} %param.9) | copy-start | bytes 100
  0.6 23.1 %copy-start.4 = (s32[1,1,8,2]{2,3,1,0:T(2,128)S(1)}, s32[1,1,8,2]{2,3,1,0:T(2,128)}, u32[]{:S(2)}) copy-start(s32[1,1,8,2]{2,3,1,0:T(2,128)} %param.10) | copy-start | bytes 196
  0.7 23.2 %copy-start.5 = (s32[1,1,8,2]{2,3,1,0:T(2,128)S(1)}, s32[1,1,8,2]{2,3,1,0:T(2,128)}, u32[]{:S(2)}) copy-start(s32[1,1,8,2]{2,3,1,0:T(2,128)} %param.11) | copy-start | bytes 196
  2.7 33.7 %copy-start = (bf16[9,256,256]{2,1,0:T(8,128)(2,1)S(1)}, bf16[9,256,256]{2,1,0:T(8,128)(2,1)}, u32[]{:S(2)}) copy-start(bf16[9,256,256]{2,1,0:T(8,128)(2,1)} %refs_4_.1) | copy-start | bytes 3538948
  3.7 18.2 %all-to-all-start = ((bf16[4,2,14,16,256]{4,3,2,1,0:T(8,128)(2,1)}), bf16[4,2,14,16,256]{4,3,2,1,0:T(8,128)(2,1)S(1)}, u32[]{:S(2)}, u32[]{:S(2)}) async-start(bf16[4,2,14,16,256]{4,3,2,1,0:T(8,128)(2,1)} %broadcast_in_dim.26), calls=%async_computation | async-start | bytes 1835008 | tf_op jit(solution)/shard_map/all_to_all | solution.py:317
  8.1 22.6 %collective-permute-start.1 = (bf16[16,64,256]{2,1,0:T(8,128)(2,1)}, bf16[16,64,256]{2,1,0:T(8,128)(2,1)}, u32[]{:S(2)}, u32[]{:S(2)}) collective-permute-start(bf16[16,64,256]{2,1,0:T(8,128)(2,1)} %bitcast.5.refs_3_), channel_id=1, source_target_pairs={{8,0},{16,8},{24,16},{32,24},{40,32},{48,40},{56,48},{64,56},{72,6... | collective-permute-start | bytes 1572872 | tf_op jit(solution)/shard_map/ppermute | solution.py:284
  21.8 18.5 %collective-permute-start = (bf16[4,2,14,16,256]{4,3,2,1,0:T(8,128)(2,1)S(1)}, bf16[4,2,14,16,256]{4,3,2,1,0:T(8,128)(2,1)S(1)}, u32[]{:S(2)}, u32[]{:S(2)}) collective-permute-start(bf16[4,2,14,16,256]{4,3,2,1,0:T(8,128)(2,1)S(1)} %all-to-all-done.refs_2_), channel_id=1, source_target_pairs={{0,1},{1,0},{2,3},{3,2},{4,5},{5,4},{6,7},{7,6},{8,9},{9,8},{10,11... | collective-permute-start | bytes 2752520 | tf_op jit(solution)/shard_map/ppermute | solution.py:318
  32.5 3.8 %collective-permute-start.2 = (bf16[896,256]{1,0:T(8,128)(2,1)S(1)}, bf16[896,256]{1,0:T(8,128)(2,1)}, u32[]{:S(2)}, u32[]{:S(2)}) collective-permute-start(bf16[896,256]{1,0:T(8,128)(2,1)S(1)} %shard_map.77.refs_1_), channel_id=1, source_target_pairs={{0,1},{1,0},{2,3},{3,2},{4,5},{5,4},{6,7},{7,6},{8,9},{9,8},{10,11... | collective-permute-start | bytes 1376264 | tf_op jit(solution)/shard_map/ppermute | solution.py:330
  44.1 72.9 %copy-start.1 = (bf16[896,256]{1,0:T(8,128)(2,1)}, bf16[896,256]{1,0:T(8,128)(2,1)S(1)}, u32[]{:S(2)}) copy-start(bf16[896,256]{1,0:T(8,128)(2,1)S(1)} %get-tuple-element.12.refs_3_) | copy-start | bytes 1376260
  115.1 25.1 %collective-permute-start.4 = (bf16[2304,128]{1,0:T(8,128)(2,1)S(1)}, bf16[2304,128]{1,0:T(8,128)(2,1)S(1)}, u32[]{:S(2)}, u32[]{:S(2)}) collective-permute-start(bf16[2304,128]{1,0:T(8,128)(2,1)S(1)} %bitcast.12), channel_id=1, source_target_pairs={{0,1},{1,0},{2,3},{3,2},{4,5},{5,4},{6,7},{7,6},{8,9},{9,8},{10,11... | collective-permute-start | bytes 1769480 | tf_op jit(solution)/shard_map/ppermute | solution.py:407
  117.0 1.0 copy-start.2
  121.6 16.4 %collective-permute-start.3 = (bf16[13,64,256]{2,1,0:T(8,128)(2,1)}, bf16[13,64,256]{2,1,0:T(8,128)(2,1)S(1)}, u32[]{:S(2)}, u32[]{:S(2)}) collective-permute-start(bf16[13,64,256]{2,1,0:T(8,128)(2,1)} %get-tuple-element.14), channel_id=1, source_target_pairs={{0,8},{8,16},{16,24},{24,32},{32,40},{40,48},{48,56},{56,64},{64,7... | collective-permute-start | bytes 1277960 | tf_op jit(solution)/shard_map/ppermute | solution.py:284

commit v7 on v5

--- a/solution.py
+++ b/solution.py
@@ -103,10 +103,10 @@
         )
 
 
-def slope_kernel(dims, me_ref, own_ref, ours_ref, across_ref, gelu_ref, shifted,
-                 terms_ref, slope_ref, lent_ref, slid, prior, partner_count, slot, partner_slot, staged, sems):
+def slope_kernel(dims, me_ref, own_ref, up_ref, gelu_ref, shifted,
+                 terms_ref, slope_ref, lent_ref, slid, prior, partner_count, slot, partner_slot, staged, kept, sems):
     side, slots, heads, _ = dims
-    boxes = ours_ref.shape[1]
+    boxes = up_ref.shape[1]
     half = gelu_ref.shape[1]
     channels = 2 * half
     area = side * XP
@@ -115,16 +115,13 @@
     core = lax.rem(me, 2)
     even = me - core
     partner = even + 1 - core
-    lanes = pl.ds(pl.multiple_of(core * half, half), half)
 
     lane = lax.broadcasted_iota(jnp.int32, (8, half), 1)
     line = lax.broadcasted_iota(jnp.int32, (8, half), 0)
     totals = jnp.zeros((8, half), F32)
     counts = jnp.zeros((8, half), F32)
     for i in range(heads):
-        row = jnp.where(
-            core == i % 2, ours_ref[i // 2, 0, 0, :, :half], across_ref[i // 2, 0, 0, :, :half]
-        ).astype(F32)[8:16]
+        row = up_ref[i, 0, 0].astype(F32)[8:16]
         totals = totals + jnp.where(i < even, row, 0.0)
         counts = counts + jnp.where(i == partner, row, 0.0)
     totals = jnp.where(line == side - 8, totals, 0.0)
@@ -146,11 +143,10 @@
     columns = lax.broadcasted_iota(jnp.int32, (side, XP, half), 1).reshape(area, half)
     for s in range(2 * slots):
         table, number, count, ref = (
-            (slot, s, used, slope_ref) if s < slots else (partner_slot, s - slots, partner_used, lent_ref)
+            (slot, s, used, slope_ref) if s < slots else (partner_slot, s - slots, partner_used, kept)
         )
         head = table[0, number]
-        where = (head // 2, table[1, number], slice(None), slice(None), lanes)
-        upstream = jnp.where(lax.rem(head, 2) == core, ours_ref[where], across_ref[where]).astype(F32)
+        upstream = up_ref[head, table[1, number]].astype(F32)
         last = jnp.where(number < count, side, 0)
         slope = upstream.reshape(area, half) * gelu_ref[pl.ds(s * area, area), :]
         slope = jnp.where(columns < last, slope, 0.0).astype(BF16)
@@ -165,7 +161,8 @@
                 )
 
     rhs = jnp.concatenate([slid[a] for a in range(3)], axis=1)
-    copies = []
+    copies = [pltpu.make_async_copy(kept, lent_ref, sems.at[9])]
+    copies[0].start()
     for b in range(3):
         terms = lax.dot_general(
             shifted[b], rhs, (((0,), (0,)), ((), ())), preferred_element_type=F32
@@ -223,12 +220,34 @@
     spill_ref[...] = canvas[pl.ds(high, halo), pl.ds(0, width), :].astype(spill_ref.dtype)
 
 
-def finish_kernel(core_ref, mine_ref, other_ref, out_ref):
-    half = mine_ref.shape[1]
-    core = core_ref[0]
-    for part in range(2):
-        source = jnp.where(core == part, mine_ref[...], other_ref[...])
-        out_ref[:, pl.ds(part * half, half)] = source.astype(F32)
+def merge_kernel(dims, main_ref, arriving_ref, out_ref):
+    halo = arriving_ref.shape[0]
+    out_ref[pl.ds(0, halo)] = main_ref[pl.ds(0, halo)] + arriving_ref[...].astype(F32)
+    out_ref[pl.ds(halo, main_ref.shape[0] - halo)] = main_ref[pl.ds(halo, main_ref.shape[0] - halo)]
+
+
+def write_half(part, source_ref, out_ref, staged, sems):
+    half = source_ref.shape[1]
+    pieces = sems.shape[0]
+    rows = source_ref.shape[0] // pieces
+    lanes = pl.ds(pl.multiple_of(part * half, half), half)
+    copies = []
+    for piece in range(pieces):
+        block = pl.ds(piece * rows, rows)
+        staged[block, :] = source_ref[block, :].astype(F32)
+        copy = pltpu.make_async_copy(staged.at[block], out_ref.at[block, lanes], sems.at[piece])
+        copy.start()
+        copies.append(copy)
+    for copy in copies:
+        copy.wait()
+
+
+def first_kernel(dims, core_ref, mine_ref, out_ref, staged, sems):
+    write_half(core_ref[0], mine_ref, out_ref, staged, sems)
+
+
+def finish_kernel(dims, core_ref, other_ref, begun_ref, out_ref, staged, sems):
+    write_half(1 - core_ref[0], other_ref, out_ref, staged, sems)
 
 
 def smem():
@@ -239,12 +258,13 @@
     return pl.BlockSpec(memory_space=pltpu.VMEM)
 
 
-def kernel(body, dims, out_shape, in_specs, scratch_shapes, out_specs=None):
+def kernel(body, dims, out_shape, in_specs, scratch_shapes, out_specs=None, aliases=None):
     return pl.pallas_call(
         lambda *refs: body(dims, *refs),
         out_shape=out_shape,
         in_specs=in_specs,
         out_specs=out_specs or jax.tree.map(lambda _: vmem(), out_shape),
+        input_output_aliases=aliases or {},
         scratch_shapes=scratch_shapes,
         compiler_params=pltpu.CompilerParams(vmem_limit_bytes=VMEM_BYTES),
     )
@@ -276,17 +296,17 @@
     own, top_rows, left_cols = send_count[0, 0], send_row[0, 0], send_col[0, 0]
     partner = [(i, i ^ 1) for i in range(owners)]
     chips = owners // 2
-    same_core = [[2 * i + c for i in range(chips)] for c in range(2)]
 
     half = channels // 2
     core = lax.rem(me, 2)
 
-    below = shift(tile_map[:halo], "tile", -1)
-    spare = jnp.pad(own.astype(BF16), (0, channels - heads))
-    spare = jnp.broadcast_to(spare, (boxes, side, XP - side, channels))
-    sent = repeated(jnp.concatenate([mask_grad[0, 0], spare], 2), chips)
-    ups = lax.all_to_all(sent, "dp", 0, 0, axis_index_groups=same_core, tiled=True)
-    partner_ups = lax.ppermute(ups, "dp", partner)
+    below = shift(tile_map, "tile", -1)
+    spare = jnp.pad(own.astype(BF16), (0, half - heads))
+    spare = jnp.broadcast_to(spare, (2, boxes, side, XP - side, half))
+    halves = mask_grad[0, 0].reshape(boxes, side, side, 2, half).transpose(3, 0, 1, 2, 4)
+    sent = repeated(jnp.concatenate([halves, spare], 3), chips)
+    sent = sent.reshape((owners,) + sent.shape[2:])
+    ups = lax.all_to_all(sent, "dp", 0, 0, tiled=True)
 
     crops = kernel(
         crop_kernel,
@@ -315,8 +335,8 @@
     terms, slope, lent = kernel(
         slope_kernel,
         dims,
-        (jax.ShapeDtypeStruct((9 * channels, half), BF16), strip, strip),
-        [smem()] * 2 + [vmem()] * 4,
+        (pltpu.HBM((9 * channels, half), BF16), strip, pltpu.HBM(strip.shape, BF16)),
+        [smem()] * 2 + [vmem()] * 3,
         [
             pltpu.VMEM((3, 2 * slots * padded, half), BF16),
             pltpu.SMEM((heads,), jnp.int32),
@@ -324,10 +344,11 @@
             pltpu.SMEM((2, slots), jnp.int32),
             pltpu.SMEM((2, slots), jnp.int32),
             pltpu.VMEM((9 * channels, half), BF16),
-            pltpu.SemaphoreType.DMA((9,)),
+            pltpu.VMEM((slots * area, half), BF16),
+            pltpu.SemaphoreType.DMA((10,)),
         ],
-        out_specs=(pl.BlockSpec(memory_space=pltpu.HBM), vmem(), vmem()),
-    )(me_array, own, ups, partner_ups, gelu, shifted)
+        (pl.BlockSpec(memory_space=pltpu.HBM), vmem(), pl.BlockSpec(memory_space=pltpu.HBM)),
+    )(me_array, own, ups, gelu, shifted)
     returned = lax.ppermute(lent, "dp", partner)
 
     main, spill = kernel(
@@ -345,7 +366,9 @@
         ],
     )(me_array, own, top_rows, left_cols, slope, returned, weight)
     arriving = shift(spill, "tile", 1)
-    map_grad = jnp.concatenate([main[:halo] + arriving.astype(F32), main[halo:]], 0)
+    map_grad = kernel(
+        merge_kernel, dims, jax.ShapeDtypeStruct((high, width, channels), F32), [vmem()] * 2, []
+    )(main, arriving)
 
     part = 9 * channels
     deep = 16 if tiles % 16 == 0 else 1
@@ -360,26 +383,23 @@
     got = lax.all_to_all(
         terms.reshape(near, part // near, half), ("tile", "dp"), 0, 0, axis_index_groups=plane, tiled=True
     )
-    column = (got.astype(F32).sum(0) / boxes).astype(BF16)
+    column = got.astype(F32).sum(0)
     got = lax.all_to_all(
         column.reshape(deep, part // near // deep, half), "tile", 0, 0, axis_index_groups=stick, tiled=True
     )
-    chunk = (got.astype(F32).sum(0) / (tiles * owners)).astype(BF16)
+    chunk = (got.sum(0) / (boxes * tiles * owners)).astype(BF16)
     got = lax.all_to_all(repeated(chunk, deep), "tile", 0, 0, axis_index_groups=stick, tiled=True)
     got = got.reshape(part // near, half)
-    got = lax.all_to_all(
-        repeated(got, near), ("tile", "dp"), 0, 0, axis_index_groups=plane, tiled=True
-    )
+    got = lax.all_to_all(repeated(got, near), ("tile", "dp"), 0, 0, axis_index_groups=plane, tiled=True)
     got = got.reshape(part, half)
     other = lax.ppermute(got, "dp", partner)
-    weight_grad = pl.pallas_call(
-        finish_kernel,
-        out_shape=jax.ShapeDtypeStruct((9 * channels, channels), F32),
-        in_specs=[smem(), vmem(), vmem()],
-        out_specs=vmem(),
-        name="finish",
-        compiler_params=pltpu.CompilerParams(vmem_limit_bytes=VMEM_BYTES),
-    )(core.reshape(1), got, other)
+    whole = pltpu.HBM((part, channels), F32)
+    room = [pltpu.VMEM((part, half), F32), pltpu.SemaphoreType.DMA((4,))]
+    hbm = pl.BlockSpec(memory_space=pltpu.HBM)
+    begun = kernel(first_kernel, dims, whole, [smem(), vmem()], room, hbm)(core.reshape(1), got)
+    weight_grad = kernel(
+        finish_kernel, dims, whole, [smem(), vmem(), hbm], room, hbm, {2: 0}
+    )(core.reshape(1), other, begun)
     return map_grad[None], weight_grad.reshape(9, channels, channels)
 
 
@@ -394,6 +414,4 @@
     )
     out_specs = (P("dp", "tile", None, None), P())
 
-    return jax.shard_map(
-        on_device, mesh=mesh, in_specs=in_specs, out_specs=out_specs, check_vma=False
-    )
+    return jax.shard_map(on_device, mesh=mesh, in_specs=in_specs, out_specs=out_specs, check_vma=False)

time: 141 us -> 140 us (level)
  the two profiles are of different devices: /device:TPU:2 before, /device:TPU:6 now
where the time goes in v7:
time: 140 us
  blocking collectives  55.8 us (40%)
  starting transfers between devices  30.4 us (22%)
  waiting for transfers between devices  25.6 us (18%)
  Pallas kernels  14.7 us (10%)
  local copies, waits for them, and re-layouts  11.2 us (8%)
    all_to_all x1, blocking collectives, on_device(): lax.all_to_all(column.reshape(deep, part // near // deep, half), 'tile',...  21.9 us
    all_to_all x1, blocking collectives, on_device(): lax.all_to_all(terms.reshape(near, part // near, half), ('tile', 'dp'), 0...  17.8 us
    ppermute x2, waiting for transfers between devices, shift(): return lax.ppermute(array, axis, pairs)  17.4 us
    all_to_all x1, blocking collectives, on_device(): lax.all_to_all(repeated(chunk, deep), 'tile', 0, 0, axis_index_groups=sti...  16.1 us
    ppermute x2, starting transfers between devices, shift(): return lax.ppermute(array, axis, pairs)  14.5 us
    unnamed x28, local copies, waits for them, and re-layouts  7.91 us
    all_to_all x1, waiting for transfers between devices, on_device(): lax.all_to_all(repeated(got, near), ('tile', 'dp'), 0, 0, axis_index_grou...  6.43 us
    all_to_all x1, starting transfers between devices, on_device(): lax.all_to_all(repeated(got, near), ('tile', 'dp'), 0, 0, axis_index_grou...  5.67 us
  transfers between devices with their start and end apart: 7, of which 4 were waited for; matrix products, arithmetic and copies ran while one was open for 2% of the time, Pallas kernels for 7%

profile of v7, /device:TPU:6, one launch (start us, length us, event | category | flops | bytes accessed | tf_op | source)
XLA Modules:
  0.0 139.7 jit_solution(17072085631351148003)
XLA Ops:
  0.6 0.0 copy-start.3
  0.6 0.0 copy-start.10
  0.7 0.0 copy-start.11
  0.7 0.0 copy-start.12
  0.7 11.8 %collective-permute-start = (bf16[16,64,256]{2,1,0:T(8,128)(2,1)}, bf16[16,64,256]{2,1,0:T(8,128)(2,1)}, u32[]{:S(2)}, u32[]{:S(2)}) collective-permute-start(bf16[16,64,256]{2,1,0:T(8,128)(2,1)} %bitcast.17), channel_id=1, source_target_pairs={{8,0},{16,8},{24,16},{32,24},{40,32},{48,40},{56,48},{64,56},{72,6... | collective-permute-start | bytes 1572872 | tf_op jit(solution)/shard_map/ppermute | solution.py:276
  12.5 0.7 bitcast_convert_fusion
  13.1 1.1 reshape_squeeze.3
  14.2 0.3 pad_maximum_fusion
  14.6 0.0 copy-start
  14.6 1.0 broadcast_in_dim.26
  15.6 4.5 %all-to-all-start = ((bf16[8,2,14,16,128]{4,3,2,1,0:T(8,128)(2,1)}), bf16[8,2,14,16,128]{4,3,2,1,0:T(8,128)(2,1)S(1)}, u32[]{:S(2)}, u32[]{:S(2)}) async-start(bf16[8,2,14,16,128]{4,3,2,1,0:T(8,128)(2,1)} %bitcast.23), calls=%async_computation | async-start | bytes 1835008 | tf_op jit(solution)/shard_map/all_to_all | solution.py:309
  20.1 0.0 copy-done.11
  20.1 0.1 copy.17.refs_1_.refs_2_
  20.2 0.1 copy.18.refs_2_.refs_3_
  20.3 3.7 %collective-permute-done.refs_4_ = bf16[16,64,256]{2,1,0:T(8,128)(2,1)} collective-permute-done((bf16[16,64,256]{2,1,0:T(8,128)(2,1)}, bf16[16,64,256]{2,1,0:T(8,128)(2,1)}, u32[]{:S(2)}, u32[]{:S(2)}) %collective-permute-start) | collective-permute-done | bytes 524320 | tf_op jit(solution)/shard_map/ppermute | solution.py:276
  24.0 1.6 %shard_map.77.refs_1_ = bf16[896,256]{1,0:T(8,128)(2,1)S(1)} custom-call(s32[8]{0:T(128)S(1)} %bitcast.19, s32[8,2]{1,0:T(8,128)S(1)} %copy.17.refs_1_.refs_2_, s32[8,2]{1,0:T(8,128)S(1)} %copy.18.refs_2_.refs_3_, bf16[16,64,256]{2,1,0:T(8,128)(2,1)S(1)} %bitcast.18, bf16[16,64,256]{2,1,0:T(8,128)(2,1)} %collective-permute-done.refs_4_), custom_call_target="tpu_custom_call" | custom-call | tf_op jit(solution)/shard_map/pallas_call | solution.py:311
  25.6 1.9 %collective-permute-start.1 = (bf16[896,256]{1,0:T(8,128)(2,1)S(1)}, bf16[896,256]{1,0:T(8,128)(2,1)S(1)}, u32[]{:S(2)}, u32[]{:S(2)}) collective-permute-start(bf16[896,256]{1,0:T(8,128)(2,1)S(1)} %shard_map.77.refs_1_), channel_id=1, source_target_pairs={{0,1},{1,0},{2,3},{3,2},{4,5},{5,4},{6,7},{7,6},{8,9},{9,8},{10,11... | collective-permute-start | bytes 1376264 | tf_op jit(solution)/shard_map/ppermute | solution.py:321
  27.5 1.8 %collective-permute-done.1.refs_2_ = bf16[896,256]{1,0:T(8,128)(2,1)S(1)} collective-permute-done((bf16[896,256]{1,0:T(8,128)(2,1)S(1)}, bf16[896,256]{1,0:T(8,128)(2,1)S(1)}, u32[]{:S(2)}, u32[]{:S(2)}) %collective-permute-start.1) | collective-permute-done | bytes 458784 | tf_op jit(solution)/shard_map/ppermute | solution.py:321
  29.3 0.8 copy-done.4
  30.1 1.0 copy-done.5
  31.1 2.7 %shard_map.78 = (f32[1792,128]{1,0:T(8,128)S(1)}, bf16[3,2048,256]{2,1,0:T(8,128)(2,1)S(1)}) custom-call(s32[1]{0:T(128)} %bitcast.refs_0_, bf16[896,256]{1,0:T(8,128)(2,1)S(1)} %shard_map.77.refs_1_, bf16[896,256]{1,0:T(8,128)(2,1)S(1)} %copy-done.5, bf16[9,256,256]{2,1,0:T(8,128)(2,1)S(1)} %copy-done), custom_call_target="tpu_custom_call" | custom-call | tf_op jit(solution)/shard_map/pallas_call | solution.py:323
  33.7 0.0 copy-start.1
  33.7 1.6 %copy-done.1 = bf16[3,2048,256]{2,1,0:T(8,128)(2,1)} copy-done((bf16[3,2048,256]{2,1,0:T(8,128)(2,1)}, bf16[3,2048,256]{2,1,0:T(8,128)(2,1)S(1)}, u32[]{:S(2)}) %copy-start.1) | copy-done | bytes 3145752
  35.4 0.0 all-to-all-done.refs_2_
  35.4 1.9 %copy-done.2 = bf16[3,2048,256]{2,1,0:T(8,128)(2,1)S(1)} copy-done((bf16[3,2048,256]{2,1,0:T(8,128)(2,1)S(1)}, bf16[3,2048,256]{2,1,0:T(8,128)(2,1)}, u32[]{:S(2)}) %copy-start.2) | copy-done | bytes 3145752
  37.3 3.7 %shard_map.79 = (bf16[2304,128]{1,0:T(8,128)(2,1)}, bf16[896,128]{1,0:T(8,128)(2,1)S(1)}, bf16[896,128]{1,0:T(8,128)(2,1)}) custom-call(s32[1]{0:T(128)} %bitcast.refs_0_, s32[8]{0:T(128)S(1)} %bitcast.20, bf16[8,2,14,16,128]{4,3,2,1,0:T(8,128)(2,1)S(1)} %all-to-all-done.refs_2_, f32[1792,128]{1,0:T(8,128)S(1)} %get-tuple-element.9.refs_3_, ...), custom_call_target="tpu_custom_call" | custom-call | tf_op jit(solution)/shard_map/pallas_call | solution.py:335
  41.0 0.0 copy-start.13
  41.0 17.8 %all_to_all.25 = bf16[16,144,128]{2,1,0:T(8,128)(2,1)S(1)} all-to-all(bf16[16,144,128]{2,1,0:T(8,128)(2,1)} %bitcast.26), channel_id=1, replica_groups={{0,2,4,6,128,130,132,134,256,258,260,262,384,386,388,390},{1,3,5,7,129,..., dimensions={0} | all-to-all | bytes 1179648 | tf_op jit(solution)/shard_map/all_to_all | solution.py:383
  58.8 0.1 convert_reduce_fusion
  58.9 21.9 %all_to_all.26 = f32[16,9,128]{2,1,0:T(8,128)S(1)} all-to-all(f32[16,9,128]{2,1,0:T(8,128)S(1)} %reshape.36), channel_id=1, replica_groups={{0,8,16,24,32,40,48,56,64,72,80,88,96,104,112,120},{128,136,144,152,160..., dimensions={0} | all-to-all | bytes 147456 | tf_op jit(solution)/shard_map/all_to_all | solution.py:387
  80.9 16.1 %all_to_all.27 = bf16[16,9,128]{2,1,0:T(8,128)(2,1)S(1)} all-to-all(bf16[16,9,128]{2,1,0:T(8,128)(2,1)S(1)} %broadcast_in_dim.28), channel_id=1, replica_groups={{0,8,16,24,32,40,48,56,64,72,80,88,96,104,112,120},{128,136,144,152,160..., dimensions={0} | all-to-all | bytes 73728 | tf_op jit(solution)/shard_map/all_to_all | solution.py:391
  97.1 0.9 broadcast_in_dim.30
  98.0 5.7 %all-to-all-start.4 = ((bf16[16,144,128]{2,1,0:T(8,128)(2,1)}), bf16[16,144,128]{2,1,0:T(8,128)(2,1)S(1)}, u32[]{:S(2)}, u32[]{:S(2)}) async-start(bf16[16,144,128]{2,1,0:T(8,128)(2,1)} %broadcast_in_dim.30), calls=%async_computation.4 | async-start | bytes 1179648 | tf_op jit(solution)/shard_map/all_to_all | solution.py:393
  103.6 1.9 %collective-permute-start.2 = (bf16[896,128]{1,0:T(8,128)(2,1)S(1)}, bf16[896,128]{1,0:T(8,128)(2,1)S(1)}, u32[]{:S(2)}, u32[]{:S(2)}) collective-permute-start(bf16[896,128]{1,0:T(8,128)(2,1)S(1)} %copy-done.13), channel_id=1, source_target_pairs={{0,1},{1,0},{2,3},{3,2},{4,5},{5,4},{6,7},{7,6},{8,9},{9,8},{10,11... | collective-permute-start | bytes 688136 | tf_op jit(solution)/shard_map/ppermute | solution.py:352
  105.6 6.4 %all-to-all-done.4 = bf16[16,144,128]{2,1,0:T(8,128)(2,1)S(1)} async-done(((bf16[16,144,128]{2,1,0:T(8,128)(2,1)}), bf16[16,144,128]{2,1,0:T(8,128)(2,1)S(1)}, u32[]{:S(2)}, u32[]{:S(2)}) %all-to-all-start.4) | async-done | bytes 589856 | tf_op jit(solution)/shard_map/all_to_all | solution.py:393
  112.0 1.9 %collective-permute-start.4 = (bf16[2304,128]{1,0:T(8,128)(2,1)S(1)}, bf16[2304,128]{1,0:T(8,128)(2,1)S(1)}, u32[]{:S(2)}, u32[]{:S(2)}) collective-permute-start(bf16[2304,128]{1,0:T(8,128)(2,1)S(1)} %bitcast.15), channel_id=1, source_target_pairs={{0,1},{1,0},{2,3},{3,2},{4,5},{5,4},{6,7},{7,6},{8,9},{9,8},{10,11... | collective-permute-start | bytes 1769480 | tf_op jit(solution)/shard_map/ppermute | solution.py:395
  113.9 0.0 collective-permute-done.2.refs_5_
  113.9 0.0 copy-start.8
  113.9 0.7 copy-done.8
  114.6 0.9 copy-done.7
  115.6 0.9 copy-done.9
  116.5 3.6 %shard_map.80 = (f32[16,64,256]{2,1,0:T(8,128)S(1)}, bf16[13,64,256]{2,1,0:T(8,128)(2,1)}) custom-call(s32[1]{0:T(128)} %bitcast.refs_0_, s32[8]{0:T(128)S(1)} %bitcast.21, s32[8,2]{1,0:T(8,128)S(1)} %copy.17.refs_1_.refs_2_, s32[8,2]{1,0:T(8,128)S(1)} %copy.18.refs_2_.refs_3_, bf16[896,128]{1,0:T(8,128)(2,1)S(1)} %copy-done.7, ...), custom_call_target="tpu_custom_call" | custom-call | tf_op jit(solution)/shard_map/pallas_call | solution.py:354
  120.1 2.7 %collective-permute-start.3 = (bf16[13,64,256]{2,1,0:T(8,128)(2,1)}, bf16[13,64,256]{2,1,0:T(8,128)(2,1)S(1)}, u32[]{:S(2)}, u32[]{:S(2)}) collective-permute-start(bf16[13,64,256]{2,1,0:T(8,128)(2,1)} %get-tuple-element.14), channel_id=1, source_target_pairs={{0,8},{8,16},{16,24},{24,32},{32,40},{40,48},{48,56},{56,64},{64,7... | collective-permute-start | bytes 1277960 | tf_op jit(solution)/shard_map/ppermute | solution.py:276
  122.8 13.7 %collective-permute-done.3.refs_1_ = bf16[13,64,256]{2,1,0:T(8,128)(2,1)S(1)} collective-permute-done((bf16[13,64,256]{2,1,0:T(8,128)(2,1)}, bf16[13,64,256]{2,1,0:T(8,128)(2,1)S(1)}, u32[]{:S(2)}, u32[]{:S(2)}) %collective-permute-start.3) | collective-permute-done | bytes 426016 | tf_op jit(solution)/shard_map/ppermute | solution.py:276
  136.5 1.1 shard_map.81
  137.5 1.1 shard_map.82.refs_2_
  138.6 0.0 collective-permute-done.4.refs_1_
  138.6 1.1 shard_map.83
  (20 shorter events, 0.2 us)
Async XLA Ops:
  0.6 23.3 %copy-start.3 = (bf16[1,16,64,256]{3,2,1,0:T(8,128)(2,1)S(1)}, bf16[1,16,64,256]{3,2,1,0:T(8,128)(2,1)}, u32[]{:S(2)}) copy-start(bf16[1,16,64,256]{3,2,1,0:T(8,128)(2,1)} %param.6) | copy-start | bytes 1572868
  0.6 23.3 %copy-start.10 = (s32[1,1,8]{2,1,0:T(1,128)S(1)}, s32[1,1,8]{2,1,0:T(1,128)}, u32[]{:S(2)}) copy-start(s32[1,1,8]{2,1,0:T(1,128)} %param.9) | copy-start | bytes 100
  0.7 19.5 %copy-start.11 = (s32[1,1,8,2]{2,3,1,0:T(2,128)S(1)}, s32[1,1,8,2]{2,3,1,0:T(2,128)}, u32[]{:S(2)}) copy-start(s32[1,1,8,2]{2,3,1,0:T(2,128)} %param.10) | copy-start | bytes 196
  0.7 19.5 %copy-start.12 = (s32[1,1,8,2]{2,3,1,0:T(2,128)S(1)}, s32[1,1,8,2]{2,3,1,0:T(2,128)}, u32[]{:S(2)}) copy-start(s32[1,1,8,2]{2,3,1,0:T(2,128)} %param.11) | copy-start | bytes 196
  0.7 23.3 %collective-permute-start = (bf16[16,64,256]{2,1,0:T(8,128)(2,1)}, bf16[16,64,256]{2,1,0:T(8,128)(2,1)}, u32[]{:S(2)}, u32[]{:S(2)}) collective-permute-start(bf16[16,64,256]{2,1,0:T(8,128)(2,1)} %bitcast.17), channel_id=1, source_target_pairs={{8,0},{16,8},{24,16},{32,24},{40,32},{48,40},{56,48},{64,56},{72,6... | collective-permute-start | bytes 1572872 | tf_op jit(solution)/shard_map/ppermute | solution.py:276
  14.6 15.5 %copy-start = (bf16[9,256,256]{2,1,0:T(8,128)(2,1)S(1)}, bf16[9,256,256]{2,1,0:T(8,128)(2,1)}, u32[]{:S(2)}) copy-start(bf16[9,256,256]{2,1,0:T(8,128)(2,1)} %refs_6_.1) | copy-start | bytes 3538948
  15.6 19.8 %all-to-all-start = ((bf16[8,2,14,16,128]{4,3,2,1,0:T(8,128)(2,1)}), bf16[8,2,14,16,128]{4,3,2,1,0:T(8,128)(2,1)S(1)}, u32[]{:S(2)}, u32[]{:S(2)}) async-start(bf16[8,2,14,16,128]{4,3,2,1,0:T(8,128)(2,1)} %bitcast.23), calls=%async_computation | async-start | bytes 1835008 | tf_op jit(solution)/shard_map/all_to_all | solution.py:309
  25.6 3.7 %collective-permute-start.1 = (bf16[896,256]{1,0:T(8,128)(2,1)S(1)}, bf16[896,256]{1,0:T(8,128)(2,1)S(1)}, u32[]{:S(2)}, u32[]{:S(2)}) collective-permute-start(bf16[896,256]{1,0:T(8,128)(2,1)S(1)} %shard_map.77.refs_1_), channel_id=1, source_target_pairs={{0,1},{1,0},{2,3},{3,2},{4,5},{5,4},{6,7},{7,6},{8,9},{9,8},{10,11... | collective-permute-start | bytes 1376264 | tf_op jit(solution)/shard_map/ppermute | solution.py:321
  29.3 0.8 copy-start.4
  30.1 1.0 copy-start.5
  33.7 1.7 %copy-start.1 = (bf16[3,2048,256]{2,1,0:T(8,128)(2,1)}, bf16[3,2048,256]{2,1,0:T(8,128)(2,1)S(1)}, u32[]{:S(2)}) copy-start(bf16[3,2048,256]{2,1,0:T(8,128)(2,1)S(1)} %get-tuple-element.10.refs_4_) | copy-start | bytes 9437188
  35.4 1.9 %copy-start.2 = (bf16[3,2048,256]{2,1,0:T(8,128)(2,1)S(1)}, bf16[3,2048,256]{2,1,0:T(8,128)(2,1)}, u32[]{:S(2)}) copy-start(bf16[3,2048,256]{2,1,0:T(8,128)(2,1)} %copy-done.1) | copy-start | bytes 9437188
  41.0 72.9 %copy-start.6 = (bf16[896,128]{1,0:T(8,128)(2,1)}, bf16[896,128]{1,0:T(8,128)(2,1)S(1)}, u32[]{:S(2)}) copy-start(bf16[896,128]{1,0:T(8,128)(2,1)S(1)} %get-tuple-element.11.refs_4_) | copy-start | bytes 688132
  41.0 62.6 %copy-start.13 = (bf16[896,128]{1,0:T(8,128)(2,1)S(1)}, bf16[896,128]{1,0:T(8,128)(2,1)}, u32[]{:S(2)}) copy-start(bf16[896,128]{1,0:T(8,128)(2,1)} %get-tuple-element.12) | copy-start | bytes 688132
  98.0 14.0 %all-to-all-start.4 = ((bf16[16,144,128]{2,1,0:T(8,128)(2,1)}), bf16[16,144,128]{2,1,0:T(8,128)(2,1)S(1)}, u32[]{:S(2)}, u32[]{:S(2)}) async-start(bf16[16,144,128]{2,1,0:T(8,128)(2,1)} %broadcast_in_dim.30), calls=%async_computation.4 | async-start | bytes 1179648 | tf_op jit(solution)/shard_map/all_to_all | solution.py:393
  103.6 10.3 %collective-permute-start.2 = (bf16[896,128]{1,0:T(8,128)(2,1)S(1)}, bf16[896,128]{1,0:T(8,128)(2,1)S(1)}, u32[]{:S(2)}, u32[]{:S(2)}) collective-permute-start(bf16[896,128]{1,0:T(8,128)(2,1)S(1)} %copy-done.13), channel_id=1, source_target_pairs={{0,1},{1,0},{2,3},{3,2},{4,5},{5,4},{6,7},{7,6},{8,9},{9,8},{10,11... | collective-permute-start | bytes 688136 | tf_op jit(solution)/shard_map/ppermute | solution.py:352
  112.0 26.6 %collective-permute-start.4 = (bf16[2304,128]{1,0:T(8,128)(2,1)S(1)}, bf16[2304,128]{1,0:T(8,128)(2,1)S(1)}, u32[]{:S(2)}, u32[]{:S(2)}) collective-permute-start(bf16[2304,128]{1,0:T(8,128)(2,1)S(1)} %bitcast.15), channel_id=1, source_target_pairs={{0,1},{1,0},{2,3},{3,2},{4,5},{5,4},{6,7},{7,6},{8,9},{9,8},{10,11... | collective-permute-start | bytes 1769480 | tf_op jit(solution)/shard_map/ppermute | solution.py:395
  113.9 0.7 copy-start.8
  114.6 0.9 copy-start.7
  115.6 0.9 copy-start.9
  120.1 16.4 %collective-permute-start.3 = (bf16[13,64,256]{2,1,0:T(8,128)(2,1)}, bf16[13,64,256]{2,1,0:T(8,128)(2,1)S(1)}, u32[]{:S(2)}, u32[]{:S(2)}) collective-permute-start(bf16[13,64,256]{2,1,0:T(8,128)(2,1)} %get-tuple-element.14), channel_id=1, source_target_pairs={{0,8},{8,16},{16,24},{24,32},{32,40},{40,48},{48,56},{56,64},{64,7... | collective-permute-start | bytes 1277960 | tf_op jit(solution)/shard_map/ppermute | solution.py:276

commit v8 on v7

--- a/solution.py
+++ b/solution.py
@@ -104,7 +104,7 @@
 
 
 def slope_kernel(dims, me_ref, own_ref, up_ref, gelu_ref, shifted,
-                 terms_ref, slope_ref, lent_ref, slid, prior, partner_count, slot, partner_slot, staged, kept, sems):
+                 terms_ref, slope_ref, lent_ref, slid, prior, partner_count, slot, partner_slot, staged, kept, loose, spread, sems):
     side, slots, heads, _ = dims
     boxes = up_ref.shape[1]
     half = gelu_ref.shape[1]
@@ -116,16 +116,18 @@
     even = me - core
     partner = even + 1 - core
 
+    cells = side * side
+    tail = cells // 8 * 8
     lane = lax.broadcasted_iota(jnp.int32, (8, half), 1)
     line = lax.broadcasted_iota(jnp.int32, (8, half), 0)
     totals = jnp.zeros((8, half), F32)
     counts = jnp.zeros((8, half), F32)
     for i in range(heads):
-        row = up_ref[i, 0, 0].astype(F32)[8:16]
+        row = up_ref[i, 0].astype(F32)[tail : tail + 8]
         totals = totals + jnp.where(i < even, row, 0.0)
         counts = counts + jnp.where(i == partner, row, 0.0)
-    totals = jnp.where(line == side - 8, totals, 0.0)
-    counts = jnp.where(line == side - 8, counts, 0.0)
+    totals = jnp.where(line == cells - tail, totals, 0.0)
+    counts = jnp.where(line == cells - tail, counts, 0.0)
     for j in range(heads):
         prior[j] = jnp.sum(jnp.where(lane == j, totals, 0.0)).astype(jnp.int32)
         partner_count[j] = jnp.sum(jnp.where(lane == j, counts, 0.0)).astype(jnp.int32)
@@ -146,9 +148,11 @@
             (slot, s, used, slope_ref) if s < slots else (partner_slot, s - slots, partner_used, kept)
         )
         head = table[0, number]
-        upstream = up_ref[head, table[1, number]].astype(F32)
+        loose[s] = up_ref[head, table[1, number]].astype(F32)
+        for y in range(side):
+            spread[s, pl.ds(y * XP, side), :] = loose[s, pl.ds(y * side, side), :]
         last = jnp.where(number < count, side, 0)
-        slope = upstream.reshape(area, half) * gelu_ref[pl.ds(s * area, area), :]
+        slope = spread[s] * gelu_ref[pl.ds(s * area, area), :]
         slope = jnp.where(columns < last, slope, 0.0).astype(BF16)
         ref[pl.ds(number * area, area), :] = slope
         for a in range(3):
@@ -176,6 +180,12 @@
             copies.append(copy)
     for copy in copies:
         copy.wait()
+
+
+def heads_kernel(dims, me_ref, own_ref, crop_ref, other_ref, weight_ref, up_ref,
+                 terms_ref, slope_ref, lent_ref, gelu, shifted, *room):
+    forward_kernel(dims, me_ref, crop_ref, other_ref, weight_ref, gelu, shifted)
+    slope_kernel(dims, me_ref, own_ref, up_ref, gelu, shifted, terms_ref, slope_ref, lent_ref, *room)
 
 
 def backward_kernel(dims, me_ref, own_ref, row_ref, col_ref, slope_ref, back_ref, weight_ref, main_ref, spill_ref, canvas, shifted,
@@ -302,9 +312,10 @@
 
     below = shift(tile_map, "tile", -1)
     spare = jnp.pad(own.astype(BF16), (0, half - heads))
-    spare = jnp.broadcast_to(spare, (2, boxes, side, XP - side, half))
-    halves = mask_grad[0, 0].reshape(boxes, side, side, 2, half).transpose(3, 0, 1, 2, 4)
-    sent = repeated(jnp.concatenate([halves, spare], 3), chips)
+    rows = side * side // 8 * 8 + 8
+    spare = jnp.broadcast_to(spare, (2, boxes, rows - side * side, half))
+    halves = mask_grad[0, 0].reshape(boxes, side * side, 2, half).transpose(2, 0, 1, 3)
+    sent = repeated(jnp.concatenate([halves, spare], 2), chips)
     sent = sent.reshape((owners,) + sent.shape[2:])
     ups = lax.all_to_all(sent, "dp", 0, 0, tiled=True)
 
@@ -320,35 +331,29 @@
     )(own, top_rows, left_cols, tile_map, below)
     partner_crops = lax.ppermute(crops, "dp", partner)
 
-    gelu, shifted = kernel(
-        forward_kernel,
+    strip = (slots * area, half)
+    hbm = pl.BlockSpec(memory_space=pltpu.HBM)
+    terms, slope, lent = kernel(
+        heads_kernel,
         dims,
-        (
+        (pltpu.HBM((9 * channels, half), BF16), jax.ShapeDtypeStruct(strip, BF16), pltpu.HBM(strip, BF16)),
+        [smem()] * 2 + [vmem()] * 4,
+        [
             pltpu.VMEM((2 * slots * area, half), F32),
             pltpu.VMEM((3, 2 * slots * padded, channels), BF16),
-        ),
-        [smem()] + [vmem()] * 3,
-        [],
-    )(me_array, crops, partner_crops, weight)
-
-    strip = jax.ShapeDtypeStruct((slots * area, half), BF16)
-    terms, slope, lent = kernel(
-        slope_kernel,
-        dims,
-        (pltpu.HBM((9 * channels, half), BF16), strip, pltpu.HBM(strip.shape, BF16)),
-        [smem()] * 2 + [vmem()] * 3,
-        [
             pltpu.VMEM((3, 2 * slots * padded, half), BF16),
             pltpu.SMEM((heads,), jnp.int32),
             pltpu.SMEM((heads,), jnp.int32),
             pltpu.SMEM((2, slots), jnp.int32),
             pltpu.SMEM((2, slots), jnp.int32),
             pltpu.VMEM((9 * channels, half), BF16),
-            pltpu.VMEM((slots * area, half), BF16),
+            pltpu.VMEM(strip, BF16),
+            pltpu.VMEM((2 * slots, rows, half), F32),
+            pltpu.VMEM((2 * slots, area, half), F32),
             pltpu.SemaphoreType.DMA((10,)),
         ],
-        (pl.BlockSpec(memory_space=pltpu.HBM), vmem(), pl.BlockSpec(memory_space=pltpu.HBM)),
-    )(me_array, own, ups, gelu, shifted)
+        (hbm, vmem(), hbm),
+    )(me_array, own, crops, partner_crops, weight, ups)
     returned = lax.ppermute(lent, "dp", partner)
 
     main, spill = kernel(
@@ -395,7 +400,6 @@
     other = lax.ppermute(got, "dp", partner)
     whole = pltpu.HBM((part, channels), F32)
     room = [pltpu.VMEM((part, half), F32), pltpu.SemaphoreType.DMA((4,))]
-    hbm = pl.BlockSpec(memory_space=pltpu.HBM)
     begun = kernel(first_kernel, dims, whole, [smem(), vmem()], room, hbm)(core.reshape(1), got)
     weight_grad = kernel(
         finish_kernel, dims, whole, [smem(), vmem(), hbm], room, hbm, {2: 0}

time: 140 us -> 135 us (0.964)
  local copies, waits for them, and re-layouts: 11.2 us -> 6.47 us
  blocking collectives: 55.8 us -> 51.1 us
  waiting for transfers between devices: 25.6 us -> 30.2 us
    all_to_all x1, waiting for transfers between devices: 0.01 us -> 6.36 us  [on_device(): ups = lax.all_to_all(sent, 'dp', 0, 0, tiled=True)]
    unnamed x28 -> x20, local copies, waits for them, and re-layouts: 7.91 us -> 3.26 us
    all_to_all x1, blocking collectives: 17.8 us -> 15.2 us  [on_device(): lax.all_to_all(terms.reshape(near, part // near, half), ('tile', 'dp'), 0...]
    all_to_all x1, blocking collectives: 21.9 us -> 19.9 us  [on_device(): lax.all_to_all(column.reshape(deep, part // near // deep, half), 'tile',...]
    ppermute x1, waiting for transfers between devices: 1.78 us -> 0.01 us  [on_device(): partner_crops = lax.ppermute(crops, 'dp', partner)]
    pallas_call x2 -> x1, Pallas kernels: 6.37 us -> 6.31 us  [on_device(): kernel(heads_kernel, dims, (pltpu.HBM((9 * channels, half), BF16), jax.Sh...]
  transfers between devices with their start and end apart: 7 -> 7, of which waited for: 4 -> 4; matrix products, arithmetic and copies ran while one was open for 2% -> 2% of each run, Pallas kernels for 7% -> 5%
where the time goes in v8:
time: 135 us; the launch traced here: 134 us
  blocking collectives  51.1 us (38%)
  starting transfers between devices  30.4 us (23%)
  waiting for transfers between devices  30.2 us (22%)
  Pallas kernels  14.3 us (11%)
  local copies, waits for them, and re-layouts  6.47 us (5%)
    all_to_all x1, blocking collectives, on_device(): lax.all_to_all(column.reshape(deep, part // near // deep, half), 'tile',...  19.9 us
    ppermute x2, waiting for transfers between devices, shift(): return lax.ppermute(array, axis, pairs)  17.4 us
    all_to_all x1, blocking collectives, on_device(): lax.all_to_all(repeated(chunk, deep), 'tile', 0, 0, axis_index_groups=sti...  16 us
    all_to_all x1, blocking collectives, on_device(): lax.all_to_all(terms.reshape(near, part // near, half), ('tile', 'dp'), 0...  15.2 us
    ppermute x2, starting transfers between devices, shift(): return lax.ppermute(array, axis, pairs)  14.6 us
    all_to_all x1, waiting for transfers between devices, on_device(): lax.all_to_all(repeated(got, near), ('tile', 'dp'), 0, 0, axis_index_grou...  6.42 us
    all_to_all x1, waiting for transfers between devices, on_device(): ups = lax.all_to_all(sent, 'dp', 0, 0, tiled=True)  6.36 us
    pallas_call x1, Pallas kernels, on_device(): kernel(heads_kernel, dims, (pltpu.HBM((9 * channels, half), BF16), jax.Sh...  6.31 us
  transfers between devices with their start and end apart: 7, of which 4 were waited for; matrix products, arithmetic and copies ran while one was open for 2% of the time, Pallas kernels for 5%

profile of v8, /device:TPU:6, one launch (start us, length us, event | category | flops | bytes accessed | tf_op | source)
XLA Modules:
  0.0 134.3 jit_solution(11491081686628216270)
XLA Ops:
  0.6 0.0 copy-start.1
  0.6 0.0 copy-start.6
  0.7 0.0 copy-start.7
  0.7 0.0 copy-start.8
  0.7 11.8 %collective-permute-start = (bf16[16,64,256]{2,1,0:T(8,128)(2,1)}, bf16[16,64,256]{2,1,0:T(8,128)(2,1)S(1)}, u32[]{:S(2)}, u32[]{:S(2)}) collective-permute-start(bf16[16,64,256]{2,1,0:T(8,128)(2,1)} %bitcast.17), channel_id=1, source_target_pairs={{8,0},{16,8},{24,16},{32,24},{40,32},{48,40},{56,48},{64,56},{72,6... | collective-permute-start | bytes 1572872 | tf_op jit(solution)/shard_map/ppermute | solution.py:286
  12.5 1.1 reshape_squeeze.3
  13.5 0.7 bitcast_convert_fusion
  14.2 0.3 pad_maximum_fusion
  14.5 0.0 copy-start
  14.5 1.0 broadcast_in_dim.26
  15.5 4.5 %all-to-all-start = ((bf16[8,2,200,128]{3,2,1,0:T(8,128)(2,1)}), bf16[8,2,200,128]{3,2,1,0:T(8,128)(2,1)S(1)}, u32[]{:S(2)}, u32[]{:S(2)}) async-start(bf16[8,2,200,128]{3,2,1,0:T(8,128)(2,1)} %bitcast.23), calls=%async_computation | async-start | bytes 1638400 | tf_op jit(solution)/shard_map/all_to_all | solution.py:320
  20.0 0.0 copy-done.7
  20.0 0.1 copy.17.refs_1_.refs_2_
  20.1 0.0 copy-done.8
  20.1 0.1 copy.18.refs_2_.refs_3_
  20.2 3.8 %collective-permute-done.refs_4_ = bf16[16,64,256]{2,1,0:T(8,128)(2,1)S(1)} collective-permute-done((bf16[16,64,256]{2,1,0:T(8,128)(2,1)}, bf16[16,64,256]{2,1,0:T(8,128)(2,1)S(1)}, u32[]{:S(2)}, u32[]{:S(2)}) %collective-permute-start) | collective-permute-done | bytes 524320 | tf_op jit(solution)/shard_map/ppermute | solution.py:286
  24.0 0.0 copy-done.1
  24.0 0.0 copy-done.6
  24.0 1.2 shard_map.77.refs_2_
  25.2 1.9 %collective-permute-start.1 = (bf16[896,256]{1,0:T(8,128)(2,1)S(1)}, bf16[896,256]{1,0:T(8,128)(2,1)S(1)}, u32[]{:S(2)}, u32[]{:S(2)}) collective-permute-start(bf16[896,256]{1,0:T(8,128)(2,1)S(1)} %shard_map.77.refs_2_), channel_id=1, source_target_pairs={{0,1},{1,0},{2,3},{3,2},{4,5},{5,4},{6,7},{7,6},{8,9},{9,8},{10,11... | collective-permute-start | bytes 1376264 | tf_op jit(solution)/shard_map/ppermute | solution.py:332
  27.1 6.4 %all-to-all-done.refs_5_ = bf16[8,2,200,128]{3,2,1,0:T(8,128)(2,1)S(1)} async-done(((bf16[8,2,200,128]{3,2,1,0:T(8,128)(2,1)}), bf16[8,2,200,128]{3,2,1,0:T(8,128)(2,1)S(1)}, u32[]{:S(2)}, u32[]{:S(2)}) %all-to-all-start) | async-done | bytes 819232 | tf_op jit(solution)/shard_map/all_to_all | solution.py:320
  33.5 0.0 collective-permute-done.1.refs_3_
  33.5 0.0 copy-done
  33.5 6.3 %shard_map.78 = (bf16[2304,128]{1,0:T(8,128)(2,1)}, bf16[896,128]{1,0:T(8,128)(2,1)S(1)}, bf16[896,128]{1,0:T(8,128)(2,1)}) custom-call(s32[1]{0:T(128)} %bitcast.refs_0_, s32[8]{0:T(128)S(1)} %bitcast.20, bf16[896,256]{1,0:T(8,128)(2,1)S(1)} %shard_map.77.refs_2_, bf16[896,256]{1,0:T(8,128)(2,1)S(1)} %collective-permute-done.1.refs_3_, ...), custom_call_target="tpu_custom_call" | custom-call | tf_op jit(solution)/shard_map/pallas_call | solution.py:336
  39.8 0.0 copy-start.2
  39.8 0.7 copy-done.2
  40.5 15.2 %all_to_all.25 = bf16[16,144,128]{2,1,0:T(8,128)(2,1)S(1)} all-to-all(bf16[16,144,128]{2,1,0:T(8,128)(2,1)} %bitcast.26), channel_id=1, replica_groups={{0,2,4,6,128,130,132,134,256,258,260,262,384,386,388,390},{1,3,5,7,129,..., dimensions={0} | all-to-all | bytes 1179648 | tf_op jit(solution)/shard_map/all_to_all | solution.py:388
  55.7 0.1 convert_reduce_fusion
  55.8 19.9 %all_to_all.26 = f32[16,9,128]{2,1,0:T(8,128)S(1)} all-to-all(f32[16,9,128]{2,1,0:T(8,128)S(1)} %reshape.36), channel_id=1, replica_groups={{0,8,16,24,32,40,48,56,64,72,80,88,96,104,112,120},{128,136,144,152,160..., dimensions={0} | all-to-all | bytes 147456 | tf_op jit(solution)/shard_map/all_to_all | solution.py:392
  75.7 16.0 %all_to_all.27 = bf16[16,9,128]{2,1,0:T(8,128)(2,1)S(1)} all-to-all(bf16[16,9,128]{2,1,0:T(8,128)(2,1)S(1)} %broadcast_in_dim.28), channel_id=1, replica_groups={{0,8,16,24,32,40,48,56,64,72,80,88,96,104,112,120},{128,136,144,152,160..., dimensions={0} | all-to-all | bytes 73728 | tf_op jit(solution)/shard_map/all_to_all | solution.py:396
  91.7 0.9 broadcast_in_dim.30
  92.6 5.7 %all-to-all-start.4 = ((bf16[16,144,128]{2,1,0:T(8,128)(2,1)}), bf16[16,144,128]{2,1,0:T(8,128)(2,1)S(1)}, u32[]{:S(2)}, u32[]{:S(2)}) async-start(bf16[16,144,128]{2,1,0:T(8,128)(2,1)} %broadcast_in_dim.30), calls=%async_computation.4 | async-start | bytes 1179648 | tf_op jit(solution)/shard_map/all_to_all | solution.py:398
  98.3 0.0 copy-done.9
  98.3 1.9 %collective-permute-start.2 = (bf16[896,128]{1,0:T(8,128)(2,1)S(1)}, bf16[896,128]{1,0:T(8,128)(2,1)S(1)}, u32[]{:S(2)}, u32[]{:S(2)}) collective-permute-start(bf16[896,128]{1,0:T(8,128)(2,1)S(1)} %copy-done.9), channel_id=1, source_target_pairs={{0,1},{1,0},{2,3},{3,2},{4,5},{5,4},{6,7},{7,6},{8,9},{9,8},{10,11... | collective-permute-start | bytes 688136 | tf_op jit(solution)/shard_map/ppermute | solution.py:357
  100.2 6.4 %all-to-all-done.4 = bf16[16,144,128]{2,1,0:T(8,128)(2,1)S(1)} async-done(((bf16[16,144,128]{2,1,0:T(8,128)(2,1)}), bf16[16,144,128]{2,1,0:T(8,128)(2,1)S(1)}, u32[]{:S(2)}, u32[]{:S(2)}) %all-to-all-start.4) | async-done | bytes 589856 | tf_op jit(solution)/shard_map/all_to_all | solution.py:398
  106.6 1.9 %collective-permute-start.4 = (bf16[2304,128]{1,0:T(8,128)(2,1)S(1)}, bf16[2304,128]{1,0:T(8,128)(2,1)S(1)}, u32[]{:S(2)}, u32[]{:S(2)}) collective-permute-start(bf16[2304,128]{1,0:T(8,128)(2,1)S(1)} %bitcast.15), channel_id=1, source_target_pairs={{0,1},{1,0},{2,3},{3,2},{4,5},{5,4},{6,7},{7,6},{8,9},{9,8},{10,11... | collective-permute-start | bytes 1769480 | tf_op jit(solution)/shard_map/ppermute | solution.py:400
  108.6 0.0 collective-permute-done.2.refs_5_
  108.6 0.0 copy-start.4
  108.6 0.7 copy-done.4
  109.3 0.9 copy-done.3
  110.2 0.9 copy-done.5
  111.1 3.6 %shard_map.79 = (f32[16,64,256]{2,1,0:T(8,128)S(1)}, bf16[13,64,256]{2,1,0:T(8,128)(2,1)}) custom-call(s32[1]{0:T(128)} %bitcast.refs_0_, s32[8]{0:T(128)S(1)} %bitcast.21, s32[8,2]{1,0:T(8,128)S(1)} %copy.17.refs_1_.refs_2_, s32[8,2]{1,0:T(8,128)S(1)} %copy.18.refs_2_.refs_3_, bf16[896,128]{1,0:T(8,128)(2,1)S(1)} %copy-done.3, ...), custom_call_target="tpu_custom_call" | custom-call | tf_op jit(solution)/shard_map/pallas_call | solution.py:359
  114.7 2.8 %collective-permute-start.3 = (bf16[13,64,256]{2,1,0:T(8,128)(2,1)}, bf16[13,64,256]{2,1,0:T(8,128)(2,1)S(1)}, u32[]{:S(2)}, u32[]{:S(2)}) collective-permute-start(bf16[13,64,256]{2,1,0:T(8,128)(2,1)} %get-tuple-element.10), channel_id=1, source_target_pairs={{0,8},{8,16},{16,24},{24,32},{32,40},{40,48},{48,56},{56,64},{64,7... | collective-permute-start | bytes 1277960 | tf_op jit(solution)/shard_map/ppermute | solution.py:286
  117.5 13.6 %collective-permute-done.3.refs_1_ = bf16[13,64,256]{2,1,0:T(8,128)(2,1)S(1)} collective-permute-done((bf16[13,64,256]{2,1,0:T(8,128)(2,1)}, bf16[13,64,256]{2,1,0:T(8,128)(2,1)S(1)}, u32[]{:S(2)}, u32[]{:S(2)}) %collective-permute-start.3) | collective-permute-done | bytes 426016 | tf_op jit(solution)/shard_map/ppermute | solution.py:286
  131.1 1.1 shard_map.80
  132.2 1.1 shard_map.81.refs_2_
  133.2 0.0 collective-permute-done.4.refs_1_
  133.2 1.1 shard_map.82
  (11 shorter events, 0.1 us)
Async XLA Ops:
  0.6 23.3 %copy-start.1 = (bf16[1,16,64,256]{3,2,1,0:T(8,128)(2,1)S(1)}, bf16[1,16,64,256]{3,2,1,0:T(8,128)(2,1)}, u32[]{:S(2)}) copy-start(bf16[1,16,64,256]{3,2,1,0:T(8,128)(2,1)} %param.6) | copy-start | bytes 1572868
  0.6 23.3 %copy-start.6 = (s32[1,1,8]{2,1,0:T(1,128)S(1)}, s32[1,1,8]{2,1,0:T(1,128)}, u32[]{:S(2)}) copy-start(s32[1,1,8]{2,1,0:T(1,128)} %param.9) | copy-start | bytes 100
  0.7 19.4 %copy-start.7 = (s32[1,1,8,2]{2,3,1,0:T(2,128)S(1)}, s32[1,1,8,2]{2,3,1,0:T(2,128)}, u32[]{:S(2)}) copy-start(s32[1,1,8,2]{2,3,1,0:T(2,128)} %param.10) | copy-start | bytes 196
  0.7 19.4 %copy-start.8 = (s32[1,1,8,2]{2,3,1,0:T(2,128)S(1)}, s32[1,1,8,2]{2,3,1,0:T(2,128)}, u32[]{:S(2)}) copy-start(s32[1,1,8,2]{2,3,1,0:T(2,128)} %param.11) | copy-start | bytes 196
  0.7 23.3 %collective-permute-start = (bf16[16,64,256]{2,1,0:T(8,128)(2,1)}, bf16[16,64,256]{2,1,0:T(8,128)(2,1)S(1)}, u32[]{:S(2)}, u32[]{:S(2)}) collective-permute-start(bf16[16,64,256]{2,1,0:T(8,128)(2,1)} %bitcast.17), channel_id=1, source_target_pairs={{8,0},{16,8},{24,16},{32,24},{40,32},{48,40},{56,48},{64,56},{72,6... | collective-permute-start | bytes 1572872 | tf_op jit(solution)/shard_map/ppermute | solution.py:286
  14.5 19.0 %copy-start = (bf16[9,256,256]{2,1,0:T(8,128)(2,1)S(1)}, bf16[9,256,256]{2,1,0:T(8,128)(2,1)}, u32[]{:S(2)}) copy-start(bf16[9,256,256]{2,1,0:T(8,128)(2,1)} %refs_6_.1) | copy-start | bytes 3538948
  15.5 17.9 %all-to-all-start = ((bf16[8,2,200,128]{3,2,1,0:T(8,128)(2,1)}), bf16[8,2,200,128]{3,2,1,0:T(8,128)(2,1)S(1)}, u32[]{:S(2)}, u32[]{:S(2)}) async-start(bf16[8,2,200,128]{3,2,1,0:T(8,128)(2,1)} %bitcast.23), calls=%async_computation | async-start | bytes 1638400 | tf_op jit(solution)/shard_map/all_to_all | solution.py:320
  25.2 8.3 %collective-permute-start.1 = (bf16[896,256]{1,0:T(8,128)(2,1)S(1)}, bf16[896,256]{1,0:T(8,128)(2,1)S(1)}, u32[]{:S(2)}, u32[]{:S(2)}) collective-permute-start(bf16[896,256]{1,0:T(8,128)(2,1)S(1)} %shard_map.77.refs_2_), channel_id=1, source_target_pairs={{0,1},{1,0},{2,3},{3,2},{4,5},{5,4},{6,7},{7,6},{8,9},{9,8},{10,11... | collective-permute-start | bytes 1376264 | tf_op jit(solution)/shard_map/ppermute | solution.py:332
  39.8 0.7 copy-start.2
  40.5 57.8 %copy-start.9 = (bf16[896,128]{1,0:T(8,128)(2,1)S(1)}, bf16[896,128]{1,0:T(8,128)(2,1)}, u32[]{:S(2)}) copy-start(bf16[896,128]{1,0:T(8,128)(2,1)} %get-tuple-element.8) | copy-start | bytes 688132
  92.6 14.0 %all-to-all-start.4 = ((bf16[16,144,128]{2,1,0:T(8,128)(2,1)}), bf16[16,144,128]{2,1,0:T(8,128)(2,1)S(1)}, u32[]{:S(2)}, u32[]{:S(2)}) async-start(bf16[16,144,128]{2,1,0:T(8,128)(2,1)} %broadcast_in_dim.30), calls=%async_computation.4 | async-start | bytes 1179648 | tf_op jit(solution)/shard_map/all_to_all | solution.py:398
  98.3 10.3 %collective-permute-start.2 = (bf16[896,128]{1,0:T(8,128)(2,1)S(1)}, bf16[896,128]{1,0:T(8,128)(2,1)S(1)}, u32[]{:S(2)}, u32[]{:S(2)}) collective-permute-start(bf16[896,128]{1,0:T(8,128)(2,1)S(1)} %copy-done.9), channel_id=1, source_target_pairs={{0,1},{1,0},{2,3},{3,2},{4,5},{5,4},{6,7},{7,6},{8,9},{9,8},{10,11... | collective-permute-start | bytes 688136 | tf_op jit(solution)/shard_map/ppermute | solution.py:357
  106.6 26.6 %collective-permute-start.4 = (bf16[2304,128]{1,0:T(8,128)(2,1)S(1)}, bf16[2304,128]{1,0:T(8,128)(2,1)S(1)}, u32[]{:S(2)}, u32[]{:S(2)}) collective-permute-start(bf16[2304,128]{1,0:T(8,128)(2,1)S(1)} %bitcast.15), channel_id=1, source_target_pairs={{0,1},{1,0},{2,3},{3,2},{4,5},{5,4},{6,7},{7,6},{8,9},{9,8},{10,11... | collective-permute-start | bytes 1769480 | tf_op jit(solution)/shard_map/ppermute | solution.py:400
  108.6 0.7 copy-start.4
  109.3 0.9 copy-start.3
  110.2 0.9 copy-start.5
  114.7 16.4 %collective-permute-start.3 = (bf16[13,64,256]{2,1,0:T(8,128)(2,1)}, bf16[13,64,256]{2,1,0:T(8,128)(2,1)S(1)}, u32[]{:S(2)}, u32[]{:S(2)}) collective-permute-start(bf16[13,64,256]{2,1,0:T(8,128)(2,1)} %get-tuple-element.10), channel_id=1, source_target_pairs={{0,8},{8,16},{16,24},{24,32},{32,40},{40,48},{48,56},{56,64},{64,7... | collective-permute-start | bytes 1277960 | tf_op jit(solution)/shard_map/ppermute | solution.py:286

commit v9 on v8

--- a/solution.py
+++ b/solution.py
@@ -49,6 +49,30 @@
         return used
 
     return lax.fori_loop(0, heads, head, 0)
+
+
+def pack_kernel(dims, own_ref, mask_ref, sent_ref, loose, staged, sems):
+    heads = dims[2]
+    boxes, cells, channels = mask_ref.shape
+    half = channels // 2
+    spare = loose.shape[2] - cells
+    lane = lax.broadcasted_iota(jnp.int32, (spare, half), 1)
+    counts = jnp.zeros((spare, half), jnp.int32)
+    for j in range(heads):
+        counts = jnp.where(lane == j, own_ref[j], counts)
+    for part in range(2):
+        for b in range(boxes):
+            loose[part, b, pl.ds(0, cells)] = mask_ref[b, :, part * half : (part + 1) * half].astype(F32)
+            loose[part, b, pl.ds(cells, spare)] = counts.astype(F32)
+            staged[part, b] = loose[part, b].astype(BF16)
+    copies = [
+        pltpu.make_async_copy(staged, sent_ref.at[chip], sems.at[chip])
+        for chip in range(sent_ref.shape[0])
+    ]
+    for copy in copies:
+        copy.start()
+    for copy in copies:
+        copy.wait()
 
 
 def crop_kernel(dims, own_ref, row_ref, col_ref, map_ref, below_ref, crop_ref, wide, slot):
@@ -311,11 +335,19 @@
     core = lax.rem(me, 2)
 
     below = shift(tile_map, "tile", -1)
-    spare = jnp.pad(own.astype(BF16), (0, half - heads))
     rows = side * side // 8 * 8 + 8
-    spare = jnp.broadcast_to(spare, (2, boxes, rows - side * side, half))
-    halves = mask_grad[0, 0].reshape(boxes, side * side, 2, half).transpose(2, 0, 1, 3)
-    sent = repeated(jnp.concatenate([halves, spare], 2), chips)
+    sent = kernel(
+        pack_kernel,
+        dims,
+        pltpu.HBM((chips, 2, boxes, rows, half), BF16),
+        [smem(), vmem()],
+        [
+            pltpu.VMEM((2, boxes, rows, half), F32),
+            pltpu.VMEM((2, boxes, rows, half), BF16),
+            pltpu.SemaphoreType.DMA((chips,)),
+        ],
+        pl.BlockSpec(memory_space=pltpu.HBM),
+    )(own, mask_grad[0, 0].reshape(boxes, side * side, channels))
     sent = sent.reshape((owners,) + sent.shape[2:])
     ups = lax.all_to_all(sent, "dp", 0, 0, tiled=True)
 

time: 135 us -> 135 us (level)
  Pallas kernels: 14.3 us -> 15.8 us
    pallas_call x0 -> x1, Pallas kernels: none -> 1.48 us  [on_device(): kernel(pack_kernel, dims, pltpu.HBM((chips, 2, boxes, rows, half), BF16),...]
    unnamed x20 -> x22, local copies, waits for them, and re-layouts: 3.26 us -> 3.92 us
  transfers between devices with their start and end apart: 7 -> 7, of which waited for: 4 -> 4; matrix products, arithmetic and copies ran while one was open for 2% -> 1% of each run, Pallas kernels for 5% -> 6%
where the time goes in v9:
time: 135 us; the launch traced here: 134 us
  blocking collectives  51 us (38%)
  starting transfers between devices  30.4 us (23%)
  waiting for transfers between devices  30.2 us (22%)
  Pallas kernels  15.8 us (12%)
  local copies, waits for them, and re-layouts  5.98 us (4%)
    all_to_all x1, blocking collectives, on_device(): lax.all_to_all(column.reshape(deep, part // near // deep, half), 'tile',...  19.4 us
    ppermute x2, waiting for transfers between devices, shift(): return lax.ppermute(array, axis, pairs)  17.4 us
    all_to_all x1, blocking collectives, on_device(): lax.all_to_all(repeated(chunk, deep), 'tile', 0, 0, axis_index_groups=sti...  16.4 us
    all_to_all x1, blocking collectives, on_device(): lax.all_to_all(terms.reshape(near, part // near, half), ('tile', 'dp'), 0...  15.2 us
    ppermute x2, starting transfers between devices, shift(): return lax.ppermute(array, axis, pairs)  14.6 us
    all_to_all x1, waiting for transfers between devices, on_device(): lax.all_to_all(repeated(got, near), ('tile', 'dp'), 0, 0, axis_index_grou...  6.43 us
    all_to_all x1, waiting for transfers between devices, on_device(): ups = lax.all_to_all(sent, 'dp', 0, 0, tiled=True)  6.42 us
    pallas_call x1, Pallas kernels, on_device(): kernel(heads_kernel, dims, (pltpu.HBM((9 * channels, half), BF16), jax.Sh...  6.29 us
  transfers between devices with their start and end apart: 7, of which 4 were waited for; matrix products, arithmetic and copies ran while one was open for 1% of the time, Pallas kernels for 6%

profile of v9, /device:TPU:6, one launch (start us, length us, event | category | flops | bytes accessed | tf_op | source)
XLA Modules:
  0.0 134.3 jit_solution(13261911874786394323)
XLA Ops:
  0.6 0.0 copy-start.1
  0.6 0.0 copy-start
  0.6 11.8 %collective-permute-start = (bf16[16,64,256]{2,1,0:T(8,128)(2,1)}, bf16[16,64,256]{2,1,0:T(8,128)(2,1)S(1)}, u32[]{:S(2)}, u32[]{:S(2)}) collective-permute-start(bf16[16,64,256]{2,1,0:T(8,128)(2,1)} %bitcast.14), channel_id=1, source_target_pairs={{8,0},{16,8},{24,16},{32,24},{40,32},{48,40},{56,48},{64,56},{72,6... | collective-permute-start | bytes 1572872 | tf_op jit(solution)/shard_map/ppermute | solution.py:310
  12.5 1.0 copy.16.refs_1_
  13.4 0.0 copy-start.6
  13.4 0.6 copy-done.6
  14.1 0.0 copy-start.8
  14.1 0.0 copy-start.9
  14.1 0.0 copy-start.7
  14.1 1.5 %shard_map.78 = bf16[4,2,2,200,128]{4,3,2,1,0:T(8,128)(2,1)} custom-call(s32[8]{0:T(128)S(1)} %bitcast.16, bf16[2,196,256]{2,1,0:T(8,128)(2,1)S(1)} %copy.16.refs_1_), custom_call_target="tpu_custom_call" | custom-call | tf_op jit(solution)/shard_map/pallas_call | solution.py:339
  15.6 4.5 %all-to-all-start = ((bf16[8,2,200,128]{3,2,1,0:T(8,128)(2,1)}), bf16[8,2,200,128]{3,2,1,0:T(8,128)(2,1)S(1)}, u32[]{:S(2)}, u32[]{:S(2)}) async-start(bf16[8,2,200,128]{3,2,1,0:T(8,128)(2,1)} %bitcast.21), calls=%async_computation | async-start | bytes 1638400 | tf_op jit(solution)/shard_map/all_to_all | solution.py:352
  20.0 0.0 copy-done.8
  20.0 0.1 copy.17.refs_1_.refs_2_
  20.1 0.0 copy-done.9
  20.1 0.1 copy.18.refs_2_.refs_3_
  20.2 3.7 %collective-permute-done.refs_4_ = bf16[16,64,256]{2,1,0:T(8,128)(2,1)S(1)} collective-permute-done((bf16[16,64,256]{2,1,0:T(8,128)(2,1)}, bf16[16,64,256]{2,1,0:T(8,128)(2,1)S(1)}, u32[]{:S(2)}, u32[]{:S(2)}) %collective-permute-start) | collective-permute-done | bytes 524320 | tf_op jit(solution)/shard_map/ppermute | solution.py:310
  23.9 0.0 copy-done.1
  23.9 0.0 copy-done.7
  23.9 1.2 shard_map.77.refs_2_
  25.2 1.9 %collective-permute-start.1 = (bf16[896,256]{1,0:T(8,128)(2,1)S(1)}, bf16[896,256]{1,0:T(8,128)(2,1)S(1)}, u32[]{:S(2)}, u32[]{:S(2)}) collective-permute-start(bf16[896,256]{1,0:T(8,128)(2,1)S(1)} %shard_map.77.refs_2_), channel_id=1, source_target_pairs={{0,1},{1,0},{2,3},{3,2},{4,5},{5,4},{6,7},{7,6},{8,9},{9,8},{10,11... | collective-permute-start | bytes 1376264 | tf_op jit(solution)/shard_map/ppermute | solution.py:364
  27.1 6.4 %all-to-all-done.refs_5_ = bf16[8,2,200,128]{3,2,1,0:T(8,128)(2,1)S(1)} async-done(((bf16[8,2,200,128]{3,2,1,0:T(8,128)(2,1)}), bf16[8,2,200,128]{3,2,1,0:T(8,128)(2,1)S(1)}, u32[]{:S(2)}, u32[]{:S(2)}) %all-to-all-start) | async-done | bytes 819232 | tf_op jit(solution)/shard_map/all_to_all | solution.py:352
  33.5 0.0 collective-permute-done.1.refs_3_
  33.5 0.0 copy-done
  33.5 6.3 %shard_map.79 = (bf16[2304,128]{1,0:T(8,128)(2,1)}, bf16[896,128]{1,0:T(8,128)(2,1)S(1)}, bf16[896,128]{1,0:T(8,128)(2,1)}) custom-call(s32[1]{0:T(128)} %bitcast.refs_0_, s32[8]{0:T(128)S(1)} %bitcast.18, bf16[896,256]{1,0:T(8,128)(2,1)S(1)} %shard_map.77.refs_2_, bf16[896,256]{1,0:T(8,128)(2,1)S(1)} %collective-permute-done.1.refs_3_, ...), custom_call_target="tpu_custom_call" | custom-call | tf_op jit(solution)/shard_map/pallas_call | solution.py:368
  39.8 0.0 copy-start.2
  39.8 0.7 copy-done.2
  40.5 15.2 %all_to_all.25 = bf16[16,144,128]{2,1,0:T(8,128)(2,1)S(1)} all-to-all(bf16[16,144,128]{2,1,0:T(8,128)(2,1)} %bitcast.23), channel_id=1, replica_groups={{0,2,4,6,128,130,132,134,256,258,260,262,384,386,388,390},{1,3,5,7,129,..., dimensions={0} | all-to-all | bytes 1179648 | tf_op jit(solution)/shard_map/all_to_all | solution.py:420
  55.7 0.1 convert_reduce_fusion
  55.8 19.4 %all_to_all.26 = f32[16,9,128]{2,1,0:T(8,128)S(1)} all-to-all(f32[16,9,128]{2,1,0:T(8,128)S(1)} %reshape.35), channel_id=1, replica_groups={{0,8,16,24,32,40,48,56,64,72,80,88,96,104,112,120},{128,136,144,152,160..., dimensions={0} | all-to-all | bytes 147456 | tf_op jit(solution)/shard_map/all_to_all | solution.py:424
  75.3 16.4 %all_to_all.27 = bf16[16,9,128]{2,1,0:T(8,128)(2,1)S(1)} all-to-all(bf16[16,9,128]{2,1,0:T(8,128)(2,1)S(1)} %broadcast_in_dim.17), channel_id=1, replica_groups={{0,8,16,24,32,40,48,56,64,72,80,88,96,104,112,120},{128,136,144,152,160..., dimensions={0} | all-to-all | bytes 73728 | tf_op jit(solution)/shard_map/all_to_all | solution.py:428
  91.7 0.9 broadcast_in_dim.19
  92.6 5.6 %all-to-all-start.4 = ((bf16[16,144,128]{2,1,0:T(8,128)(2,1)}), bf16[16,144,128]{2,1,0:T(8,128)(2,1)S(1)}, u32[]{:S(2)}, u32[]{:S(2)}) async-start(bf16[16,144,128]{2,1,0:T(8,128)(2,1)} %broadcast_in_dim.19), calls=%async_computation.4 | async-start | bytes 1179648 | tf_op jit(solution)/shard_map/all_to_all | solution.py:430
  98.3 0.0 copy-done.10
  98.3 1.9 %collective-permute-start.2 = (bf16[896,128]{1,0:T(8,128)(2,1)S(1)}, bf16[896,128]{1,0:T(8,128)(2,1)S(1)}, u32[]{:S(2)}, u32[]{:S(2)}) collective-permute-start(bf16[896,128]{1,0:T(8,128)(2,1)S(1)} %copy-done.10), channel_id=1, source_target_pairs={{0,1},{1,0},{2,3},{3,2},{4,5},{5,4},{6,7},{7,6},{8,9},{9,8},{10,11... | collective-permute-start | bytes 688136 | tf_op jit(solution)/shard_map/ppermute | solution.py:389
  100.2 6.4 %all-to-all-done.4 = bf16[16,144,128]{2,1,0:T(8,128)(2,1)S(1)} async-done(((bf16[16,144,128]{2,1,0:T(8,128)(2,1)}), bf16[16,144,128]{2,1,0:T(8,128)(2,1)S(1)}, u32[]{:S(2)}, u32[]{:S(2)}) %all-to-all-start.4) | async-done | bytes 589856 | tf_op jit(solution)/shard_map/all_to_all | solution.py:430
  106.6 1.9 %collective-permute-start.4 = (bf16[2304,128]{1,0:T(8,128)(2,1)S(1)}, bf16[2304,128]{1,0:T(8,128)(2,1)S(1)}, u32[]{:S(2)}, u32[]{:S(2)}) collective-permute-start(bf16[2304,128]{1,0:T(8,128)(2,1)S(1)} %bitcast.12), channel_id=1, source_target_pairs={{0,1},{1,0},{2,3},{3,2},{4,5},{5,4},{6,7},{7,6},{8,9},{9,8},{10,11... | collective-permute-start | bytes 1769480 | tf_op jit(solution)/shard_map/ppermute | solution.py:432
  108.6 0.0 collective-permute-done.2.refs_5_
  108.6 0.0 copy-start.4
  108.6 0.7 copy-done.4
  109.3 0.9 copy-done.3
  110.2 0.9 copy-done.5
  111.1 3.6 %shard_map.80 = (f32[16,64,256]{2,1,0:T(8,128)S(1)}, bf16[13,64,256]{2,1,0:T(8,128)(2,1)}) custom-call(s32[1]{0:T(128)} %bitcast.refs_0_, s32[8]{0:T(128)S(1)} %bitcast.19, s32[8,2]{1,0:T(8,128)S(1)} %copy.17.refs_1_.refs_2_, s32[8,2]{1,0:T(8,128)S(1)} %copy.18.refs_2_.refs_3_, bf16[896,128]{1,0:T(8,128)(2,1)S(1)} %copy-done.3, ...), custom_call_target="tpu_custom_call" | custom-call | tf_op jit(solution)/shard_map/pallas_call | solution.py:391
  114.7 2.8 %collective-permute-start.3 = (bf16[13,64,256]{2,1,0:T(8,128)(2,1)}, bf16[13,64,256]{2,1,0:T(8,128)(2,1)S(1)}, u32[]{:S(2)}, u32[]{:S(2)}) collective-permute-start(bf16[13,64,256]{2,1,0:T(8,128)(2,1)} %get-tuple-element.10), channel_id=1, source_target_pairs={{0,8},{8,16},{16,24},{24,32},{32,40},{40,48},{48,56},{56,64},{64,7... | collective-permute-start | bytes 1277960 | tf_op jit(solution)/shard_map/ppermute | solution.py:310
  117.5 13.6 %collective-permute-done.3.refs_1_ = bf16[13,64,256]{2,1,0:T(8,128)(2,1)S(1)} collective-permute-done((bf16[13,64,256]{2,1,0:T(8,128)(2,1)}, bf16[13,64,256]{2,1,0:T(8,128)(2,1)S(1)}, u32[]{:S(2)}, u32[]{:S(2)}) %collective-permute-start.3) | collective-permute-done | bytes 426016 | tf_op jit(solution)/shard_map/ppermute | solution.py:310
  131.1 1.1 shard_map.81
  132.2 1.1 shard_map.82.refs_2_
  133.3 0.0 collective-permute-done.4.refs_1_
  133.3 1.1 shard_map.83
  (8 shorter events, 0.1 us)
Async XLA Ops:
  0.6 23.3 %copy-start.1 = (bf16[1,16,64,256]{3,2,1,0:T(8,128)(2,1)S(1)}, bf16[1,16,64,256]{3,2,1,0:T(8,128)(2,1)}, u32[]{:S(2)}) copy-start(bf16[1,16,64,256]{3,2,1,0:T(8,128)(2,1)} %param.6) | copy-start | bytes 1572868
  0.6 32.9 %copy-start = (bf16[9,256,256]{2,1,0:T(8,128)(2,1)S(1)}, bf16[9,256,256]{2,1,0:T(8,128)(2,1)}, u32[]{:S(2)}) copy-start(bf16[9,256,256]{2,1,0:T(8,128)(2,1)} %refs_6_.1) | copy-start | bytes 3538948
  0.6 23.3 %collective-permute-start = (bf16[16,64,256]{2,1,0:T(8,128)(2,1)}, bf16[16,64,256]{2,1,0:T(8,128)(2,1)S(1)}, u32[]{:S(2)}, u32[]{:S(2)}) collective-permute-start(bf16[16,64,256]{2,1,0:T(8,128)(2,1)} %bitcast.14), channel_id=1, source_target_pairs={{8,0},{16,8},{24,16},{32,24},{40,32},{48,40},{56,48},{64,56},{72,6... | collective-permute-start | bytes 1572872 | tf_op jit(solution)/shard_map/ppermute | solution.py:310
  13.4 0.7 copy-start.6
  14.1 6.0 %copy-start.8 = (s32[1,1,8,2]{2,3,1,0:T(2,128)S(1)}, s32[1,1,8,2]{2,3,1,0:T(2,128)}, u32[]{:S(2)}) copy-start(s32[1,1,8,2]{2,3,1,0:T(2,128)} %param.10) | copy-start | bytes 196
  14.1 6.1 %copy-start.9 = (s32[1,1,8,2]{2,3,1,0:T(2,128)S(1)}, s32[1,1,8,2]{2,3,1,0:T(2,128)}, u32[]{:S(2)}) copy-start(s32[1,1,8,2]{2,3,1,0:T(2,128)} %param.11) | copy-start | bytes 196
  14.1 9.9 %copy-start.7 = (s32[1,1,8]{2,1,0:T(1,128)S(1)}, s32[1,1,8]{2,1,0:T(1,128)}, u32[]{:S(2)}) copy-start(s32[1,1,8]{2,1,0:T(1,128)} %param.9) | copy-start | bytes 100
  15.6 18.0 %all-to-all-start = ((bf16[8,2,200,128]{3,2,1,0:T(8,128)(2,1)}), bf16[8,2,200,128]{3,2,1,0:T(8,128)(2,1)S(1)}, u32[]{:S(2)}, u32[]{:S(2)}) async-start(bf16[8,2,200,128]{3,2,1,0:T(8,128)(2,1)} %bitcast.21), calls=%async_computation | async-start | bytes 1638400 | tf_op jit(solution)/shard_map/all_to_all | solution.py:352
  25.2 8.4 %collective-permute-start.1 = (bf16[896,256]{1,0:T(8,128)(2,1)S(1)}, bf16[896,256]{1,0:T(8,128)(2,1)S(1)}, u32[]{:S(2)}, u32[]{:S(2)}) collective-permute-start(bf16[896,256]{1,0:T(8,128)(2,1)S(1)} %shard_map.77.refs_2_), channel_id=1, source_target_pairs={{0,1},{1,0},{2,3},{3,2},{4,5},{5,4},{6,7},{7,6},{8,9},{9,8},{10,11... | collective-permute-start | bytes 1376264 | tf_op jit(solution)/shard_map/ppermute | solution.py:364
  39.8 0.7 copy-start.2
  40.5 57.7 %copy-start.10 = (bf16[896,128]{1,0:T(8,128)(2,1)S(1)}, bf16[896,128]{1,0:T(8,128)(2,1)}, u32[]{:S(2)}) copy-start(bf16[896,128]{1,0:T(8,128)(2,1)} %get-tuple-element.8) | copy-start | bytes 688132
  92.6 14.0 %all-to-all-start.4 = ((bf16[16,144,128]{2,1,0:T(8,128)(2,1)}), bf16[16,144,128]{2,1,0:T(8,128)(2,1)S(1)}, u32[]{:S(2)}, u32[]{:S(2)}) async-start(bf16[16,144,128]{2,1,0:T(8,128)(2,1)} %broadcast_in_dim.19), calls=%async_computation.4 | async-start | bytes 1179648 | tf_op jit(solution)/shard_map/all_to_all | solution.py:430
  98.3 10.3 %collective-permute-start.2 = (bf16[896,128]{1,0:T(8,128)(2,1)S(1)}, bf16[896,128]{1,0:T(8,128)(2,1)S(1)}, u32[]{:S(2)}, u32[]{:S(2)}) collective-permute-start(bf16[896,128]{1,0:T(8,128)(2,1)S(1)} %copy-done.10), channel_id=1, source_target_pairs={{0,1},{1,0},{2,3},{3,2},{4,5},{5,4},{6,7},{7,6},{8,9},{9,8},{10,11... | collective-permute-start | bytes 688136 | tf_op jit(solution)/shard_map/ppermute | solution.py:389
  106.6 26.6 %collective-permute-start.4 = (bf16[2304,128]{1,0:T(8,128)(2,1)S(1)}, bf16[2304,128]{1,0:T(8,128)(2,1)S(1)}, u32[]{:S(2)}, u32[]{:S(2)}) collective-permute-start(bf16[2304,128]{1,0:T(8,128)(2,1)S(1)} %bitcast.12), channel_id=1, source_target_pairs={{0,1},{1,0},{2,3},{3,2},{4,5},{5,4},{6,7},{7,6},{8,9},{9,8},{10,11... | collective-permute-start | bytes 1769480 | tf_op jit(solution)/shard_map/ppermute | solution.py:432
  108.6 0.7 copy-start.4
  109.3 0.9 copy-start.3
  110.2 0.9 copy-start.5
  114.7 16.4 %collective-permute-start.3 = (bf16[13,64,256]{2,1,0:T(8,128)(2,1)}, bf16[13,64,256]{2,1,0:T(8,128)(2,1)S(1)}, u32[]{:S(2)}, u32[]{:S(2)}) collective-permute-start(bf16[13,64,256]{2,1,0:T(8,128)(2,1)} %get-tuple-element.10), channel_id=1, source_target_pairs={{0,8},{8,16},{16,24},{24,32},{32,40},{40,48},{48,56},{56,64},{64,7... | collective-permute-start | bytes 1277960 | tf_op jit(solution)/shard_map/ppermute | solution.py:310
